TPU v7x, 512 devices: a whole 4x4x16 slice. The times are simulated.
512 devices in a mesh: tile: 128 (over z, y_hi, x), trc: 4 (over y_lo, core).
Axes of the slice: x: 4, y: 4 (y_hi: 2, y_lo: 2; y = y_hi * 2 + y_lo), z: 16, core: 2. Of those that a mesh axis runs over, the one named last changes fastest.
Arguments:
- tracers: float32 [256, 4, 512, 128], P('trc', None, 'tile'), may hold values from 0.1 to 4
- courant_cycle: float32 [4, 512, 128], P(None, 'tile'), may hold values from -0.45 to 0.45
- courant_edge: float32 [4, 512, 128], P(None, 'tile'), may hold values from -0.45 to 0.45
- seam_flags: int32 [128, 2], P('tile'), may hold values from 0 to 1, as said below
- sunlit: int32 [512, 128], P('tile', 'trc'), may hold values from 0 to 1, as said below
- table_entry: int32 [4, 4, 512, 128], P(None, None, 'tile', 'trc'), may hold values from 0 to 3
- linear_maps: bfloat16 [4, 256, 256], replicated, may hold values from -0.375 to 0.375
- offsets: float32 [4, 256], replicated, may hold values from -4 to 4
- mixing: float32 [3, 512, 128], P(None, 'tile', 'trc'), may hold values from 0.05 to 5
Outputs:
- tracers_out: float32 [256, 4, 512, 128], P('trc', None, 'tile')
Inputs may be any that keep to these rules, and one draw needn't show every extreme that they name: seam_flags[t, 1] equals seam_flags[t + 1, 0] (tile numbers mod 128); a flag is 1 only on the edge before a tile whose number is a multiple of 32, and at least one flag is 1. In every row of the edge-cell dimension, cycle column x is sunlit exactly when cycle column x + 512 / 2 (mod 512) is not; some tile is sunlit in all of its columns.
All inputs are finite; a program needn't handle non-finite values.
Results may differ from a plain program's by a relative error of at most 0.0025.
Values may be sent and summed in bfloat16 or wider, within the bound.
No kernel may reach another device: no remote copies, remote signals or barrier semaphores. Data moves between devices by JAX's collectives and lax.ppermute only.
A program may use at most 64 MiB of HBM per device.

v0:
```python
import jax
import jax.numpy as jnp
from jax import lax
from jax.sharding import PartitionSpec as P

block_boxes = 128


def padded_2(block, sides, width):
    for axis, dim in sides:
        count = lax.axis_size(axis)
        forward = [(i, i + 1) for i in range(count - 1)]
        forward.append((count - 1, 0))
        backward = [(target, source) for source, target in forward]
        low = lax.ppermute(
            lax.slice_in_dim(block, block.shape[dim] - width, None, axis=dim), axis, forward
        )
        high = lax.ppermute(lax.slice_in_dim(block, 0, width, axis=dim), axis, backward)
        block = jnp.concatenate([low, block, high], axis=dim)
    return block


def cut_range(values, start, stop, direction):
    return lax.slice_in_dim(values, start, stop, axis=direction)


def edge_values(stencil, direction):
    length = stencil.shape[direction]
    inner_sum = cut_range(stencil, 1, length - 2, direction) + cut_range(
        stencil, 2, length - 1, direction
    )
    outer_sum = cut_range(stencil, 0, length - 3, direction) + cut_range(
        stencil, 3, length, direction
    )
    return 7.0 / 12.0 * inner_sum - 1.0 / 12.0 * outer_sum


def sweep_flux(stencil, courant, direction):
    inside = stencil.shape[direction] - 6
    edge_vals = edge_values(stencil, direction)
    left_pos = cut_range(edge_vals, 0, inside + 1, direction)
    middle = cut_range(edge_vals, 1, inside + 2, direction)
    right_neg = cut_range(edge_vals, 2, inside + 3, direction)
    center_pos = cut_range(stencil, 2, inside + 3, direction)
    center_neg = cut_range(stencil, 3, inside + 4, direction)
    curve_pos = 6.0 * center_pos - 3.0 * (left_pos + middle)
    flux_pos = courant * (
        middle - 0.5 * courant * (middle - left_pos - (1.0 - 2.0 * courant / 3.0) * curve_pos)
    )
    reverse_speed = -courant
    curve_neg = 6.0 * center_neg - 3.0 * (middle + right_neg)
    flux_neg = courant * (
        middle
        + 0.5 * reverse_speed * (right_neg - middle + (1.0 - 2.0 * reverse_speed / 3.0) * curve_neg)
    )
    return jnp.where(courant > 0.0, flux_pos, flux_neg)


def tendency(flux, direction):
    length = flux.shape[direction]
    return cut_range(flux, 0, length - 1, direction) - cut_range(flux, 1, length, direction)


def wall_faces(courant_edge):
    closed = jnp.zeros(courant_edge.shape[:-1] + (1,), jnp.float32)
    return jnp.concatenate([closed, courant_edge[..., 1:], closed], axis=-1)


def edge_sweep(tracers, courant_edge):
    stencil = jnp.pad(tracers, ((0, 0), (0, 0), (0, 0), (3, 3)), mode="edge")
    return tendency(sweep_flux(stencil, wall_faces(courant_edge)[None], 3), 3)


def solve_columns(values, coupling):
    levels = values.shape[1]
    zero_row = jnp.zeros(values.shape[2:], jnp.float32)
    ratio_list = []
    solved_list = []
    for level_index in range(levels):
        coupling_below = coupling[level_index - 1] if level_index > 0 else zero_row
        coupling_above = coupling[level_index] if level_index < levels - 1 else zero_row
        diagonal = 1.0 + coupling_below + coupling_above
        if level_index == 0:
            pivot_value = diagonal
            current = values[:, 0] / pivot_value
        else:
            pivot_value = diagonal - coupling_below * ratio_list[-1]
            current = (values[:, level_index] + coupling_below * solved_list[-1]) / pivot_value
        ratio_list.append(coupling_above / pivot_value)
        solved_list.append(current)
    result_list = [solved_list[-1]]
    for level_index in range(levels - 2, -1, -1):
        result_list.append(solved_list[level_index] + ratio_list[level_index] * result_list[-1])
    return jnp.stack(result_list[::-1], axis=1)


def orient(block_cells, reverse_flag):
    return jnp.where(reverse_flag > 0, block_cells[..., ::-1], block_cells)


def grouped_maps(values, entry_ids, linear_maps, offsets):
    species, box_count = values.shape
    entries = linear_maps.shape[0]
    member = (entry_ids[:, None] == jnp.arange(entries, dtype=jnp.int32)[None, :]).astype(jnp.int32)
    counts = jnp.sum(member, axis=0)
    padded = (counts + block_boxes - 1) // block_boxes * block_boxes
    group_end = jnp.cumsum(padded)
    group_start = group_end - padded
    within = jnp.sum((jnp.cumsum(member, axis=0) - 1) * member, axis=1)
    target = jnp.sum(member * group_start[None, :], axis=1) + within
    capacity = (box_count + block_boxes - 1) // block_boxes * block_boxes + entries * block_boxes
    buffer = jnp.zeros((species, capacity), jnp.bfloat16).at[:, target].set(values)
    tile_count = capacity // block_boxes
    tile_start = jnp.arange(tile_count, dtype=jnp.int32) * block_boxes
    tile_entry = jnp.minimum(
        jnp.sum((group_end[None, :] <= tile_start[:, None]).astype(jnp.int32), axis=1), entries - 1
    )
    chosen = jnp.take(linear_maps, tile_entry, axis=0)
    product = jnp.einsum(
        "toi,itb->otb",
        chosen,
        buffer.reshape(species, tile_count, block_boxes),
        preferred_element_type=jnp.float32,
    )
    gathered = jnp.take(product.reshape(species, capacity), target, axis=1)
    shift_terms = jnp.dot(offsets.T, member.T.astype(jnp.float32), precision=lax.Precision.HIGHEST)
    return gathered + shift_terms


def chemistry_steps(work_boxes, work_entry, linear_maps, offsets):
    species, levels, columns = work_boxes.shape
    chem_input = work_boxes.reshape(species, levels * columns)
    result = chem_input.astype(jnp.float32)
    for substep in range(work_entry.shape[0]):
        result = jnp.maximum(
            grouped_maps(
                chem_input, work_entry[substep].reshape(levels * columns), linear_maps, offsets
            ),
            0.0,
        )
        chem_input = result.astype(jnp.bfloat16)
    return result.reshape(species, levels, columns)


def shards(
    tracers,
    courant_cycle,
    courant_edge,
    seam_flags,
    sunlit,
    table_entry,
    linear_maps,
    offsets,
    mixing,
):
    quarter, levels, tile_width, edge_length = tracers.shape
    stacked = jnp.concatenate([tracers, courant_cycle[None]], axis=0)
    padded = padded_2(stacked, (("tile", 2),), 3)
    before = orient(padded[:, :, :3, :], seam_flags[0, 0])
    after_cols = orient(padded[:, :, tile_width + 3 :, :], seam_flags[0, 1])
    stencil = jnp.concatenate([before[:quarter], tracers, after_cols[:quarter]], axis=2)
    cycle_faces = jnp.concatenate([courant_cycle, after_cols[quarter][:, :1, :]], axis=1)
    edge_part = edge_sweep(tracers, courant_edge)
    cycle_part = tendency(sweep_flux(stencil, cycle_faces[None], 2), 2)
    advected = tracers + cycle_part + edge_part
    rounded = advected.astype(jnp.bfloat16)
    box_data = lax.all_to_all(rounded, "trc", split_axis=3, concat_axis=0, tiled=True)
    species = box_data.shape[0]
    columns = tile_width * box_data.shape[3]
    box_data = box_data.reshape(species, levels, columns)
    entry_cols = table_entry.reshape(table_entry.shape[0], levels, columns)
    daylit = sunlit.reshape(columns)
    changed = chemistry_steps(box_data, entry_cols, linear_maps, offsets)
    chem_out = jnp.where(daylit[None, None, :] > 0, changed, box_data.astype(jnp.float32))
    mixed_out = solve_columns(chem_out, mixing.reshape(levels - 1, columns))
    tracer_back = mixed_out.reshape(species, levels, tile_width, columns // tile_width)
    return lax.all_to_all(tracer_back, "trc", split_axis=0, concat_axis=3, tiled=True)


def solution(mesh):
    placed = (
        P("trc", None, "tile", None),
        P(None, "tile", None),
        P(None, "tile", None),
        P("tile", None),
        P("tile", "trc"),
        P(None, None, "tile", "trc"),
        P(),
        P(),
        P(None, "tile", "trc"),
    )
    return jax.shard_map(
        shards, mesh=mesh, in_specs=placed, out_specs=P("trc", None, "tile", None), check_vma=False
    )
```

profile of v0, /device:TPU:1, one launch (start us, length us, event | category | flops | bytes accessed | tf_op | source)
XLA Modules:
  0.0 167.8 jit_solution(18216518793525321394)
XLA Ops:
  3.0 16.8 %collective-permute-start = (f32[65,4,3,128]{3,1,2,0:T(4,128)}, f32[65,4,3,128]{3,1,2,0:T(4,128)S(1)}, u32[]{:S(2)}, u32[]{:S(2)}) collective-permute-start(f32[65,4,3,128]{3,1,2,0:T(4,128)} %get-tuple-element.46), channel_id=1, source_target_pairs={{4,0},{8,4},{12,8},{16,12},{20,16},{24,20},{28,24},{32,28},{36,32}... | collective-permute-start | bytes 1198088 | tf_op jit(solution)/shard_map/ppermute | solution.py:18
  19.7 1.9 %collective-permute-start.1 = (f32[65,4,3,128]{3,1,2,0:T(4,128)}, f32[65,4,3,128]{3,1,2,0:T(4,128)}, u32[]{:S(2)}, u32[]{:S(2)}) collective-permute-start(f32[65,4,3,128]{3,1,2,0:T(4,128)} %get-tuple-element.45), channel_id=1, source_target_pairs={{0,4},{4,8},{8,12},{12,16},{16,20},{20,24},{24,28},{28,32},{32,36}... | collective-permute-start | bytes 1198088 | tf_op jit(solution)/shard_map/ppermute | solution.py:15
  48.4 1.6 gather_fusion
  50.0 1.6 gather_fusion.2
  53.9 1.6 gather_fusion.4
  62.2 8.3 %multiply_select_fusion = f32[64,4,4,129]{0,2,1,3:T(4,128)} fusion(f32[64,4,4,3]{0,2,1,3:T(4,128)S(1)} %reshape.1150, f32[64,4,4,131]{0,2,1,3:T(4,128)S(1)} %fusion.37, f32[64,4,4,3]{0,2,1,3:T(4,128)S(1)} %reshape.1149, f32[64,4,4,128]{0,2,1,3:T(4,128)S(1)} %copy.171, f32[4,4,129]{1,0,2:T(4,128)} %copy.182, f32[4,4,129]{1,0,2:T(4,128)} %copy.181, ...), kind=kLoop, calls=%fused_computation.83 | loop fusion | flops 3038208 | bytes 2705744 | tf_op jit(solution)/shard_map/jit(_where)/select_n | solution.py:56
  73.2 2.2 %rev.7 = f32[65,4,3,128]{3,1,2,0:T(4,128)S(1)} reverse(f32[65,4,3,128]{3,1,2,0:T(4,128)} %collective-permute-done.1), dimensions={3} | reverse | bytes 798720 | tf_op jit(solution)/shard_map/rev | solution.py:98
  77.9 2.5 %pad_maximum_fusion = f32[64,4,10,128]{0,2,1,3:T(8,128)S(1)} fusion(f32[64,4,3,128]{0,2,1,3:T(4,128)S(1)} %copy.162, f32[64,4,4,128]{0,2,1,3:T(4,128)S(1)} %copy.171, f32[64,4,3,128]{0,2,1,3:T(4,128)} %copy.160), kind=kLoop, calls=%fused_computation.12 | loop fusion | flops 655360 | bytes 2621440 | tf_op jit(solution)/shard_map/concatenate | solution.py:161
  80.5 3.0 %fusion.11 = f32[64,4,7,128]{0,2,1,3:T(8,128)} fusion(f32[64,4,3,128]{0,2,1,3:T(4,128)S(1)} %copy.162, f32[64,4,4,128]{0,2,1,3:T(4,128)S(1)} %copy.171, f32[64,4,3,128]{0,2,1,3:T(4,128)S(1)} %copy-done.1, f32[64,4,10,128]{0,2,1,3:T(8,128)S(1)} %pad_maximum_fusion), kind=kLoop, calls=%fused_computation.30 | loop fusion | flops 1605632 | bytes 4063232 | tf_op jit(solution)/shard_map/sub | solution.py:35
  85.9 8.3 %fusion.8 = f32[64,4,5,128]{0,2,1,3:T(8,128)S(1)} fusion(f32[64,4,4,128]{0,2,1,3:T(4,128)S(1)} %copy.171, f32[64,4,3,128]{0,2,1,3:T(4,128)S(1)} %copy.162, f32[64,4,3,128]{0,2,1,3:T(4,128)} %copy.160, f32[64,4,7,128]{0,2,1,3:T(8,128)} %fusion.11, f32[4,5,128]{1,0,2:T(4,128)} %copy.170, f32[4,5,128]{1,0,2:T(4,128)} %copy.169, f32[4,5,128]{1,0,2:T(4,128)S(1)} %copy.168, ...), kind=kLoop, calls=%fused_computation.27 | loop fusion | flops 3768320 | bytes 3985920 | tf_op jit(solution)/shard_map/jit(_where)/select_n | solution.py:56
  96.0 4.3 %all-to-all-start = ((bf16[4,2,16384]{2,1,0:T(2,128)(2,1)}), bf16[4,2,16384]{2,1,0:T(2,128)(2,1)S(1)}, u32[]{:S(2)}, u32[]{:S(2)}) async-start(bf16[4,2,16384]{2,1,0:T(2,128)(2,1)} %reshape.1293), calls=%async_computation | async-start | bytes 524288 | tf_op jit(solution)/shard_map/all_to_all | solution.py:167
  100.3 5.0 %all-to-all-done = bf16[4,2,16384]{2,1,0:T(2,128)(2,1)S(1)} async-done(((bf16[4,2,16384]{2,1,0:T(2,128)(2,1)}), bf16[4,2,16384]{2,1,0:T(2,128)(2,1)S(1)}, u32[]{:S(2)}, u32[]{:S(2)}) %all-to-all-start) | async-done | bytes 262176 | tf_op jit(solution)/shard_map/all_to_all | solution.py:167
  107.7 1.8 %reshape.1160 = f32[256,4,128]{0,2,1:T(8,128)S(1)} reshape(f32[4,64,4,4,32]{1,0,4,3,2:T(4,128)} %copy.185) | data formatting | bytes 1048576 | tf_op jit(solution)/shard_map/convert_element_type | solution.py:174
  109.6 3.3 %scatter_custom_fusion = bf16[256,1024]{0,1:T(8,128)(2,1)} fusion(s32[512]{0:T(512)} %bitcast.249, bf16[256,512]{0,1:T(8,128)(2,1)S(1)} %reshape.1226, bf16[]{:T(256)} %constant.130.clone.1), kind=kCustom, calls=%fused_computation.108 | custom fusion | bytes 786944 | tf_op jit(solution)/shard_map/scatter | solution.py:112
  112.8 1.6 fusion.62
  114.5 2.2 %gather_fusion.1 = f32[512,256]{1,0:T(8,128)} fusion(f32[256,1024]{0,1:T(8,128)S(1)} %bitcast.222, s32[1024]{0:T(1024)S(1)} %copy-done.29), kind=kCustom, calls=%fused_computation.1.clone | custom fusion | bytes 1050624 | tf_op jit(solution)/shard_map/jit(_take)/gather | solution.py:125
  116.8 1.7 fusion.34
  118.4 3.3 %scatter_custom_fusion.1 = bf16[256,1024]{0,1:T(8,128)(2,1)} fusion(s32[512]{0:T(512)} %bitcast.250, bf16[512,256]{1,0:T(8,128)(2,1)S(1)} %fusion.34, bf16[]{:T(256)} %constant.130.clone.1), kind=kCustom, calls=%fused_computation.114 | custom fusion | bytes 524800 | tf_op jit(solution)/shard_map/scatter | solution.py:112
  121.7 1.6 fusion.60
  123.4 2.2 %gather_fusion.3 = f32[512,256]{1,0:T(8,128)} fusion(f32[256,1024]{0,1:T(8,128)S(1)} %bitcast.220, s32[1024]{0:T(1024)S(1)} %copy-done.28), kind=kCustom, calls=%fused_computation.5.clone | custom fusion | bytes 1050624 | tf_op jit(solution)/shard_map/jit(_take)/gather | solution.py:125
  125.6 1.7 fusion.33
  127.3 3.3 %scatter_custom_fusion.2 = bf16[256,1024]{0,1:T(8,128)(2,1)} fusion(s32[512]{0:T(512)} %bitcast.251, bf16[512,256]{1,0:T(8,128)(2,1)S(1)} %fusion.33, bf16[]{:T(256)} %constant.130.clone.1), kind=kCustom, calls=%fused_computation.112 | custom fusion | bytes 524800 | tf_op jit(solution)/shard_map/scatter | solution.py:112
  132.2 2.5 %gather_fusion.5 = f32[512,256]{1,0:T(8,128)} fusion(f32[256,1024]{0,1:T(8,128)S(1)} %bitcast.223, s32[1024]{0:T(1024)S(1)} %copy-done.27), kind=kCustom, calls=%fused_computation.6.clone | custom fusion | bytes 1050624 | tf_op jit(solution)/shard_map/jit(_take)/gather | solution.py:125
  134.7 1.7 fusion.32
  136.4 3.1 %scatter_custom_fusion.3 = bf16[256,1024]{0,1:T(8,128)(2,1)} fusion(s32[512]{0:T(512)S(1)} %bitcast.252, bf16[512,256]{1,0:T(8,128)(2,1)S(1)} %fusion.32, bf16[]{:T(256)} %constant.130.clone.1), kind=kCustom, calls=%fused_computation.110 | custom fusion | bytes 524290 | tf_op jit(solution)/shard_map/scatter | solution.py:112
  139.5 1.6 fusion.56
  144.0 1.9 %copy.186 = f32[256,4,4,32]{3,2,1,0:T(4,128)} copy(f32[256,4,4,32]{0,3,2,1:T(8,128)S(1)} %pad_maximum_fusion.6) | data formatting | bytes 1048576 | tf_op jit(solution)/shard_map/stack | solution.py:94
  145.9 2.6 %reshape.1295 = f32[4,1,32768]{2,1,0:T(1,128)S(1)} reshape(f32[256,4,4,32]{3,2,1,0:T(4,128)} %copy.186) | data formatting | bytes 1048576
  148.5 11.1 %all_to_all.33 = f32[4,1,32768]{2,1,0:T(1,128)S(1)} all-to-all(f32[4,1,32768]{2,1,0:T(1,128)S(1)} %reshape.1295), channel_id=1, replica_groups=mesh['tile'=128,'trc'=4] {'trc'}, dimensions={0} | all-to-all | bytes 1048576 | tf_op jit(solution)/shard_map/all_to_all | solution.py:177
  160.1 2.1 %reduce.8 = f32[4,32768]{1,0:T(4,128)S(1)} reduce(f32[4,1,32768]{2,1,0:T(1,128)S(1)} %all_to_all.33, f32[]{:T(128)} %broadcast.1161), dimensions={1}, to_apply=%all_to_all.27.reduce_sub_computation | reduce | bytes 1048580 | tf_op jit(solution)/shard_map/all_to_all | solution.py:177
  162.3 2.5 %reshape.1296 = f32[256,4,4,32]{3,2,1,0:T(4,128)} reshape(f32[4,32768]{1,0:T(4,128)S(1)} %reduce.8) | data formatting | bytes 1048576
  164.8 1.9 %copy.188 = f32[64,4,4,4,32]{0,4,3,2,1:T(8,128)S(1)} copy(f32[64,4,4,4,32]{4,2,1,0,3:T(4,128)} %bitcast.224) | data formatting | bytes 1048576 | tf_op jit(solution)/shard_map/all_to_all | solution.py:177
  (253 shorter events, 54.7 us)
Async XLA Ops:
  0.0 48.4 %copy-start = (bf16[4,256,256]{2,1,0:T(8,128)(2,1)S(1)}, bf16[4,256,256]{2,1,0:T(8,128)(2,1)}, u32[]{:S(2)}) copy-start(bf16[4,256,256]{2,1,0:T(8,128)(2,1)} %param.19) | copy-start | bytes 1572868
  0.0 21.7 %copy-start.3 = (f32[64,4,4,128]{3,2,1,0:T(4,128)S(1)}, f32[64,4,4,128]{3,2,1,0:T(4,128)}, u32[]{:S(2)}) copy-start(f32[64,4,4,128]{3,2,1,0:T(4,128)} %param.13) | copy-start | bytes 1572868
  0.0 22.4 %copy-start.22 = (f32[4,4,128]{2,1,0:T(4,128)S(1)}, f32[4,4,128]{2,1,0:T(4,128)}, u32[]{:S(2)}) copy-start(f32[4,4,128]{2,1,0:T(4,128)} %param.14) | copy-start | bytes 24580
  3.0 68.7 %collective-permute-start = (f32[65,4,3,128]{3,1,2,0:T(4,128)}, f32[65,4,3,128]{3,1,2,0:T(4,128)S(1)}, u32[]{:S(2)}, u32[]{:S(2)}) collective-permute-start(f32[65,4,3,128]{3,1,2,0:T(4,128)} %get-tuple-element.46), channel_id=1, source_target_pairs={{4,0},{8,4},{12,8},{16,12},{20,16},{24,20},{28,24},{32,28},{36,32}... | collective-permute-start | bytes 1198088 | tf_op jit(solution)/shard_map/ppermute | solution.py:18
  19.7 53.4 %collective-permute-start.1 = (f32[65,4,3,128]{3,1,2,0:T(4,128)}, f32[65,4,3,128]{3,1,2,0:T(4,128)}, u32[]{:S(2)}, u32[]{:S(2)}) collective-permute-start(f32[65,4,3,128]{3,1,2,0:T(4,128)} %get-tuple-element.45), channel_id=1, source_target_pairs={{0,4},{4,8},{8,12},{12,16},{16,20},{20,24},{24,28},{28,32},{32,36}... | collective-permute-start | bytes 1198088 | tf_op jit(solution)/shard_map/ppermute | solution.py:15
  35.3 5.3 %copy-start.33 = (s32[4,128]{1,0:T(4,128)S(1)}, s32[4,128]{1,0:T(4,128)}, u32[]{:S(2)}) copy-start(s32[4,128]{1,0:T(4,128)} %eq.156) | copy-start | bytes 6148
  35.3 8.4 %copy-start.14 = (s32[512]{0:T(512)S(1)}, s32[512]{0:T(512)}, u32[]{:S(2)}) copy-start(s32[512]{0:T(512)} %eq.128) | copy-start | bytes 6148
  35.3 8.8 %copy-start.18 = (s32[512]{0:T(512)S(1)}, s32[512]{0:T(512)}, u32[]{:S(2)}) copy-start(s32[512]{0:T(512)} %eq.144) | copy-start | bytes 6148
  35.3 9.1 %copy-start.16 = (s32[512]{0:T(512)S(1)}, s32[512]{0:T(512)}, u32[]{:S(2)}) copy-start(s32[512]{0:T(512)} %eq.136) | copy-start | bytes 6148
  35.3 9.4 %copy-start.58 = (s32[8]{0:T(128)S(1)}, s32[8]{0:T(128)}, u32[]{:S(2)}) copy-start(s32[8]{0:T(128)} %iota_multiply_fusion) | copy-start | bytes 100
  35.3 10.1 %copy-start.32 = (s32[4,128]{1,0:T(4,128)S(1)}, s32[4,128]{1,0:T(4,128)}, u32[]{:S(2)}) copy-start(s32[4,128]{1,0:T(4,128)} %eq.148) | copy-start | bytes 6148
  50.0 6.1 %copy-start.30 = (s32[4,128]{1,0:T(4,128)S(1)}, s32[4,128]{1,0:T(4,128)}, u32[]{:S(2)}) copy-start(s32[4,128]{1,0:T(4,128)} %eq.132) | copy-start | bytes 6148
  53.9 6.2 %copy-start.49 = (s32[4,32]{1,0:T(4,128)S(1)}, s32[4,32]{1,0:T(4,128)}, u32[]{:S(2)}) copy-start(s32[4,32]{1,0:T(4,128)} %param.17) | copy-start | bytes 1540
  53.9 6.8 %copy-start.34 = (f32[3,4,32]{2,1,0:T(4,128)S(1)}, f32[3,4,32]{2,1,0:T(4,128)}, u32[]{:S(2)}) copy-start(f32[3,4,32]{2,1,0:T(4,128)} %param.21) | copy-start | bytes 4612
  58.5 12.0 %copy-start.23 = (s32[512]{0:T(512)}, s32[512]{0:T(512)S(1)}, u32[]{:S(2)}) copy-start(s32[512]{0:T(512)S(1)} %get-tuple-element.30) | copy-start | bytes 6148
  60.8 10.2 %copy-start.35 = (f32[128]{0:T(128)}, f32[128]{0:T(128)S(1)}, u32[]{:S(2)}) copy-start(f32[128]{0:T(128)S(1)} %squeeze.10) | copy-start | bytes 1540
  60.9 10.2 %copy-start.37 = (f32[128]{0:T(128)}, f32[128]{0:T(128)S(1)}, u32[]{:S(2)}) copy-start(f32[128]{0:T(128)S(1)} %squeeze.11) | copy-start | bytes 1540
  61.0 10.1 %copy-start.39 = (f32[128]{0:T(128)}, f32[128]{0:T(128)S(1)}, u32[]{:S(2)}) copy-start(f32[128]{0:T(128)S(1)} %squeeze.9) | copy-start | bytes 1540
  85.9 8.3 %copy-start.2 = (f32[64,4,4,129]{0,2,1,3:T(4,128)S(1)}, f32[64,4,4,129]{0,2,1,3:T(4,128)}, u32[]{:S(2)}) copy-start(f32[64,4,4,129]{0,2,1,3:T(4,128)} %multiply_select_fusion) | copy-start | bytes 1585156
  94.2 6.0 %copy-start.24 = (s32[512]{0:T(512)S(1)}, s32[512]{0:T(512)}, u32[]{:S(2)}) copy-start(s32[512]{0:T(512)} %copy-done.23) | copy-start | bytes 6148
  96.0 9.4 %all-to-all-start = ((bf16[4,2,16384]{2,1,0:T(2,128)(2,1)}), bf16[4,2,16384]{2,1,0:T(2,128)(2,1)S(1)}, u32[]{:S(2)}, u32[]{:S(2)}) async-start(bf16[4,2,16384]{2,1,0:T(2,128)(2,1)} %reshape.1293), calls=%async_computation | async-start | bytes 524288 | tf_op jit(solution)/shard_map/all_to_all | solution.py:167
  106.1 6.7 %copy-start.6 = (bf16[8,256,256]{2,1,0:T(8,128)(2,1)S(1)}, bf16[8,256,256]{2,1,0:T(8,128)(2,1)}, u32[]{:S(2)}) copy-start(bf16[8,256,256]{2,1,0:T(8,128)(2,1)} %gather_fusion) | copy-start | bytes 3145732
  106.1 6.7 %copy-start.54 = (pred[8]{0:T(512)(128)(4,1)S(1)}, pred[8]{0:T(512)(128)(4,1)}, u32[]{:S(2)}) copy-start(pred[8]{0:T(512)(128)(4,1)} %get-tuple-element.71) | copy-start | bytes 28
  114.5 7.2 %copy-start.4 = (bf16[8,256,256]{2,1,0:T(8,128)(2,1)S(1)}, bf16[8,256,256]{2,1,0:T(8,128)(2,1)}, u32[]{:S(2)}) copy-start(bf16[8,256,256]{2,1,0:T(8,128)(2,1)} %gather_fusion.2) | copy-start | bytes 3145732
  114.5 7.2 %copy-start.53 = (pred[8]{0:T(512)(128)(4,1)S(1)}, pred[8]{0:T(512)(128)(4,1)}, u32[]{:S(2)}) copy-start(pred[8]{0:T(512)(128)(4,1)} %get-tuple-element.39) | copy-start | bytes 28
  116.7 6.6 %copy-start.28 = (s32[1024]{0:T(1024)S(1)}, s32[1024]{0:T(1024)}, u32[]{:S(2)}) copy-start(s32[1024]{0:T(1024)} %get-tuple-element.75) | copy-start | bytes 12292
  123.3 7.2 %copy-start.5 = (bf16[8,256,256]{2,1,0:T(8,128)(2,1)S(1)}, bf16[8,256,256]{2,1,0:T(8,128)(2,1)}, u32[]{:S(2)}) copy-start(bf16[8,256,256]{2,1,0:T(8,128)(2,1)} %gather_fusion.4) | copy-start | bytes 3145732
  123.3 7.2 %copy-start.56 = (pred[8]{0:T(512)(128)(4,1)S(1)}, pred[8]{0:T(512)(128)(4,1)}, u32[]{:S(2)}) copy-start(pred[8]{0:T(512)(128)(4,1)} %get-tuple-element.69) | copy-start | bytes 28
  125.6 6.6 %copy-start.27 = (s32[1024]{0:T(1024)S(1)}, s32[1024]{0:T(1024)}, u32[]{:S(2)}) copy-start(s32[1024]{0:T(1024)} %get-tuple-element.74) | copy-start | bytes 12292
  132.2 7.3 %copy-start.7 = (bf16[8,256,256]{2,1,0:T(8,128)(2,1)S(1)}, bf16[8,256,256]{2,1,0:T(8,128)(2,1)}, u32[]{:S(2)}) copy-start(bf16[8,256,256]{2,1,0:T(8,128)(2,1)} %gather_fusion.6) | copy-start | bytes 3145732
  132.2 7.3 %copy-start.55 = (pred[8]{0:T(512)(128)(4,1)S(1)}, pred[8]{0:T(512)(128)(4,1)}, u32[]{:S(2)}) copy-start(pred[8]{0:T(512)(128)(4,1)} %get-tuple-element.31) | copy-start | bytes 28
  134.7 6.4 %copy-start.26 = (s32[1024]{0:T(1024)S(1)}, s32[1024]{0:T(1024)}, u32[]{:S(2)}) copy-start(s32[1024]{0:T(1024)} %get-tuple-element.73) | copy-start | bytes 12292
  (30 other events, 61.9 us)
where the time goes:
time: 169 us; the launch traced here: 168 us
  local copies, waits for them, and re-layouts  70.2 us (42%)
  other arithmetic  44.1 us (26%)
  starting transfers between devices  23 us (14%)
  matrix products  12 us (7%)
  blocking collectives  11.1 us (7%)
  waiting for transfers between devices  5.04 us (3%)
  between operations  2.32 us (1%)
    ppermute x1, starting transfers between devices, padded_2(): lax.ppermute(lax.slice_in_dim(block, 0, width, axis=dim), axis, backward)  16.8 us
    select_n x2, other arithmetic, sweep_flux(): return jnp.where(courant > 0.0, flux_pos, flux_neg)  16.6 us
    scatter x4, local copies, waits for them, and re-layouts, grouped_maps(): jnp.zeros((species, capacity), jnp.bfloat16).at[:, target].set(values)  12.9 us
    all_to_all x1, blocking collectives, shards(): lax.all_to_all(tracer_back, 'trc', split_axis=0, concat_axis=3, tiled=True)  11.1 us
    unnamed x125, local copies, waits for them, and re-layouts  8.77 us
    gather x4, local copies, waits for them, and re-layouts, grouped_maps(): gathered = jnp.take(product.reshape(species, capacity), target, axis=1)  8.54 us
    another operation x12, other arithmetic  6.52 us
    gather x4, local copies, waits for them, and re-layouts, grouped_maps(): chosen = jnp.take(linear_maps, tile_entry, axis=0)  6.42 us
  transfers between devices with their start and end apart: 3, of which 1 were waited for; matrix products, arithmetic and copies ran while one was open for 30% of the time, Pallas kernels for 0%

commit v1 on v0

v1 whole, which is shorter than its diff:
```python
import functools

import jax
import jax.numpy as jnp
from jax import lax
from jax.experimental import pallas as pl
from jax.experimental.pallas import tpu as pltpu
from jax.sharding import PartitionSpec as P

F32 = jnp.float32
BF16 = jnp.bfloat16
LANES = 128
CHUNK = 16


def vmem():
    return pl.BlockSpec(memory_space=pltpu.VMEM)


def smem():
    return pl.BlockSpec(memory_space=pltpu.SMEM)


def params(mib):
    return pltpu.CompilerParams(vmem_limit_bytes=mib << 20)


def flux_weights(courant):
    speed = jnp.abs(courant)
    rest = 1.0 - speed
    return (
        courant * rest * rest,
        -courant * speed * rest,
        courant * speed * (3.0 - 2.0 * speed),
        courant > 0.0,
    )


def edge_value(outer_low, inner_low, inner_high, outer_high):
    return (7.0 / 12.0) * (inner_low + inner_high) - (1.0 / 12.0) * (outer_low + outer_high)


def face_flux(weights, values_low, values_mid, values_high, cell_low, cell_high):
    w_mid, w_far, w_centre, positive = weights
    far = jnp.where(positive, values_low, values_high)
    centre = jnp.where(positive, cell_low, cell_high)
    return w_mid * values_mid + w_far * far + w_centre * centre


def block_transpose(rows, lane):
    low = lane < 64
    even = (lane & 32) == 0
    r0, r1, r2, r3 = rows
    b0 = jnp.where(low, r0, pltpu.roll(r2, 64, 1))
    b2 = jnp.where(low, pltpu.roll(r0, 64, 1), r2)
    b1 = jnp.where(low, r1, pltpu.roll(r3, 64, 1))
    b3 = jnp.where(low, pltpu.roll(r1, 64, 1), r3)
    return (
        jnp.where(even, b0, pltpu.roll(b1, 32, 1)),
        jnp.where(even, pltpu.roll(b0, 96, 1), b1),
        jnp.where(even, b2, pltpu.roll(b3, 32, 1)),
        jnp.where(even, pltpu.roll(b2, 96, 1), b3),
    )


def pack_kernel(levels, width, quarter, x_ref, u_ref, next_ref, prev_ref):
    grid = levels * width
    for level in range(levels):
        for col in range(width):
            values = x_ref[pl.ds(level * width + col, quarter, stride=grid), :].astype(BF16)
            if col >= width - 3:
                row = (level * 3 + col - (width - 3)) * quarter
                next_ref[row : row + quarter, :] = values
            if col < 3:
                row = (level * 3 + col) * quarter
                prev_ref[row : row + quarter, :] = values
    first = u_ref[pl.ds(0, levels, stride=width), :]
    high = first.astype(BF16).astype(F32)
    rest = first - high
    mid = rest.astype(BF16).astype(F32)
    low = rest - mid
    row = levels * 3 * quarter
    parts = jnp.concatenate([high, mid, low, jnp.zeros_like(low)], axis=0)
    prev_ref[row : row + 4 * levels, :] = parts.astype(BF16)


def edge_kernel(levels, width, quarter, x_ref, u_ref, base_ref):
    grid = levels * width
    lane = lax.broadcasted_iota(jnp.int32, (CHUNK, LANES), 1)
    first = lane == 0
    last = lane == LANES - 1
    for cell in range(grid):
        courant = jnp.where(first, 0.0, jnp.broadcast_to(u_ref[cell : cell + 1, :], lane.shape))
        weights = flux_weights(courant)
        for start in range(0, quarter, CHUNK):
            x = x_ref[pl.ds(start * grid + cell, CHUNK, stride=grid), :]
            below = jnp.where(first, x, pltpu.roll(x, 1, 1))
            below2 = jnp.where(first, below, pltpu.roll(below, 1, 1))
            above = jnp.where(last, x, pltpu.roll(x, LANES - 1, 1))
            mid = edge_value(below2, below, x, above)
            end = (13.0 / 12.0) * x - (1.0 / 12.0) * below
            after = jnp.where(last, end, pltpu.roll(mid, LANES - 1, 1))
            flux = face_flux(weights, pltpu.roll(mid, 1, 1), mid, after, below, x)
            base_ref[cell, start : start + CHUNK, :] = x + (flux - pltpu.roll(flux, LANES - 1, 1))


def flow_kernel(
    levels, width, quarter, flag_ref, x_ref, base_ref, u_ref, before_ref, after_ref, out_ref
):
    grid = levels * width
    lane = lax.broadcasted_iota(jnp.int32, (CHUNK, LANES), 1)
    turn_before = jnp.where(flag_ref[0, 0] > 0, LANES - 1 - lane, lane)
    turn_after = jnp.where(flag_ref[0, 1] > 0, LANES - 1 - lane, lane)
    tail = levels * 3 * quarter
    split = after_ref[tail : tail + 4 * levels, :].astype(F32)
    split = jnp.take_along_axis(split, turn_after, axis=1)
    closing = split[0:levels] + split[levels : 2 * levels] + split[2 * levels : 3 * levels]
    for level in range(levels):
        faces = [u_ref[level * width + f : level * width + f + 1, :] for f in range(width)]
        faces.append(closing[level : level + 1, :])
        weights = [flux_weights(jnp.broadcast_to(f, lane.shape)) for f in faces]
        for start in range(0, quarter, CHUNK):
            cells = []
            for col in range(3):
                row = (level * 3 + col) * quarter + start
                halo = before_ref[row : row + CHUNK, :].astype(F32)
                cells.append(jnp.take_along_axis(halo, turn_before, axis=1))
            for col in range(width):
                cells.append(
                    x_ref[pl.ds(start * grid + level * width + col, CHUNK, stride=grid), :]
                )
            for col in range(3):
                row = (level * 3 + col) * quarter + start
                halo = after_ref[row : row + CHUNK, :].astype(F32)
                cells.append(jnp.take_along_axis(halo, turn_after, axis=1))
            values = [edge_value(*cells[i : i + 4]) for i in range(width + 3)]
            fluxes = [
                face_flux(weights[f], *values[f : f + 3], cells[f + 2], cells[f + 3])
                for f in range(width + 1)
            ]
            moved = [
                base_ref[level * width + col, start : start + CHUNK, :]
                + (fluxes[col] - fluxes[col + 1])
                for col in range(width)
            ]
            for part, rows in enumerate(block_transpose(moved, lane)):
                out_ref[part, level, start : start + CHUNK, :] = rows.astype(BF16)


def chem_kernel(
    levels, quarter, x_ref, entry_ref, sun_ref, mix_ref, map_ref, off_ref, out_ref, chem_ref
):
    parts = x_ref.shape[0]
    species = parts * quarter
    entries = map_ref.shape[0] // species
    substeps = entry_ref.shape[0] // levels
    halves = levels // 2
    start = []
    for half in range(halves):
        pair = [
            jnp.concatenate([x_ref[p, 2 * half + k] for p in range(parts)], axis=0)
            for k in range(2)
        ]
        start.append(jnp.concatenate(pair, axis=1))
    state = list(start)
    result = [None] * halves
    for step in range(substeps):
        for half in range(halves):
            product = jnp.dot(map_ref[...], state[half], preferred_element_type=F32)
            row = step * levels + 2 * half
            entry = jnp.concatenate(
                [entry_ref[row : row + 1, :], entry_ref[row + 1 : row + 2, :]], axis=1
            )
            chosen = product[0:species] + off_ref[:, 0:1]
            for e in range(1, entries):
                chosen = jnp.where(
                    entry == e,
                    product[e * species : (e + 1) * species] + off_ref[:, e : e + 1],
                    chosen,
                )
            result[half] = jnp.maximum(chosen, 0.0)
            state[half] = result[half].astype(BF16)
    lit = jnp.concatenate([sun_ref[...], sun_ref[...]], axis=1) > 0
    for half in range(halves):
        chem = jnp.where(lit, result[half], start[half].astype(F32))
        chem_ref[2 * half] = chem[:, 0:LANES]
        chem_ref[2 * half + 1] = chem[:, LANES : 2 * LANES]
    mixing = [mix_ref[k : k + 1, :] for k in range(levels - 1)]
    inverse, ratio = [], []
    for level in range(levels):
        diagonal = 1.0
        if level > 0:
            diagonal = diagonal + mixing[level - 1]
        if level < levels - 1:
            diagonal = diagonal + mixing[level]
        if level > 0:
            diagonal = diagonal - mixing[level - 1] * ratio[level - 1]
        inverse.append(1.0 / diagonal)
        if level < levels - 1:
            ratio.append(mixing[level] * inverse[level])
    for p in range(parts):
        for begin in range(0, quarter, CHUNK):
            rows = slice(p * quarter + begin, p * quarter + begin + CHUNK)
            solved = []
            for level in range(levels):
                value = chem_ref[level, rows, :]
                if level > 0:
                    value = value + mixing[level - 1] * solved[-1]
                solved.append(value * inverse[level])
            for level in range(levels - 2, -1, -1):
                solved[level] = solved[level] + ratio[level] * solved[level + 1]
            for level in range(levels):
                out_ref[p, level, begin : begin + CHUNK, :] = solved[level].astype(BF16)


def unpack_kernel(levels, width, quarter, y_ref, out_ref):
    grid = levels * width
    lane = lax.broadcasted_iota(jnp.int32, (CHUNK, LANES), 1)
    for level in range(levels):
        for start in range(0, quarter, CHUNK):
            rows = [y_ref[q, level, start : start + CHUNK, :].astype(F32) for q in range(4)]
            for col, values in enumerate(block_transpose(rows, lane)):
                out_ref[pl.ds(start * grid + level * width + col, CHUNK, stride=grid), :] = values


def shards(
    tracers,
    courant_cycle,
    courant_edge,
    seam_flags,
    sunlit,
    table_entry,
    linear_maps,
    offsets,
    mixing,
):
    quarter, levels, width, length = tracers.shape
    grid = levels * width
    substeps = table_entry.shape[0]
    entries, species, _ = linear_maps.shape
    count = lax.axis_size("tile")
    parts = lax.axis_size("trc")
    forward = [(i, (i + 1) % count) for i in range(count)]
    backward = [(target, source) for source, target in forward]
    x = tracers.reshape(quarter * grid, length)
    cycle = courant_cycle.reshape(grid, length)
    halo = levels * 3 * quarter
    to_next, to_prev = pl.pallas_call(
        functools.partial(pack_kernel, levels, width, quarter),
        out_shape=(
            jax.ShapeDtypeStruct((halo, length), BF16),
            jax.ShapeDtypeStruct((halo + 4 * levels, length), BF16),
        ),
        in_specs=[vmem()] * 2,
        out_specs=(vmem(), vmem()),
        compiler_params=params(8),
        name="pack",
    )(x, cycle)
    before = lax.ppermute(to_next, "tile", forward)
    after = lax.ppermute(to_prev, "tile", backward)
    base = pl.pallas_call(
        functools.partial(edge_kernel, levels, width, quarter),
        out_shape=jax.ShapeDtypeStruct((grid, quarter, length), F32),
        in_specs=[vmem()] * 2,
        out_specs=vmem(),
        compiler_params=params(8),
        cost_estimate=pl.CostEstimate(flops=4000000, bytes_accessed=1 << 20, transcendentals=0),
        name="edge",
    )(x, courant_edge.reshape(grid, length))
    moved = pl.pallas_call(
        functools.partial(flow_kernel, levels, width, quarter),
        out_shape=jax.ShapeDtypeStruct((parts, levels, quarter, length), BF16),
        in_specs=[smem()] + [vmem()] * 5,
        out_specs=vmem(),
        compiler_params=params(8),
        name="flow",
    )(seam_flags, x, base, cycle, before, after)
    boxes = lax.all_to_all(moved, "trc", split_axis=0, concat_axis=0, tiled=True)
    mixed = pl.pallas_call(
        functools.partial(chem_kernel, levels, quarter),
        out_shape=jax.ShapeDtypeStruct((parts, levels, quarter, length), BF16),
        in_specs=[vmem()] * 6,
        out_specs=vmem(),
        scratch_shapes=[pltpu.VMEM((levels, species, length), F32)],
        compiler_params=params(24),
        name="chem",
    )(
        boxes,
        table_entry.reshape(substeps * levels, length),
        sunlit.reshape(1, length),
        mixing.reshape(levels - 1, length),
        linear_maps.reshape(entries * species, species),
        offsets.T,
    )
    back = lax.all_to_all(mixed, "trc", split_axis=0, concat_axis=0, tiled=True)
    out = pl.pallas_call(
        functools.partial(unpack_kernel, levels, width, quarter),
        out_shape=jax.ShapeDtypeStruct((quarter * grid, length), F32),
        in_specs=[vmem()],
        out_specs=vmem(),
        compiler_params=params(8),
        name="unpack",
    )(back)
    return out.reshape(quarter, levels, width, length)


def solution(mesh):
    placed = (
        P("trc", None, "tile", None),
        P(None, "tile", None),
        P(None, "tile", None),
        P("tile", None),
        P("tile", "trc"),
        P(None, None, "tile", "trc"),
        P(),
        P(),
        P(None, "tile", "trc"),
    )
    return jax.shard_map(
        shards, mesh=mesh, in_specs=placed, out_specs=P("trc", None, "tile", None), check_vma=False
    )
```

time: 169 us -> 56.9 us (0.34)
  local copies, waits for them, and re-layouts: 70.2 us -> 3.97 us
  other arithmetic: 44.1 us -> 0 us
  Pallas kernels: 0 us -> 14.9 us
  matrix products: 12 us -> 0 us
  blocking collectives: 11.1 us -> 8.33 us
  between operations: 2.32 us -> 0.08 us
    select_n x13 -> x0, other arithmetic: 19.7 us -> none  [the longest x2 16.6 us: sweep_flux(): return jnp.where(courant > 0.0, flux_pos, flux_neg)]
    gather x8 -> x0, local copies, waits for them, and re-layouts: 15 us -> none  [the longest x4 8.54 us: grouped_maps(): gathered = jnp.take(product.reshape(species, capacity), target, axis=1)]
    pallas_call x0 -> x5, Pallas kernels: none -> 14.9 us  [the longest x1 8.87 us: shards(): pl.pallas_call(functools.partial(edge_kernel, levels, width, quarter), ou...]
    scatter x4 -> x0, local copies, waits for them, and re-layouts: 12.9 us -> none  [grouped_maps(): jnp.zeros((species, capacity), jnp.bfloat16).at[:, target].set(values)]
    dot_general x8 -> x0, matrix products: 12 us -> none  [the longest x4 6.36 us: grouped_maps(): jnp.einsum('toi,itb->otb', chosen, buffer.reshape(species, tile_count, bl...]
    slice x12 -> x0, local copies, waits for them, and re-layouts: 6.94 us -> none  [the longest x1 1.42 us: shards(): before[:quarter]]
    another operation x13 -> x0, other arithmetic: 6.56 us -> none
    eq x8 -> x0, local copies, waits for them, and re-layouts: 5.35 us -> none  [grouped_maps(): entry_ids[:, None] == jnp.arange(entries, dtype=jnp.int32)[None, :]]
  transfers between devices with their start and end apart: 3 -> 3, of which waited for: 1 -> 2; matrix products, arithmetic and copies ran while one was open for 30% -> 1% of each run, Pallas kernels for 0% -> 16%
where the time goes in v1:
time: 56.9 us; the launch traced here: 56.4 us
  starting transfers between devices  24.1 us (42%)
  Pallas kernels  14.9 us (26%)
  blocking collectives  8.33 us (15%)
  waiting for transfers between devices  5.11 us (9%)
  local copies, waits for them, and re-layouts  3.97 us (7%)
    ppermute x1, starting transfers between devices, shards(): after = lax.ppermute(to_prev, 'tile', backward)  16.8 us
    pallas_call x1, Pallas kernels, shards(): pl.pallas_call(functools.partial(edge_kernel, levels, width, quarter), ou...  8.87 us
    all_to_all x1, blocking collectives, shards(): back = lax.all_to_all(mixed, 'trc', split_axis=0, concat_axis=0, tiled=True)  8.33 us
    all_to_all x1, starting transfers between devices, shards(): lax.all_to_all(moved, 'trc', split_axis=0, concat_axis=0, tiled=True)  5.41 us
    unnamed x21, local copies, waits for them, and re-layouts  3.72 us
    all_to_all x1, waiting for transfers between devices, shards(): lax.all_to_all(moved, 'trc', split_axis=0, concat_axis=0, tiled=True)  2.82 us
    pallas_call x1, Pallas kernels, shards(): pl.pallas_call(functools.partial(flow_kernel, levels, width, quarter), ou...  2.69 us
    ppermute x1, waiting for transfers between devices, shards(): before = lax.ppermute(to_next, 'tile', forward)  2.28 us
  transfers between devices with their start and end apart: 3, of which 2 were waited for; matrix products, arithmetic and copies ran while one was open for 1% of the time, Pallas kernels for 16%

profile of v1, /device:TPU:1, one launch (start us, length us, event | category | flops | bytes accessed | tf_op | source)
XLA Modules:
  0.0 56.4 jit_solution(7543311087649914210)
XLA Ops:
  0.0 0.0 copy-start
  0.0 1.0 %copy-done = f32[64,4,4,128]{3,2,1,0:T(4,128)S(1)} copy-done((f32[64,4,4,128]{3,2,1,0:T(4,128)S(1)}, f32[64,4,4,128]{3,2,1,0:T(4,128)}, u32[]{:S(2)}) %copy-start) | copy-done | bytes 524312
  1.0 0.0 copy-start.2
  1.0 0.7 %copy-done.2 = f32[4,4,128]{2,1,0:T(4,128)S(1)} copy-done((f32[4,4,128]{2,1,0:T(4,128)S(1)}, f32[4,4,128]{2,1,0:T(4,128)}, u32[]{:S(2)}) %copy-start.2) | copy-done | bytes 8216
  1.7 0.0 copy-start.4
  1.7 0.2 pack.1
  1.9 16.8 %collective-permute-start.1 = (bf16[784,128]{1,0:T(8,128)(2,1)S(1)}, bf16[784,128]{1,0:T(8,128)(2,1)S(1)}, u32[]{:S(2)}, u32[]{:S(2)}) collective-permute-start(bf16[784,128]{1,0:T(8,128)(2,1)S(1)} %get-tuple-element.8), channel_id=1, source_target_pairs={{4,0},{8,4},{12,8},{16,12},{20,16},{24,20},{28,24},{32,28},{36,32}... | collective-permute-start | bytes 602120 | tf_op jit(solution)/shard_map/ppermute | solution.py:260
  18.7 1.9 %collective-permute-start = (bf16[768,128]{1,0:T(8,128)(2,1)S(1)}, bf16[768,128]{1,0:T(8,128)(2,1)S(1)}, u32[]{:S(2)}, u32[]{:S(2)}) collective-permute-start(bf16[768,128]{1,0:T(8,128)(2,1)S(1)} %get-tuple-element.7), channel_id=1, source_target_pairs={{0,4},{4,8},{8,12},{12,16},{16,20},{20,24},{24,28},{28,32},{32,36}... | collective-permute-start | bytes 589832 | tf_op jit(solution)/shard_map/ppermute | solution.py:259
  20.6 0.0 copy-done.4
  20.6 0.0 copy-start.3
  20.6 0.0 copy-start.5
  20.6 8.9 %edge.1.base_ref = f32[16,64,128]{2,1,0:T(8,128)S(1)} custom-call(f32[1024,128]{1,0:T(8,128)S(1)} %bitcast.7, f32[16,128]{1,0:T(8,128)S(1)} %bitcast.13), custom_call_target="tpu_custom_call" | custom-call | flops 4000000 | bytes 1048576 | tf_op jit(solution)/shard_map/edge/pallas_call | solution.py:261
  29.5 2.3 %collective-permute-done.before_ref = bf16[768,128]{1,0:T(8,128)(2,1)S(1)} collective-permute-done((bf16[768,128]{1,0:T(8,128)(2,1)S(1)}, bf16[768,128]{1,0:T(8,128)(2,1)S(1)}, u32[]{:S(2)}, u32[]{:S(2)}) %collective-permute-start) | collective-permute-done | bytes 196640 | tf_op jit(solution)/shard_map/ppermute | solution.py:259
  31.8 0.0 collective-permute-done.1.after_ref
  31.8 0.0 copy-done.3
  31.8 0.0 copy-done.5
  31.8 0.0 copy-start.8
  31.8 2.7 %flow.1 = bf16[4,4,64,128]{3,2,1,0:T(8,128)(2,1)} custom-call(s32[1,2]{1,0:T(1,128)S(1)} %copy-done.5, f32[1024,128]{1,0:T(8,128)S(1)} %bitcast.8, f32[16,64,128]{2,1,0:T(8,128)S(1)} %edge.1.base_ref, f32[16,128]{1,0:T(8,128)S(1)} %bitcast.12, bf16[768,128]{1,0:T(8,128)(2,1)S(1)} %collective-permute-done.before_ref, ...), custom_call_target="tpu_custom_call" | custom-call | tf_op jit(solution)/shard_map/flow/pallas_call | solution.py:270
  34.5 5.4 %all-to-all-start = ((bf16[4,4,64,128]{3,2,1,0:T(8,128)(2,1)}), bf16[4,4,64,128]{3,2,1,0:T(8,128)(2,1)S(1)}, u32[]{:S(2)}, u32[]{:S(2)}) async-start(bf16[4,4,64,128]{3,2,1,0:T(8,128)(2,1)} %flow.1), calls=%async_computation | async-start | bytes 524288 | tf_op jit(solution)/shard_map/all_to_all | solution.py:278
  39.9 0.0 copy-done.8
  39.9 0.1 copy.10
  40.1 0.6 %copy-done.6 = s32[4,4,4,32]{3,2,1,0:T(4,128)S(1)} copy-done((s32[4,4,4,32]{3,2,1,0:T(4,128)S(1)}, s32[4,4,4,32]{3,2,1,0:T(4,128)}, u32[]{:S(2)}) %copy-start.6) | copy-done | bytes 8216
  40.7 0.1 reshape.27.entry_ref
  40.8 0.6 %copy-done.7 = f32[3,4,32]{2,1,0:T(4,128)S(1)} copy-done((f32[3,4,32]{2,1,0:T(4,128)S(1)}, f32[3,4,32]{2,1,0:T(4,128)}, u32[]{:S(2)}) %copy-start.7) | copy-done | bytes 1560
  41.4 0.1 reshape.29.mix_ref
  41.5 0.6 %copy-done.9 = s32[4,32]{1,0:T(4,128)S(1)} copy-done((s32[4,32]{1,0:T(4,128)S(1)}, s32[4,32]{1,0:T(4,128)}, u32[]{:S(2)}) %copy-start.9) | copy-done | bytes 536
  42.1 0.1 reshape.28.sun_ref
  42.2 2.8 %all-to-all-done.x_ref = bf16[4,4,64,128]{3,2,1,0:T(8,128)(2,1)S(1)} async-done(((bf16[4,4,64,128]{3,2,1,0:T(8,128)(2,1)}), bf16[4,4,64,128]{3,2,1,0:T(8,128)(2,1)S(1)}, u32[]{:S(2)}, u32[]{:S(2)}) %all-to-all-start) | async-done | bytes 262176 | tf_op jit(solution)/shard_map/all_to_all | solution.py:278
  45.0 0.0 copy-done.1
  45.0 1.8 %chem.1 = bf16[4,4,64,128]{3,2,1,0:T(8,128)(2,1)S(1)} custom-call(bf16[4,4,64,128]{3,2,1,0:T(8,128)(2,1)S(1)} %all-to-all-done.x_ref, s32[16,128]{1,0:T(8,128)S(1)} %reshape.27.entry_ref, s32[1,128]{1,0:T(1,128)S(1)} %reshape.28.sun_ref, f32[3,128]{1,0:T(4,128)S(1)} %reshape.29.mix_ref, bf16[1024,256]{1,0:T(8,128)(2,1)S(1)} %bitcast.10, f32[256,4]{1,0:T(8,128)S(1)} %bitcast.9), custom_call_target="tpu_custom_call" | custom-call | tf_op jit(solution)/shard_map/chem/pallas_call | solution.py:279
  46.8 8.3 %all_to_all.10.y_ref = bf16[4,4,64,128]{3,2,1,0:T(8,128)(2,1)S(1)} all-to-all(bf16[4,4,64,128]{3,2,1,0:T(8,128)(2,1)S(1)} %chem.1), channel_id=1, replica_groups=mesh['tile'=128,'trc'=4] {'trc'}, dimensions={0} | all-to-all | bytes 524288 | tf_op jit(solution)/shard_map/all_to_all | solution.py:295
  55.1 1.3 %unpack.1 = f32[1024,128]{1,0:T(8,128)} custom-call(bf16[4,4,64,128]{3,2,1,0:T(8,128)(2,1)S(1)} %all_to_all.10.y_ref), custom_call_target="tpu_custom_call" | custom-call | tf_op jit(solution)/shard_map/unpack/pallas_call | solution.py:296
  (4 shorter events, 0.0 us)
Async XLA Ops:
  0.0 1.0 %copy-start = (f32[64,4,4,128]{3,2,1,0:T(4,128)S(1)}, f32[64,4,4,128]{3,2,1,0:T(4,128)}, u32[]{:S(2)}) copy-start(f32[64,4,4,128]{3,2,1,0:T(4,128)} %param.9) | copy-start | bytes 1572868
  1.0 0.7 %copy-start.2 = (f32[4,4,128]{2,1,0:T(4,128)S(1)}, f32[4,4,128]{2,1,0:T(4,128)}, u32[]{:S(2)}) copy-start(f32[4,4,128]{2,1,0:T(4,128)} %param.10) | copy-start | bytes 24580
  1.7 18.9 %copy-start.4 = (f32[4,4,128]{2,1,0:T(4,128)S(1)}, f32[4,4,128]{2,1,0:T(4,128)}, u32[]{:S(2)}) copy-start(f32[4,4,128]{2,1,0:T(4,128)} %param.11) | copy-start | bytes 24580
  1.9 29.9 %collective-permute-start.1 = (bf16[784,128]{1,0:T(8,128)(2,1)S(1)}, bf16[784,128]{1,0:T(8,128)(2,1)S(1)}, u32[]{:S(2)}, u32[]{:S(2)}) collective-permute-start(bf16[784,128]{1,0:T(8,128)(2,1)S(1)} %get-tuple-element.8), channel_id=1, source_target_pairs={{4,0},{8,4},{12,8},{16,12},{20,16},{24,20},{28,24},{32,28},{36,32}... | collective-permute-start | bytes 602120 | tf_op jit(solution)/shard_map/ppermute | solution.py:260
  18.7 13.1 %collective-permute-start = (bf16[768,128]{1,0:T(8,128)(2,1)S(1)}, bf16[768,128]{1,0:T(8,128)(2,1)S(1)}, u32[]{:S(2)}, u32[]{:S(2)}) collective-permute-start(bf16[768,128]{1,0:T(8,128)(2,1)S(1)} %get-tuple-element.7), channel_id=1, source_target_pairs={{0,4},{4,8},{8,12},{12,16},{16,20},{20,24},{24,28},{28,32},{32,36}... | collective-permute-start | bytes 589832 | tf_op jit(solution)/shard_map/ppermute | solution.py:259
  20.6 11.2 %copy-start.3 = (f32[4,4,128]{2,1,0:T(4,128)S(1)}, f32[4,4,128]{2,1,0:T(4,128)}, u32[]{:S(2)}) copy-start(f32[4,4,128]{2,1,0:T(4,128)} %param.10) | copy-start | bytes 24580
  20.6 11.2 %copy-start.5 = (s32[1,2]{1,0:T(1,128)S(1)}, s32[1,2]{1,0:T(1,128)}, u32[]{:S(2)}) copy-start(s32[1,2]{1,0:T(1,128)} %flag_ref.1) | copy-start | bytes 28
  31.8 8.1 %copy-start.8 = (f32[4,256]{1,0:T(4,128)S(1)}, f32[4,256]{1,0:T(4,128)}, u32[]{:S(2)}) copy-start(f32[4,256]{1,0:T(4,128)} %param.16) | copy-start | bytes 12292
  34.5 10.5 %copy-start.1 = (bf16[4,256,256]{2,1,0:T(8,128)(2,1)S(1)}, bf16[4,256,256]{2,1,0:T(8,128)(2,1)}, u32[]{:S(2)}) copy-start(bf16[4,256,256]{2,1,0:T(8,128)(2,1)} %param.15) | copy-start | bytes 1572868
  34.5 10.5 %all-to-all-start = ((bf16[4,4,64,128]{3,2,1,0:T(8,128)(2,1)}), bf16[4,4,64,128]{3,2,1,0:T(8,128)(2,1)S(1)}, u32[]{:S(2)}, u32[]{:S(2)}) async-start(bf16[4,4,64,128]{3,2,1,0:T(8,128)(2,1)} %flow.1), calls=%async_computation | async-start | bytes 524288 | tf_op jit(solution)/shard_map/all_to_all | solution.py:278
  39.9 0.8 %copy-start.6 = (s32[4,4,4,32]{3,2,1,0:T(4,128)S(1)}, s32[4,4,4,32]{3,2,1,0:T(4,128)}, u32[]{:S(2)}) copy-start(s32[4,4,4,32]{3,2,1,0:T(4,128)} %param.14) | copy-start | bytes 24580
  40.7 0.7 %copy-start.7 = (f32[3,4,32]{2,1,0:T(4,128)S(1)}, f32[3,4,32]{2,1,0:T(4,128)}, u32[]{:S(2)}) copy-start(f32[3,4,32]{2,1,0:T(4,128)} %param.17) | copy-start | bytes 4612
  41.4 0.7 %copy-start.9 = (s32[4,32]{1,0:T(4,128)S(1)}, s32[4,32]{1,0:T(4,128)}, u32[]{:S(2)}) copy-start(s32[4,32]{1,0:T(4,128)} %param.13) | copy-start | bytes 1540

commit v2 on v1

v2 whole, which is shorter than its diff:
```python
import functools

import jax
import jax.numpy as jnp
from jax import lax
from jax.experimental import pallas as pl
from jax.experimental.pallas import tpu as pltpu
from jax.sharding import PartitionSpec as P

F32 = jnp.float32
BF16 = jnp.bfloat16
LANES = 128
TABLE_ROWS = 32


def vmem():
    return pl.BlockSpec(memory_space=pltpu.VMEM)


def smem():
    return pl.BlockSpec(memory_space=pltpu.SMEM)


def hbm():
    return pl.BlockSpec(memory_space=pltpu.HBM)


def in_hbm(array):
    return pltpu.with_memory_space_constraint(array, pltpu.HBM)


def params(mib):
    return pltpu.CompilerParams(vmem_limit_bytes=mib << 20)


def face_weights(courant):
    speed = jnp.abs(courant)
    rest = 1.0 - speed
    mid = courant * rest * rest
    far = -courant * speed * rest
    centre = courant * speed * (3.0 - 2.0 * speed)
    positive = courant > 0.0
    far_low = jnp.where(positive, far, 0.0)
    far_high = far - far_low
    centre_low = jnp.where(positive, centre, 0.0)
    centre_high = centre - centre_low
    small, large = 1.0 / 12.0, 7.0 / 12.0
    return [
        -small * far_low,
        large * far_low - small * mid,
        large * (mid + far_low) - small * far_high + centre_low,
        large * (mid + far_high) - small * far_low + centre_high,
        large * far_high - small * mid,
        -small * far_high,
    ]


def cell_weights(before, after):
    zero = jnp.zeros_like(before[0])
    return [a - b for a, b in zip(before + [zero], [zero] + after)]


def block_transpose(rows, lane):
    low = lane < 64
    even = (lane & 32) == 0
    r0, r1, r2, r3 = rows
    b0 = jnp.where(low, r0, pltpu.roll(r2, 64, 1))
    b2 = jnp.where(low, pltpu.roll(r0, 64, 1), r2)
    b1 = jnp.where(low, r1, pltpu.roll(r3, 64, 1))
    b3 = jnp.where(low, pltpu.roll(r1, 64, 1), r3)
    return (
        jnp.where(even, b0, pltpu.roll(b1, 32, 1)),
        jnp.where(even, pltpu.roll(b0, 96, 1), b1),
        jnp.where(even, b2, pltpu.roll(b3, 32, 1)),
        jnp.where(even, pltpu.roll(b2, 96, 1), b3),
    )


def split3(values):
    high = values.astype(BF16).astype(F32)
    rest = values - high
    mid = rest.astype(BF16).astype(F32)
    return high, mid, rest - mid


def pack_kernel(levels, width, quarter, x_hbm, u_hbm, next_ref, prev_ref, x_ref, u_ref, sems):
    grid = levels * width
    pieces = sems.shape[0] - 1
    part = quarter // pieces
    copies = [pltpu.make_async_copy(u_hbm, u_ref, sems.at[pieces])]
    for i in range(pieces):
        rows = pl.ds(i * part * grid, part * grid)
        copies.append(pltpu.make_async_copy(x_hbm.at[rows], x_ref.at[rows], sems.at[i]))
    for copy in copies:
        copy.start()
    copies[0].wait()
    row = levels * 3 * quarter
    parts = split3(u_ref[pl.ds(0, levels, stride=width), :])
    parts = jnp.concatenate(parts + (jnp.zeros_like(parts[0]),), axis=0)
    prev_ref[row : row + 4 * levels, :] = parts.astype(BF16)
    for i in range(pieces):
        copies[1 + i].wait()
        for level in range(levels):
            for col in range(width):
                start = i * part * grid + level * width + col
                values = x_ref[pl.ds(start, part, stride=grid), :].astype(BF16)
                if col >= width - 3:
                    row = (level * 3 + col - (width - 3)) * quarter + i * part
                    next_ref[row : row + part, :] = values
                if col < 3:
                    row = (level * 3 + col) * quarter + i * part
                    prev_ref[row : row + part, :] = values


def local_kernel(
    levels,
    width,
    quarter,
    flag_ref,
    x_ref,
    cycle_ref,
    edge_ref,
    entry_ref,
    sun_ref,
    mix_ref,
    base_ref,
    weight_ref,
    table_ref,
    turn_ref,
    own_ref,
    tab_ref,
):
    grid = levels * width
    chunk = 32
    row = lax.broadcasted_iota(jnp.int32, (LANES, LANES), 0)
    col = lax.broadcasted_iota(jnp.int32, (LANES, LANES), 1)
    for side in range(2):
        source = jnp.where(flag_ref[0, side] > 0, LANES - 1 - col, col)
        turn_ref[side] = jnp.where(row == source, 1.0, 0.0).astype(BF16)
    entries = entry_ref.shape[0]
    tab_ref[...] = jnp.zeros_like(tab_ref)
    tab_ref[0:entries, :] = entry_ref[...].astype(F32)
    tab_ref[entries : entries + 1, :] = sun_ref[...].astype(F32)
    for i, part in enumerate(split3(mix_ref[...])):
        row = entries + 1 + i * (levels - 1)
        tab_ref[row : row + levels - 1, :] = part
    table_ref[...] = tab_ref[...].astype(BF16)
    shape = (grid, LANES)
    lane = lax.broadcasted_iota(jnp.int32, shape, 1)
    column = lax.broadcasted_iota(jnp.int32, shape, 0) % width
    faces = face_weights(cycle_ref[...])
    after = [jnp.where(column == width - 1, 0.0, pltpu.roll(w, grid - 1, 0)) for w in faces]
    across = cell_weights(faces, after)
    for k in range(7):
        weight_ref[k] = across[k]
    faces = face_weights(jnp.where(lane == 0, 0.0, edge_ref[...]))
    along = cell_weights(faces, [pltpu.roll(w, LANES - 1, 1) for w in faces])
    low3, low2, low1, here, high1, high2, high3 = along
    here = jnp.where(lane == 0, here + low1 + low2 + low3, here)
    low1 = jnp.where(lane == 1, low1 + low2 + low3, low1)
    low2 = jnp.where(lane == 2, low2 + low3, low2)
    here = jnp.where(lane == LANES - 1, here + high1 + high2 + high3, here)
    high1 = jnp.where(lane == LANES - 2, high1 + high2 + high3, high1)
    high2 = jnp.where(lane == LANES - 3, high2 + high3, high2)
    own_ref[0] = jnp.where(lane < 3, 0.0, low3)
    own_ref[1] = jnp.where(lane < 2, 0.0, low2)
    own_ref[2] = jnp.where(lane < 1, 0.0, low1)
    own_ref[3] = 1.0 + here + across[3]
    own_ref[4] = jnp.where(lane > LANES - 2, 0.0, high1)
    own_ref[5] = jnp.where(lane > LANES - 3, 0.0, high2)
    own_ref[6] = jnp.where(lane > LANES - 4, 0.0, high3)
    for level in range(levels):
        for start in range(0, quarter, chunk):
            cells = [
                x_ref[pl.ds(start * grid + level * width + col, chunk, stride=grid), :]
                for col in range(width)
            ]
            for col in range(width):
                cell = level * width + col
                total = cells[col] * own_ref[3, cell : cell + 1, :]
                for k in (-3, -2, -1, 1, 2, 3):
                    moved = pltpu.roll(cells[col], (-k) % LANES, 1)
                    total = total + moved * own_ref[3 + k, cell : cell + 1, :]
                    if 0 <= col + k < width:
                        total = total + cells[col + k] * weight_ref[3 + k, cell : cell + 1, :]
                base_ref[cell, start : start + chunk, :] = total


def maps_kernel(rank_ref, map_ref, off_ref, full_ref, last_ref, shift_ref, scratch_ref):
    rank = rank_ref[0, 0]
    count, quarter, species = full_ref.shape
    parts = species // quarter
    entries = count // parts
    row = lax.broadcasted_iota(jnp.int32, (species, species), 0)
    col = lax.broadcasted_iota(jnp.int32, (species, species), 1)
    shuffle = jnp.where(row == (col ^ (rank * quarter)), 1.0, 0.0).astype(BF16)
    for e in range(entries):
        moved = jnp.dot(map_ref[e], shuffle, preferred_element_type=F32).astype(BF16)
        for k in range(parts):
            scratch_ref[e * parts + k] = moved[k * quarter : (k + 1) * quarter, :]
    for e in range(entries):
        for k in range(parts):
            block = scratch_ref[e * parts + (rank ^ k)]
            full_ref[e * parts + k] = block
            if k == 0:
                last_ref[e] = block
    for k in range(parts):
        shift_ref[k] = off_ref[rank ^ k]


def flow_kernel(
    levels,
    first,
    some,
    width,
    quarter,
    x_ref,
    base_ref,
    weight_ref,
    table_ref,
    turn_ref,
    before_ref,
    after_ref,
    out_ref,
):
    grid = levels * width
    turn_before, turn_after = turn_ref[0], turn_ref[1]
    halo = levels * 3 * quarter
    split = jnp.dot(
        after_ref[halo : halo + 4 * levels, :], turn_after, preferred_element_type=F32
    )
    closing = split[0:levels] + split[levels : 2 * levels] + split[2 * levels : 3 * levels]
    closing = face_weights(closing)
    chunk = 32
    for level in range(first, first + some):
        for start in range(0, quarter, chunk):
            low, high = [], []
            for i in range(3):
                begin = (level * 3 + i) * quarter + start
                low.append(before_ref[begin : begin + chunk, :])
                high.append(after_ref[begin : begin + chunk, :])
            low = jnp.dot(
                jnp.concatenate(low, axis=0), turn_before, preferred_element_type=F32
            )
            high = jnp.dot(
                jnp.concatenate(high, axis=0), turn_after, preferred_element_type=F32
            )
            outer = {i - 3: low[i * chunk : (i + 1) * chunk] for i in range(3)}
            outer.update({width + i: high[i * chunk : (i + 1) * chunk] for i in range(3)})
            for c in range(width):
                cell = level * width + c
                total = base_ref[cell, start : start + chunk, :]
                for k in range(-3, 4):
                    if c + k in outer and not (c == width - 1 and k == 3):
                        total = total + outer[c + k] * weight_ref[3 + k, cell : cell + 1, :]
                if c == width - 1:
                    for k in range(-3, 3):
                        if width + k in outer:
                            value = outer[width + k]
                        else:
                            begin = start * grid + level * width + width + k
                            value = x_ref[pl.ds(begin, chunk, stride=grid), :]
                        total = total - value * closing[3 + k][level : level + 1, :]
                begin = ((level - first) * width + c) * quarter + start
                out_ref[begin : begin + chunk, :] = total.astype(BF16)
    if first == 0:
        begin = some * width * quarter
        out_ref[begin : begin + TABLE_ROWS, :] = table_ref[...]


def tables_of(rank, tails):
    lane = lax.broadcasted_iota(jnp.int32, (TABLE_ROWS, LANES), 1)
    t0, t1, t2, t3 = [t.astype(F32) for t in tails]
    odd = (rank & 1) > 0
    t0, t1 = jnp.where(odd, t1, t0), jnp.where(odd, t0, t1)
    t2, t3 = jnp.where(odd, t3, t2), jnp.where(odd, t2, t3)
    upper = (rank & 2) > 0
    t0, t2 = jnp.where(upper, t2, t0), jnp.where(upper, t0, t2)
    t1, t3 = jnp.where(upper, t3, t1), jnp.where(upper, t1, t3)
    return block_transpose((t0, t1, t2, t3), lane)


def chem_kernel(
    levels, first, some, width, quarter, entries, substeps, last_call, rank_ref, *refs
):
    parts = 4
    species = parts * quarter
    block_refs = refs[0:parts]
    tail_refs = refs[parts : 2 * parts]
    map_ref, last_ref, off_ref = refs[2 * parts : 2 * parts + 3]
    tail = refs[2 * parts + 3 :]
    columns = tables_of(rank_ref[0, 0], [r[...] for r in tail_refs])
    groups = some * width
    tiles = groups // 2

    def row_of(group, index):
        return columns[group % width][index : index + 1, :]

    def pair_of(tile, function):
        return jnp.concatenate([function(2 * tile), function(2 * tile + 1)], axis=1)

    def block(part, group):
        return block_refs[part][group * quarter : (group + 1) * quarter, :]

    start = [
        pair_of(
            tile, lambda g: jnp.concatenate([block(p, g) for p in range(parts)], axis=0)
        )
        for tile in range(tiles)
    ]
    state = list(start)
    result = [None] * tiles
    for step in range(substeps):
        final = step == substeps - 1
        rows = quarter if final else species
        matrix = last_ref[...] if final else map_ref[...]
        for tile in range(tiles):
            product = jnp.dot(matrix, state[tile], preferred_element_type=F32)
            entry = pair_of(
                tile, lambda g: row_of(g, step * levels + first + g // width)
            )
            chosen = product[0:rows] + off_ref[0:rows, 0:1]
            for e in range(1, entries):
                chosen = jnp.where(
                    entry == float(e),
                    product[e * rows : (e + 1) * rows] + off_ref[0:rows, e : e + 1],
                    chosen,
                )
            result[tile] = jnp.maximum(chosen, 0.0)
            if not final:
                state[tile] = result[tile].astype(BF16)
    sun = substeps * levels
    chem_ref = tail[-1]
    for tile in range(tiles):
        lit = pair_of(tile, lambda g: row_of(g, sun)) > 0.0
        chem = jnp.where(lit, result[tile], start[tile][0:quarter].astype(F32))
        chem_ref[2 * tile] = chem[:, 0:LANES]
        chem_ref[2 * tile + 1] = chem[:, LANES : 2 * LANES]
    if not last_call:
        return
    earlier_refs = tail[:-2]
    out_ref = tail[-2]
    grid = levels * width
    chunk = 32
    for col in range(width):
        pieces = [
            columns[col][sun + 1 + i * (levels - 1) : sun + 1 + (i + 1) * (levels - 1), :]
            for i in range(3)
        ]
        mixed = pieces[0] + pieces[1] + pieces[2]
        mixing = [mixed[k : k + 1, :] for k in range(levels - 1)]
        inverse, ratio = [], []
        for level in range(levels):
            diagonal = 1.0
            if level > 0:
                diagonal = diagonal + mixing[level - 1]
            if level < levels - 1:
                diagonal = diagonal + mixing[level]
            if level > 0:
                diagonal = diagonal - mixing[level - 1] * ratio[level - 1]
            inverse.append(1.0 / diagonal)
            if level < levels - 1:
                ratio.append(mixing[level] * inverse[level])
        for begin in range(0, quarter, chunk):
            solved = []
            for level in range(levels):
                source = chem_ref if level >= first else earlier_refs[level // some]
                value = source[(level % some) * width + col, begin : begin + chunk, :]
                if level > 0:
                    value = value + mixing[level - 1] * solved[-1]
                solved.append(value * inverse[level])
            for level in range(levels - 2, -1, -1):
                solved[level] = solved[level] + ratio[level] * solved[level + 1]
            for level in range(levels):
                place = begin * grid + level * width + col
                out_ref[pl.ds(place, chunk, stride=grid), :] = solved[level]


CALLS = 1


def shards(
    tracers,
    courant_cycle,
    courant_edge,
    seam_flags,
    sunlit,
    table_entry,
    linear_maps,
    offsets,
    mixing,
):
    quarter, levels, width, length = tracers.shape
    grid = levels * width
    substeps = table_entry.shape[0]
    entries, species, _ = linear_maps.shape
    count = lax.axis_size("tile")
    parts = lax.axis_size("trc")
    forward = [(i, (i + 1) % count) for i in range(count)]
    backward = [(target, source) for source, target in forward]
    x = tracers.reshape(quarter * grid, length)
    cycle = courant_cycle.reshape(grid, length)
    halo = levels * 3 * quarter
    pieces = 4
    shape = jax.ShapeDtypeStruct
    to_next, to_prev = pl.pallas_call(
        functools.partial(pack_kernel, levels, width, quarter),
        out_shape=(
            shape((halo, length), BF16),
            shape((halo + 4 * levels, length), BF16),
        ),
        in_specs=[hbm()] * 2,
        out_specs=(vmem(), vmem()),
        scratch_shapes=[
            pltpu.VMEM((quarter * grid, length), F32),
            pltpu.VMEM((grid, length), F32),
            pltpu.SemaphoreType.DMA((pieces + 1,)),
        ],
        compiler_params=params(8),
        name="pack",
    )(in_hbm(x), in_hbm(cycle))
    before = lax.ppermute(to_next, "tile", forward)
    after = lax.ppermute(to_prev, "tile", backward)
    rank = lax.axis_index("trc").astype(jnp.int32).reshape(1, 1)
    base, weights, table, turns = pl.pallas_call(
        functools.partial(local_kernel, levels, width, quarter),
        out_shape=(
            shape((grid, quarter, length), F32),
            shape((7, grid, length), F32),
            shape((TABLE_ROWS, length), BF16),
            shape((2, length, length), BF16),
        ),
        in_specs=[smem()] + [vmem()] * 6,
        out_specs=(vmem(),) * 4,
        scratch_shapes=[
            pltpu.VMEM((7, grid, length), F32),
            pltpu.VMEM((TABLE_ROWS, length), F32),
        ],
        compiler_params=params(8),
        cost_estimate=pl.CostEstimate(flops=4000000, bytes_accessed=1 << 20, transcendentals=0),
        name="local",
    )(
        seam_flags,
        x,
        cycle,
        courant_edge.reshape(grid, length),
        table_entry.reshape(substeps * levels, length),
        sunlit.reshape(1, length),
        mixing.reshape(levels - 1, length),
    )
    full, last, shift = pl.pallas_call(
        maps_kernel,
        out_shape=(
            shape((entries * parts, quarter, species), BF16),
            shape((entries, quarter, species), BF16),
            shape((parts, quarter, entries), F32),
        ),
        in_specs=[smem()] + [vmem()] * 2,
        out_specs=(vmem(),) * 3,
        scratch_shapes=[pltpu.VMEM((entries * parts, quarter, species), BF16)],
        compiler_params=params(8),
        cost_estimate=pl.CostEstimate(flops=4000000, bytes_accessed=1 << 20, transcendentals=0),
        name="maps",
    )(rank, linear_maps, offsets.T.reshape(parts, quarter, entries))
    before, after, base, full, last, shift = lax.optimization_barrier(
        (before, after, base, full, last, shift)
    )
    some = levels // CALLS
    chunks = []
    for call in range(CALLS):
        rows = some * width * quarter + (TABLE_ROWS if call == 0 else 0)
        own = pl.pallas_call(
            functools.partial(flow_kernel, levels, call * some, some, width, quarter),
            out_shape=shape((rows, length), BF16),
            in_specs=[vmem()] * 7,
            out_specs=vmem(),
            compiler_params=params(8),
        )(x, base, weights, table, turns, before, after)
        chunks.append([own])
    swap = {k: [(i, i ^ k) for i in range(parts)] for k in (1, 2)}
    for chunk in chunks:
        chunk.append(lax.ppermute(chunk[0], "trc", swap[1]))
        chunk.append(lax.ppermute(chunk[0], "trc", swap[2]))
        chunk.append(lax.ppermute(chunk[2], "trc", swap[1]))
    tails = [c[some * width * quarter :] for c in chunks[0]]
    results = []
    for call, chunk in enumerate(chunks):
        last_call = call == CALLS - 1
        chem_shape = (some * width, quarter, length)
        if last_call:
            out_shape = shape((quarter * grid, length), F32)
            scratch = [pltpu.VMEM(chem_shape, F32)]
        else:
            out_shape = shape(chem_shape, F32)
            scratch = []
        results.append(
            pl.pallas_call(
                functools.partial(
                    chem_kernel,
                    levels,
                    call * some,
                    some,
                    width,
                    quarter,
                    entries,
                    substeps,
                    last_call,
                ),
                out_shape=out_shape,
                in_specs=[smem()] + [vmem()] * (11 + (len(results) if last_call else 0)),
                out_specs=vmem(),
                scratch_shapes=scratch,
                compiler_params=params(24),
            )(
                rank,
                *chunk,
                *tails,
                full.reshape(entries * species, species),
                last.reshape(entries * quarter, species),
                shift.reshape(species, entries),
                *(results if last_call else []),
            )
        )
    return results[-1].reshape(quarter, levels, width, length)


def solution(mesh):
    placed = (
        P("trc", None, "tile", None),
        P(None, "tile", None),
        P(None, "tile", None),
        P("tile", None),
        P("tile", "trc"),
        P(None, None, "tile", "trc"),
        P(),
        P(),
        P(None, "tile", "trc"),
    )
    return jax.shard_map(
        shards, mesh=mesh, in_specs=placed, out_specs=P("trc", None, "tile", None), check_vma=False
    )
```

time: 56.9 us -> 51.3 us (0.902)
  blocking collectives: 8.33 us -> 0 us
  Pallas kernels: 14.9 us -> 8.84 us
  starting transfers between devices: 24.1 us -> 29.9 us
  waiting for transfers between devices: 5.11 us -> 10.3 us
  local copies, waits for them, and re-layouts: 3.97 us -> 1.75 us
    ppermute x0 -> x3, starting transfers between devices: none -> 11.1 us  [the longest x1 4.67 us: shards(): chunk.append(lax.ppermute(chunk[2], 'trc', swap[1]))]
    all_to_all x1 -> x0, blocking collectives: 8.33 us -> none  [shards(): back = lax.all_to_all(mixed, 'trc', split_axis=0, concat_axis=0, tiled=True)]
    pallas_call x4, Pallas kernels: 14.7 us -> 7.58 us  [the longest x1 5.39 us: shards(): pl.pallas_call(functools.partial(chem_kernel, levels, call * some, some,...]
    all_to_all x1 -> x0, starting transfers between devices: 5.41 us -> none  [shards(): lax.all_to_all(moved, 'trc', split_axis=0, concat_axis=0, tiled=True)]
    ppermute x1, waiting for transfers between devices: 2.28 us -> 7.6 us  [shards(): before = lax.ppermute(to_next, 'tile', forward)]
    unnamed x21 -> x16, local copies, waits for them, and re-layouts: 3.72 us -> 0.67 us
    all_to_all x1 -> x0, waiting for transfers between devices: 2.82 us -> none  [shards(): lax.all_to_all(moved, 'trc', split_axis=0, concat_axis=0, tiled=True)]
    ppermute x0 -> x3, waiting for transfers between devices: none -> 2.71 us  [the longest x1 1.6 us: shards(): chunk.append(lax.ppermute(chunk[0], 'trc', swap[2]))]
  transfers between devices with their start and end apart: 3 -> 5, of which waited for: 2 -> 3; matrix products, arithmetic and copies ran while one was open for 1% -> 2% of each run, Pallas kernels for 16% -> 4%
where the time goes in v2:
time: 51.3 us; the launch traced here: 51 us
  starting transfers between devices  29.9 us (58%)
  waiting for transfers between devices  10.3 us (20%)
  Pallas kernels  8.84 us (17%)
  local copies, waits for them, and re-layouts  1.75 us (3%)
    ppermute x1, starting transfers between devices, shards(): after = lax.ppermute(to_prev, 'tile', backward)  16.9 us
    ppermute x1, waiting for transfers between devices, shards(): before = lax.ppermute(to_next, 'tile', forward)  7.6 us
    pallas_call x1, Pallas kernels, shards(): pl.pallas_call(functools.partial(chem_kernel, levels, call * some, some,...  5.39 us
    ppermute x1, starting transfers between devices, shards(): chunk.append(lax.ppermute(chunk[2], 'trc', swap[1]))  4.67 us
    ppermute x1, starting transfers between devices, shards(): chunk.append(lax.ppermute(chunk[0], 'trc', swap[1]))  4.1 us
    ppermute x1, starting transfers between devices, shards(): chunk.append(lax.ppermute(chunk[0], 'trc', swap[2]))  2.31 us
    ppermute x1, starting transfers between devices, shards(): before = lax.ppermute(to_next, 'tile', forward)  1.92 us
    ppermute x1, waiting for transfers between devices, shards(): chunk.append(lax.ppermute(chunk[0], 'trc', swap[2]))  1.6 us
  transfers between devices with their start and end apart: 5, of which 3 were waited for; matrix products, arithmetic and copies ran while one was open for 2% of the time, Pallas kernels for 4%

profile of v2, /device:TPU:1, one launch (start us, length us, event | category | flops | bytes accessed | tf_op | source)
XLA Modules:
  0.0 51.0 jit_solution(12856371173668090684)
XLA Ops:
  0.0 0.0 copy-start.7
  0.0 1.3 %pack.1 = (bf16[768,128]{1,0:T(8,128)(2,1)S(1)}, bf16[784,128]{1,0:T(8,128)(2,1)S(1)}) custom-call(f32[1024,128]{1,0:T(8,128)} %bitcast.10, f32[16,128]{1,0:T(8,128)} %bitcast.17), custom_call_target="tpu_custom_call" | custom-call | tf_op jit(solution)/shard_map/pack/pallas_call | solution.py:406
  1.3 0.0 copy-start
  1.3 16.9 %collective-permute-start.1 = (bf16[784,128]{1,0:T(8,128)(2,1)S(1)}, bf16[784,128]{1,0:T(8,128)(2,1)S(1)}, u32[]{:S(2)}, u32[]{:S(2)}) collective-permute-start(bf16[784,128]{1,0:T(8,128)(2,1)S(1)} %get-tuple-element.21), channel_id=1, source_target_pairs={{4,0},{8,4},{12,8},{16,12},{20,16},{24,20},{28,24},{32,28},{36,32}... | collective-permute-start | bytes 602120 | tf_op jit(solution)/shard_map/ppermute | solution.py:423
  18.2 1.9 %collective-permute-start = (bf16[768,128]{1,0:T(8,128)(2,1)S(1)}, bf16[768,128]{1,0:T(8,128)(2,1)S(1)}, u32[]{:S(2)}, u32[]{:S(2)}) collective-permute-start(bf16[768,128]{1,0:T(8,128)(2,1)S(1)} %get-tuple-element.20), channel_id=1, source_target_pairs={{0,4},{4,8},{8,12},{12,16},{16,20},{20,24},{24,28},{28,32},{32,36}... | collective-permute-start | bytes 589832 | tf_op jit(solution)/shard_map/ppermute | solution.py:422
  20.1 0.8 %reshape.41.sun_ref = s32[1,128]{1,0:T(1,128)S(1)} reshape(s32[4,32]{1,0:T(4,128)} %param.13) | data formatting | bytes 1024 | tf_op jit(solution)/shard_map/reshape | solution.py:448
  20.9 0.0 copy-done.6
  20.9 0.1 reshape.42.mix_ref
  21.0 0.0 copy-done.5
  21.0 0.1 reshape.40.entry_ref
  21.1 0.0 copy-done.7
  21.1 0.1 copy.10
  21.2 0.0 copy-done.1
  21.2 0.0 copy-start.2
  21.2 0.0 copy-start.3
  21.3 0.4 maps.1
  21.6 0.0 copy-start.4
  21.6 0.0 copy-done
  21.6 0.3 copy-done.2
  21.9 0.0 copy-done.3
  21.9 0.3 copy-done.4
  22.3 1.4 %local.1 = (f32[16,64,128]{2,1,0:T(8,128)S(1)}, f32[7,16,128]{2,1,0:T(8,128)S(1)}, bf16[32,128]{1,0:T(8,128)(2,1)S(1)}, bf16[2,128,128]{2,1,0:T(8,128)(2,1)S(1)}) custom-call(s32[1,2]{1,0:T(1,128)S(1)} %copy-done.4, f32[1024,128]{1,0:T(8,128)S(1)} %bitcast.11, f32[16,128]{1,0:T(8,128)S(1)} %bitcast.18, f32[16,128]{1,0:T(8,128)S(1)} %bitcast.19, ...), custom_call_target="tpu_custom_call" | custom-call | flops 4000000 | bytes 1048576 | tf_op jit(solution)/shard_map/local/pallas_call | solution.py:425
  23.7 7.6 %collective-permute-done.before_ref = bf16[768,128]{1,0:T(8,128)(2,1)S(1)} collective-permute-done((bf16[768,128]{1,0:T(8,128)(2,1)S(1)}, bf16[768,128]{1,0:T(8,128)(2,1)S(1)}, u32[]{:S(2)}, u32[]{:S(2)}) %collective-permute-start) | collective-permute-done | bytes 196640 | tf_op jit(solution)/shard_map/ppermute | solution.py:422
  31.3 0.0 collective-permute-done.1.after_ref
  31.3 0.4 shard_map.91.refs_0_
  31.7 2.3 %collective-permute-start.3 = (bf16[1056,128]{1,0:T(8,128)(2,1)S(1)}, bf16[1056,128]{1,0:T(8,128)(2,1)S(1)}, u32[]{:S(2)}, u32[]{:S(2)}) collective-permute-start(bf16[1056,128]{1,0:T(8,128)(2,1)S(1)} %shard_map.91.refs_0_), channel_id=1, source_target_pairs={{0,2},{1,3},{2,0},{3,1},{4,6},{5,7},{6,4},{7,5},{8,10},{9,11},{10,... | collective-permute-start | bytes 811016 | tf_op jit(solution)/shard_map/ppermute | solution.py:483
  34.1 4.1 %collective-permute-start.2 = (bf16[1056,128]{1,0:T(8,128)(2,1)S(1)}, bf16[1056,128]{1,0:T(8,128)(2,1)S(1)}, u32[]{:S(2)}, u32[]{:S(2)}) collective-permute-start(bf16[1056,128]{1,0:T(8,128)(2,1)S(1)} %shard_map.91.refs_0_), channel_id=1, source_target_pairs={{0,1},{1,0},{2,3},{3,2},{4,5},{5,4},{6,7},{7,6},{8,9},{9,8},{10,11... | collective-permute-start | bytes 811016 | tf_op jit(solution)/shard_map/ppermute | solution.py:482
  38.2 1.6 %collective-permute-done.3.refs_2_ = bf16[1056,128]{1,0:T(8,128)(2,1)S(1)} collective-permute-done((bf16[1056,128]{1,0:T(8,128)(2,1)S(1)}, bf16[1056,128]{1,0:T(8,128)(2,1)S(1)}, u32[]{:S(2)}, u32[]{:S(2)}) %collective-permute-start.3) | collective-permute-done | bytes 270368 | tf_op jit(solution)/shard_map/ppermute | solution.py:483
  39.8 4.7 %collective-permute-start.4 = (bf16[1056,128]{1,0:T(8,128)(2,1)S(1)}, bf16[1056,128]{1,0:T(8,128)(2,1)S(1)}, u32[]{:S(2)}, u32[]{:S(2)}) collective-permute-start(bf16[1056,128]{1,0:T(8,128)(2,1)S(1)} %collective-permute-done.3.refs_2_), channel_id=1, source_target_pairs={{0,1},{1,0},{2,3},{3,2},{4,5},{5,4},{6,7},{7,6},{8,9},{9,8},{10,11... | collective-permute-start | bytes 811016 | tf_op jit(solution)/shard_map/ppermute | solution.py:484
  44.5 0.0 collective-permute-done.2.refs_1_
  44.5 1.1 %collective-permute-done.4.refs_3_ = bf16[1056,128]{1,0:T(8,128)(2,1)S(1)} collective-permute-done((bf16[1056,128]{1,0:T(8,128)(2,1)S(1)}, bf16[1056,128]{1,0:T(8,128)(2,1)S(1)}, u32[]{:S(2)}, u32[]{:S(2)}) %collective-permute-start.4) | collective-permute-done | bytes 270368 | tf_op jit(solution)/shard_map/ppermute | solution.py:484
  45.6 5.4 %shard_map.92 = f32[1024,128]{1,0:T(8,128)} custom-call(s32[1,1]{1,0:T(1,128)} %bitcast.rank_ref, bf16[1056,128]{1,0:T(8,128)(2,1)S(1)} %shard_map.91.refs_0_, bf16[1056,128]{1,0:T(8,128)(2,1)S(1)} %collective-permute-done.2.refs_1_, bf16[1056,128]{1,0:T(8,128)(2,1)S(1)} %collective-permute-done.3.refs_2_, ...), custom_call_target="tpu_custom_call" | custom-call | tf_op jit(solution)/shard_map/pallas_call | solution.py:497
  (7 shorter events, 0.0 us)
Async XLA Ops:
  0.0 20.9 %copy-start.6 = (f32[3,4,32]{2,1,0:T(4,128)S(1)}, f32[3,4,32]{2,1,0:T(4,128)}, u32[]{:S(2)}) copy-start(f32[3,4,32]{2,1,0:T(4,128)} %param.17) | copy-start | bytes 4612
  0.0 21.0 %copy-start.5 = (s32[4,4,4,32]{3,2,1,0:T(4,128)S(1)}, s32[4,4,4,32]{3,2,1,0:T(4,128)}, u32[]{:S(2)}) copy-start(s32[4,4,4,32]{3,2,1,0:T(4,128)} %param.14) | copy-start | bytes 24580
  0.0 21.2 %copy-start.1 = (bf16[4,256,256]{2,1,0:T(8,128)(2,1)S(1)}, bf16[4,256,256]{2,1,0:T(8,128)(2,1)}, u32[]{:S(2)}) copy-start(bf16[4,256,256]{2,1,0:T(8,128)(2,1)} %map_ref.1) | copy-start | bytes 1572868
  0.0 21.1 %copy-start.7 = (f32[4,256]{1,0:T(4,128)S(1)}, f32[4,256]{1,0:T(4,128)}, u32[]{:S(2)}) copy-start(f32[4,256]{1,0:T(4,128)} %param.16) | copy-start | bytes 12292
  1.3 20.3 %copy-start = (f32[64,4,4,128]{3,2,1,0:T(4,128)S(1)}, f32[64,4,4,128]{3,2,1,0:T(4,128)}, u32[]{:S(2)}) copy-start(f32[64,4,4,128]{3,2,1,0:T(4,128)} %param.9) | copy-start | bytes 1572868
  1.3 30.0 %collective-permute-start.1 = (bf16[784,128]{1,0:T(8,128)(2,1)S(1)}, bf16[784,128]{1,0:T(8,128)(2,1)S(1)}, u32[]{:S(2)}, u32[]{:S(2)}) collective-permute-start(bf16[784,128]{1,0:T(8,128)(2,1)S(1)} %get-tuple-element.21), channel_id=1, source_target_pairs={{4,0},{8,4},{12,8},{16,12},{20,16},{24,20},{28,24},{32,28},{36,32}... | collective-permute-start | bytes 602120 | tf_op jit(solution)/shard_map/ppermute | solution.py:423
  18.2 13.1 %collective-permute-start = (bf16[768,128]{1,0:T(8,128)(2,1)S(1)}, bf16[768,128]{1,0:T(8,128)(2,1)S(1)}, u32[]{:S(2)}, u32[]{:S(2)}) collective-permute-start(bf16[768,128]{1,0:T(8,128)(2,1)S(1)} %get-tuple-element.20), channel_id=1, source_target_pairs={{0,4},{4,8},{8,12},{12,16},{16,20},{20,24},{24,28},{28,32},{32,36}... | collective-permute-start | bytes 589832 | tf_op jit(solution)/shard_map/ppermute | solution.py:422
  21.2 0.7 %copy-start.2 = (f32[4,4,128]{2,1,0:T(4,128)S(1)}, f32[4,4,128]{2,1,0:T(4,128)}, u32[]{:S(2)}) copy-start(f32[4,4,128]{2,1,0:T(4,128)} %param.10) | copy-start | bytes 24580
  21.2 0.7 %copy-start.3 = (f32[4,4,128]{2,1,0:T(4,128)S(1)}, f32[4,4,128]{2,1,0:T(4,128)}, u32[]{:S(2)}) copy-start(f32[4,4,128]{2,1,0:T(4,128)} %param.11) | copy-start | bytes 24580
  21.6 0.7 %copy-start.4 = (s32[1,2]{1,0:T(1,128)S(1)}, s32[1,2]{1,0:T(1,128)}, u32[]{:S(2)}) copy-start(s32[1,2]{1,0:T(1,128)} %flag_ref.1) | copy-start | bytes 28
  31.7 8.0 %collective-permute-start.3 = (bf16[1056,128]{1,0:T(8,128)(2,1)S(1)}, bf16[1056,128]{1,0:T(8,128)(2,1)S(1)}, u32[]{:S(2)}, u32[]{:S(2)}) collective-permute-start(bf16[1056,128]{1,0:T(8,128)(2,1)S(1)} %shard_map.91.refs_0_), channel_id=1, source_target_pairs={{0,2},{1,3},{2,0},{3,1},{4,6},{5,7},{6,4},{7,5},{8,10},{9,11},{10,... | collective-permute-start | bytes 811016 | tf_op jit(solution)/shard_map/ppermute | solution.py:483
  34.1 10.4 %collective-permute-start.2 = (bf16[1056,128]{1,0:T(8,128)(2,1)S(1)}, bf16[1056,128]{1,0:T(8,128)(2,1)S(1)}, u32[]{:S(2)}, u32[]{:S(2)}) collective-permute-start(bf16[1056,128]{1,0:T(8,128)(2,1)S(1)} %shard_map.91.refs_0_), channel_id=1, source_target_pairs={{0,1},{1,0},{2,3},{3,2},{4,5},{5,4},{6,7},{7,6},{8,9},{9,8},{10,11... | collective-permute-start | bytes 811016 | tf_op jit(solution)/shard_map/ppermute | solution.py:482
  39.8 5.8 %collective-permute-start.4 = (bf16[1056,128]{1,0:T(8,128)(2,1)S(1)}, bf16[1056,128]{1,0:T(8,128)(2,1)S(1)}, u32[]{:S(2)}, u32[]{:S(2)}) collective-permute-start(bf16[1056,128]{1,0:T(8,128)(2,1)S(1)} %collective-permute-done.3.refs_2_), channel_id=1, source_target_pairs={{0,1},{1,0},{2,3},{3,2},{4,5},{5,4},{6,7},{7,6},{8,9},{9,8},{10,11... | collective-permute-start | bytes 811016 | tf_op jit(solution)/shard_map/ppermute | solution.py:484

commit v3 on v2

v3 whole, which is shorter than its diff:
```python
import functools

import jax
import jax.numpy as jnp
from jax import lax
from jax.experimental import pallas as pl
from jax.experimental.pallas import tpu as pltpu
from jax.sharding import PartitionSpec as P

F32 = jnp.float32
BF16 = jnp.bfloat16
LANES = 128
TABLE_ROWS = 32


def vmem():
    return pl.BlockSpec(memory_space=pltpu.VMEM)


def smem():
    return pl.BlockSpec(memory_space=pltpu.SMEM)


def hbm():
    return pl.BlockSpec(memory_space=pltpu.HBM)


def in_hbm(array):
    return pltpu.with_memory_space_constraint(array, pltpu.HBM)


def params(mib):
    return pltpu.CompilerParams(vmem_limit_bytes=mib << 20)


def face_weights(courant):
    speed = jnp.abs(courant)
    rest = 1.0 - speed
    mid = courant * rest * rest
    far = -courant * speed * rest
    centre = courant * speed * (3.0 - 2.0 * speed)
    positive = courant > 0.0
    far_low = jnp.where(positive, far, 0.0)
    far_high = far - far_low
    centre_low = jnp.where(positive, centre, 0.0)
    centre_high = centre - centre_low
    small, large = 1.0 / 12.0, 7.0 / 12.0
    return [
        -small * far_low,
        large * far_low - small * mid,
        large * (mid + far_low) - small * far_high + centre_low,
        large * (mid + far_high) - small * far_low + centre_high,
        large * far_high - small * mid,
        -small * far_high,
    ]


def cell_weights(before, after):
    zero = jnp.zeros_like(before[0])
    return [a - b for a, b in zip(before + [zero], [zero] + after)]


def block_transpose(rows, lane):
    low = lane < 64
    even = (lane & 32) == 0
    r0, r1, r2, r3 = rows
    b0 = jnp.where(low, r0, pltpu.roll(r2, 64, 1))
    b2 = jnp.where(low, pltpu.roll(r0, 64, 1), r2)
    b1 = jnp.where(low, r1, pltpu.roll(r3, 64, 1))
    b3 = jnp.where(low, pltpu.roll(r1, 64, 1), r3)
    return (
        jnp.where(even, b0, pltpu.roll(b1, 32, 1)),
        jnp.where(even, pltpu.roll(b0, 96, 1), b1),
        jnp.where(even, b2, pltpu.roll(b3, 32, 1)),
        jnp.where(even, pltpu.roll(b2, 96, 1), b3),
    )


def split3(values):
    high = values.astype(BF16).astype(F32)
    rest = values - high
    mid = rest.astype(BF16).astype(F32)
    return high, mid, rest - mid


def pack_kernel(levels, width, quarter, pieces, *refs):
    even = (refs[0][0, 0] & 1) == 0
    refs = refs[1:]
    count = (len(refs) - 3) // 2
    sources, (a_ref, b_ref), targets = refs[:count], refs[count : count + 2], refs[count + 2 : -1]
    sems = refs[-1]
    x_ref, u_ref = targets[0], targets[1]
    grid = levels * width
    part = quarter // pieces
    small, large = [], []
    for i in range(1, count):
        small.append(pltpu.make_async_copy(sources[i], targets[i], sems.at[pieces + i - 1]))
    for i in range(pieces):
        rows = pl.ds(i * part * grid, part * grid)
        large.append(pltpu.make_async_copy(sources[0].at[rows], x_ref.at[rows], sems.at[i]))
    small[0].start()
    for copy in large + small[1:]:
        copy.start()
    small[0].wait()
    row = levels * 3 * quarter
    parts = split3(u_ref[pl.ds(0, levels, stride=width), :])
    parts = jnp.concatenate(parts + (jnp.zeros_like(parts[0]),), axis=0)
    a_ref[row : row + 4 * levels, :] = parts.astype(BF16)
    b_ref[row : row + 4 * levels, :] = parts.astype(BF16)
    for i in range(pieces):
        large[i].wait()
        for level in range(levels):
            start = i * part * grid + level * width
            cells = [x_ref[pl.ds(start + c, part, stride=grid), :] for c in range(width)]
            for c in range(3):
                row = (level * 3 + c) * quarter + i * part
                low, high = cells[c], cells[width - 3 + c]
                a_ref[row : row + part, :] = jnp.where(even, high, low).astype(BF16)
                b_ref[row : row + part, :] = jnp.where(even, low, high).astype(BF16)
    for copy in small[1:]:
        copy.wait()


def local_kernel(
    levels,
    width,
    quarter,
    tile_ref,
    flag_ref,
    x_ref,
    cycle_ref,
    edge_ref,
    entry_ref,
    sun_ref,
    mix_ref,
    base_ref,
    weight_ref,
    table_ref,
    turn_ref,
    own_ref,
    tab_ref,
):
    grid = levels * width
    chunk = 32
    row = lax.broadcasted_iota(jnp.int32, (LANES, LANES), 0)
    col = lax.broadcasted_iota(jnp.int32, (LANES, LANES), 1)
    even = (tile_ref[0, 0] & 1) == 0
    for side in range(2):
        flag = jnp.broadcast_to(flag_ref[0:1, side : side + 1], (LANES, LANES))
        source = jnp.where(flag > 0, LANES - 1 - col, col)
        turn = jnp.where(row == source, 1.0, 0.0)
        from_a = jnp.logical_xor(even, side == 0)
        place = slice(side * LANES, (side + 1) * LANES)
        turn_ref[0:LANES, place] = jnp.where(from_a, turn, 0.0).astype(BF16)
        turn_ref[LANES : 2 * LANES, place] = jnp.where(from_a, 0.0, turn).astype(BF16)
    entries = entry_ref.shape[0]
    tab_ref[...] = jnp.zeros_like(tab_ref)
    tab_ref[0:entries, :] = entry_ref[...].astype(F32)
    tab_ref[entries : entries + 1, :] = sun_ref[...].astype(F32)
    for i, part in enumerate(split3(mix_ref[...])):
        row = entries + 1 + i * (levels - 1)
        tab_ref[row : row + levels - 1, :] = part
    table_ref[...] = tab_ref[...].astype(BF16)
    shape = (grid, LANES)
    lane = lax.broadcasted_iota(jnp.int32, shape, 1)
    column = lax.broadcasted_iota(jnp.int32, shape, 0) % width
    faces = face_weights(cycle_ref[...])
    after = [jnp.where(column == width - 1, 0.0, pltpu.roll(w, grid - 1, 0)) for w in faces]
    across = cell_weights(faces, after)
    for k in range(7):
        weight_ref[k] = across[k]
    faces = face_weights(jnp.where(lane == 0, 0.0, edge_ref[...]))
    along = cell_weights(faces, [pltpu.roll(w, LANES - 1, 1) for w in faces])
    low3, low2, low1, here, high1, high2, high3 = along
    here = jnp.where(lane == 0, here + low1 + low2 + low3, here)
    low1 = jnp.where(lane == 1, low1 + low2 + low3, low1)
    low2 = jnp.where(lane == 2, low2 + low3, low2)
    here = jnp.where(lane == LANES - 1, here + high1 + high2 + high3, here)
    high1 = jnp.where(lane == LANES - 2, high1 + high2 + high3, high1)
    high2 = jnp.where(lane == LANES - 3, high2 + high3, high2)
    own_ref[0] = jnp.where(lane < 3, 0.0, low3)
    own_ref[1] = jnp.where(lane < 2, 0.0, low2)
    own_ref[2] = jnp.where(lane < 1, 0.0, low1)
    own_ref[3] = 1.0 + here + across[3]
    own_ref[4] = jnp.where(lane > LANES - 2, 0.0, high1)
    own_ref[5] = jnp.where(lane > LANES - 3, 0.0, high2)
    own_ref[6] = jnp.where(lane > LANES - 4, 0.0, high3)
    for level in range(levels):
        for start in range(0, quarter, chunk):
            cells = [
                x_ref[pl.ds(start * grid + level * width + col, chunk, stride=grid), :]
                for col in range(width)
            ]
            for col in range(width):
                cell = level * width + col
                total = cells[col] * own_ref[3, cell : cell + 1, :]
                for k in (-3, -2, -1, 1, 2, 3):
                    moved = pltpu.roll(cells[col], (-k) % LANES, 1)
                    total = total + moved * own_ref[3 + k, cell : cell + 1, :]
                    if 0 <= col + k < width:
                        total = total + cells[col + k] * weight_ref[3 + k, cell : cell + 1, :]
                base_ref[cell, start : start + chunk, :] = total


def maps_kernel(rank_ref, map_ref, off_ref, full_ref, last_ref, shift_ref, scratch_ref):
    rank = rank_ref[0, 0]
    count, quarter, species = full_ref.shape
    parts = species // quarter
    entries = count // parts
    row = lax.broadcasted_iota(jnp.int32, (species, species), 0)
    col = lax.broadcasted_iota(jnp.int32, (species, species), 1)
    shuffle = jnp.where(row == (col ^ (rank * quarter)), 1.0, 0.0).astype(BF16)
    for e in range(entries):
        moved = jnp.dot(map_ref[e], shuffle, preferred_element_type=F32).astype(BF16)
        for k in range(parts):
            scratch_ref[e * parts + k] = moved[k * quarter : (k + 1) * quarter, :]
    for e in range(entries):
        for k in range(parts):
            block = scratch_ref[e * parts + (rank ^ k)]
            full_ref[e * parts + k] = block
            if k < 2:
                last_ref[2 * e + k] = block
    for k in range(parts):
        shift_ref[k] = off_ref[rank ^ k]


def flow_kernel(
    levels,
    width,
    quarter,
    rank_ref,
    x_ref,
    base_ref,
    weight_ref,
    table_ref,
    turn_ref,
    a0_ref,
    a1_ref,
    b_ref,
    mine_ref,
    other_ref,
):
    grid = levels * width
    even = (rank_ref[0, 0] & 1) == 0
    halo = levels * 3 * quarter

    def received(begin, size):
        rows = slice(begin, begin + size)
        return jnp.concatenate([a0_ref[rows, :] + a1_ref[rows, :], b_ref[rows, :]], axis=1)

    def turned(values):
        both = jnp.dot(values, turn_ref[...], preferred_element_type=F32)
        return both[:, 0:LANES], both[:, LANES : 2 * LANES]

    _, split = turned(received(halo, 4 * levels))
    closing = split[0:levels] + split[levels : 2 * levels] + split[2 * levels : 3 * levels]
    closing = face_weights(closing)
    chunk = 32
    for level in range(levels):
        for start in range(0, quarter, chunk):
            begins = [(level * 3 + i) * quarter + start for i in range(3)]
            low, high = turned(
                jnp.concatenate([received(begin, chunk) for begin in begins], axis=0)
            )
            outer = {i - 3: low[i * chunk : (i + 1) * chunk] for i in range(3)}
            outer.update({width + i: high[i * chunk : (i + 1) * chunk] for i in range(3)})
            moved = []
            for c in range(width):
                cell = level * width + c
                total = base_ref[cell, start : start + chunk, :]
                for k in range(-3, 4):
                    if c + k in outer and not (c == width - 1 and k == 3):
                        total = total + outer[c + k] * weight_ref[3 + k, cell : cell + 1, :]
                if c == width - 1:
                    for k in range(-3, 3):
                        if width + k in outer:
                            value = outer[width + k]
                        else:
                            begin = start * grid + level * width + width + k
                            value = x_ref[pl.ds(begin, chunk, stride=grid), :]
                        total = total - value * closing[3 + k][level : level + 1, :]
                moved.append(total)
            for k in range(width // 2):
                low, high = moved[k], moved[width // 2 + k]
                begin = (level * (width // 2) + k) * quarter + start
                mine_ref[begin : begin + chunk, :] = jnp.where(even, low, high).astype(BF16)
                other_ref[begin : begin + chunk, :] = jnp.where(even, high, low).astype(BF16)
    begin = grid // 2 * quarter
    mine_ref[begin : begin + TABLE_ROWS, :] = table_ref[...]
    other_ref[begin : begin + TABLE_ROWS, :] = table_ref[...]


def tables_of(rank, tails):
    lane = lax.broadcasted_iota(jnp.int32, (TABLE_ROWS, LANES), 1)
    t0, t1, t2, t3 = [t.astype(F32) for t in tails]
    odd = (rank & 1) > 0
    t0, t1 = jnp.where(odd, t1, t0), jnp.where(odd, t0, t1)
    t2, t3 = jnp.where(odd, t3, t2), jnp.where(odd, t2, t3)
    upper = (rank & 2) > 0
    t0, t2 = jnp.where(upper, t2, t0), jnp.where(upper, t0, t2)
    t1, t3 = jnp.where(upper, t3, t1), jnp.where(upper, t1, t3)
    return block_transpose((t0, t1, t2, t3), lane)


def chem_kernel(
    levels,
    width,
    quarter,
    entries,
    substeps,
    rank_ref,
    block0_ref,
    block1_ref,
    block2_ref,
    block3_ref,
    tail0_ref,
    tail1_ref,
    tail2_ref,
    tail3_ref,
    map_ref,
    last_ref,
    off_ref,
    keep_ref,
    give_ref,
    chem_ref,
):
    block_refs = (block0_ref, block1_ref, block2_ref, block3_ref)
    tail_refs = (tail0_ref, tail1_ref, tail2_ref, tail3_ref)
    parts = len(block_refs)
    species = parts * quarter
    half = width // 2
    even = (rank_ref[0, 0] & 1) == 0
    tables = tables_of(rank_ref[0, 0], [r[...] for r in tail_refs])
    columns = [jnp.where(even, tables[k], tables[half + k]) for k in range(half)]

    def row_of(index):
        return jnp.concatenate([columns[k][index : index + 1, :] for k in range(half)], axis=1)

    def block(part, group):
        return block_refs[part][group * quarter : (group + 1) * quarter, :]

    sun = substeps * levels
    lit = row_of(sun) > 0.0
    any_lit = jnp.max(row_of(sun)) > 0.0

    @pl.when(any_lit)
    def lit_tile():
        start = []
        for level in range(levels):
            cells = [
                jnp.concatenate([block(p, level * half + k) for p in range(parts)], axis=0)
                for k in range(half)
            ]
            start.append(jnp.concatenate(cells, axis=1))
        state = list(start)
        for step in range(substeps):
            final = step == substeps - 1
            rows = 2 * quarter if final else species
            matrix = last_ref[...] if final else map_ref[...]
            for level in range(levels):
                product = jnp.dot(matrix, state[level], preferred_element_type=F32)
                entry = row_of(step * levels + level)
                chosen = product[0:rows] + off_ref[0:rows, 0:1]
                for e in range(1, entries):
                    chosen = jnp.where(
                        entry == float(e),
                        product[e * rows : (e + 1) * rows] + off_ref[0:rows, e : e + 1],
                        chosen,
                    )
                chosen = jnp.maximum(chosen, 0.0)
                if not final:
                    state[level] = chosen.astype(BF16)
                    continue
                chem = jnp.where(lit, chosen, start[level][0:rows].astype(F32))
                for k in range(half):
                    chem_ref[level * half + k] = chem[:, k * LANES : (k + 1) * LANES]

    @pl.when(jnp.logical_not(any_lit))
    def dark_tile():
        for group in range(levels * half):
            for p in range(2):
                rows = slice(p * quarter, (p + 1) * quarter)
                chem_ref[group, rows, :] = block(p, group).astype(F32)

    chunk = 32
    for k in range(half):
        pieces = [
            columns[k][sun + 1 + i * (levels - 1) : sun + 1 + (i + 1) * (levels - 1), :]
            for i in range(3)
        ]
        mixed = pieces[0] + pieces[1] + pieces[2]
        mixing = [mixed[i : i + 1, :] for i in range(levels - 1)]
        inverse, ratio = [], []
        for level in range(levels):
            diagonal = 1.0
            if level > 0:
                diagonal = diagonal + mixing[level - 1]
            if level < levels - 1:
                diagonal = diagonal + mixing[level]
            if level > 0:
                diagonal = diagonal - mixing[level - 1] * ratio[level - 1]
            inverse.append(1.0 / diagonal)
            if level < levels - 1:
                ratio.append(mixing[level] * inverse[level])
        for p, out_ref in enumerate((keep_ref, give_ref)):
            for begin in range(0, quarter, chunk):
                solved = []
                for level in range(levels):
                    rows = slice(p * quarter + begin, p * quarter + begin + chunk)
                    value = chem_ref[level * half + k, rows, :]
                    if level > 0:
                        value = value + mixing[level - 1] * solved[-1]
                    solved.append(value * inverse[level])
                for level in range(levels - 2, -1, -1):
                    solved[level] = solved[level] + ratio[level] * solved[level + 1]
                for level in range(levels):
                    place = begin * levels * half + level * half + k
                    out_ref[pl.ds(place, chunk, stride=levels * half), :] = solved[level]


def keep_kernel(rank_ref, keep_ref, out_hbm, sem):
    copy = pltpu.make_async_copy(keep_ref, out_hbm.at[:, rank_ref[0, 0] & 1], sem)
    copy.start()
    copy.wait()


def fill_kernel(rank_ref, got_ref, part_hbm, out_hbm, sem):
    del part_hbm
    copy = pltpu.make_async_copy(got_ref, out_hbm.at[:, 1 - (rank_ref[0, 0] & 1)], sem)
    copy.start()
    copy.wait()


def shards(
    tracers,
    courant_cycle,
    courant_edge,
    seam_flags,
    sunlit,
    table_entry,
    linear_maps,
    offsets,
    mixing,
):
    quarter, levels, width, length = tracers.shape
    grid = levels * width
    substeps = table_entry.shape[0]
    entries, species, _ = linear_maps.shape
    count = lax.axis_size("tile")
    parts = lax.axis_size("trc")
    pairs = [(i, i ^ 1) for i in range(count)]
    seams = [(i, (i + (1 if i % 2 else -1)) % count) for i in range(count)]
    tile = lax.axis_index("tile").astype(jnp.int32).reshape(1, 1)
    halo = levels * 3 * quarter
    pieces = 4
    shape = jax.ShapeDtypeStruct
    brought = [
        tracers.reshape(quarter * grid, length),
        courant_cycle.reshape(grid, length),
        courant_edge.reshape(grid, length),
        table_entry,
        sunlit,
        mixing,
        seam_flags,
    ]
    to_a, to_b, x, cycle, edge, entry, sun, mix, flags = pl.pallas_call(
        functools.partial(pack_kernel, levels, width, quarter, pieces),
        out_shape=(
            shape((halo + 4 * levels, length), BF16),
            shape((halo + 4 * levels, length), BF16),
            *[shape(array.shape, array.dtype) for array in brought],
        ),
        in_specs=[smem()] + [hbm()] * len(brought),
        out_specs=(vmem(),) * (2 + len(brought)),
        scratch_shapes=[pltpu.SemaphoreType.DMA((pieces + len(brought) - 1,))],
        compiler_params=params(8),
        name="pack",
    )(tile, *[in_hbm(array) for array in brought])
    from_a0 = lax.ppermute(to_a, "tile", pairs[:2])
    from_b = lax.ppermute(to_b, "tile", seams)
    from_a1 = lax.ppermute(to_a, "tile", pairs[2:])
    rank = lax.axis_index("trc").astype(jnp.int32).reshape(1, 1)
    base, weights, table, turns = pl.pallas_call(
        functools.partial(local_kernel, levels, width, quarter),
        out_shape=(
            shape((grid, quarter, length), F32),
            shape((7, grid, length), F32),
            shape((TABLE_ROWS, length), BF16),
            shape((2 * length, 2 * length), BF16),
        ),
        in_specs=[smem()] + [vmem()] * 7,
        out_specs=(vmem(),) * 4,
        scratch_shapes=[
            pltpu.VMEM((7, grid, length), F32),
            pltpu.VMEM((TABLE_ROWS, length), F32),
        ],
        compiler_params=params(8),
        cost_estimate=pl.CostEstimate(flops=4000000, bytes_accessed=1 << 20, transcendentals=0),
        name="local",
    )(
        tile,
        flags,
        x,
        cycle,
        edge,
        entry.reshape(substeps * levels, length),
        sun.reshape(1, length),
        mix.reshape(levels - 1, length),
    )
    rows = grid // 2 * quarter
    mine, other = pl.pallas_call(
        functools.partial(flow_kernel, levels, width, quarter),
        out_shape=(shape((rows + TABLE_ROWS, length), BF16),) * 2,
        in_specs=[smem()] + [vmem()] * 8,
        out_specs=(vmem(),) * 2,
        compiler_params=params(8),
        name="flow",
    )(rank, x, base, weights, table, turns, from_a0, from_a1, from_b)
    swap = {k: [(i, i ^ k) for i in range(parts)] for k in (1, 2, 3)}
    second = lax.ppermute(mine, "trc", swap[2])
    third = lax.ppermute(other, "trc", swap[3])
    first = lax.ppermute(other, "trc", swap[1])
    full, last, shift = pl.pallas_call(
        maps_kernel,
        out_shape=(
            shape((entries * parts, quarter, species), BF16),
            shape((2 * entries, quarter, species), BF16),
            shape((parts, quarter, entries), F32),
        ),
        in_specs=[smem()] + [vmem()] * 2,
        out_specs=(vmem(),) * 3,
        scratch_shapes=[pltpu.VMEM((entries * parts, quarter, species), BF16)],
        compiler_params=params(8),
        cost_estimate=pl.CostEstimate(flops=4000000, bytes_accessed=1 << 20, transcendentals=0),
        name="maps",
    )(rank, linear_maps, offsets.T.reshape(parts, quarter, entries))
    blocks = [mine, first, second, third]
    keep, give = pl.pallas_call(
        functools.partial(chem_kernel, levels, width, quarter, entries, substeps),
        out_shape=(shape((rows, length), F32),) * 2,
        in_specs=[smem()] + [vmem()] * 11,
        out_specs=(vmem(),) * 2,
        scratch_shapes=[pltpu.VMEM((grid // 2, 2 * quarter, length), F32)],
        compiler_params=params(24),
        name="chem",
    )(
        rank,
        *blocks,
        *[b[rows:] for b in blocks],
        full.reshape(entries * species, species),
        last.reshape(2 * entries * quarter, species),
        shift.reshape(species, entries),
    )
    got = lax.ppermute(give, "trc", swap[1])
    pair = (quarter * levels, width // 2, length)
    whole = shape((quarter * levels, 2, width // 2, length), F32)
    part = pl.pallas_call(
        keep_kernel,
        out_shape=whole,
        in_specs=[smem(), vmem()],
        out_specs=hbm(),
        scratch_shapes=[pltpu.SemaphoreType.DMA],
        compiler_params=params(4),
        cost_estimate=pl.CostEstimate(flops=1000000, bytes_accessed=1 << 19, transcendentals=0),
        name="keep",
    )(rank, keep.reshape(pair))
    out = pl.pallas_call(
        fill_kernel,
        out_shape=whole,
        in_specs=[smem(), vmem(), hbm()],
        out_specs=hbm(),
        scratch_shapes=[pltpu.SemaphoreType.DMA],
        input_output_aliases={2: 0},
        compiler_params=params(4),
        name="fill",
    )(rank, got.reshape(pair), part)
    return out.reshape(quarter, levels, width, length)


def solution(mesh):
    placed = (
        P("trc", None, "tile", None),
        P(None, "tile", None),
        P(None, "tile", None),
        P("tile", None),
        P("tile", "trc"),
        P(None, None, "tile", "trc"),
        P(),
        P(),
        P(None, "tile", "trc"),
    )
    return jax.shard_map(
        shards, mesh=mesh, in_specs=placed, out_specs=P("trc", None, "tile", None), check_vma=False
    )
```

time: 51.3 us -> 44.7 us (0.87)
  Pallas kernels: 8.84 us -> 4.91 us
  waiting for transfers between devices: 10.3 us -> 8.01 us
  local copies, waits for them, and re-layouts: 1.75 us -> 0.4 us
  starting transfers between devices: 29.9 us -> 30.9 us
    pallas_call x3 -> x5, Pallas kernels: 7.05 us -> 3.62 us  [the longest x1 1.25 us: shards(): pl.pallas_call(functools.partial(pack_kernel, levels, width, quarter, pie...]
    ppermute x5 -> x7, waiting for transfers between devices: 10.3 us -> 8.01 us  [the longest x1 3.19 us: shards(): from_b = lax.ppermute(to_b, 'tile', seams)]
    ppermute x5 -> x7, starting transfers between devices: 29.9 us -> 30.9 us  [the longest x1 15.3 us: shards(): from_b = lax.ppermute(to_b, 'tile', seams)]
    reshape x3, local copies, waits for them, and re-layouts: 0.93 us -> 0.25 us  [the longest x1 0.08 us: shards(): mix.reshape(levels - 1, length)]
    unnamed x16 -> x4, local copies, waits for them, and re-layouts: 0.67 us -> 0.01 us
  transfers between devices with their start and end apart: 5 -> 7, of which waited for: 3 -> 4; matrix products, arithmetic and copies ran while one was open for 2% -> 1% of each run, Pallas kernels for 4% -> 5%
where the time goes in v3:
time: 44.7 us; the launch traced here: 44.4 us
  starting transfers between devices  30.9 us (69%)
  waiting for transfers between devices  8.01 us (18%)
  Pallas kernels  4.91 us (11%)
    ppermute x1, starting transfers between devices, shards(): from_b = lax.ppermute(to_b, 'tile', seams)  15.3 us
    ppermute x1, starting transfers between devices, shards(): from_a0 = lax.ppermute(to_a, 'tile', pairs[:2])  3.94 us
    ppermute x1, starting transfers between devices, shards(): first = lax.ppermute(other, 'trc', swap[1])  3.44 us
    ppermute x1, waiting for transfers between devices, shards(): from_b = lax.ppermute(to_b, 'tile', seams)  3.19 us
    ppermute x1, waiting for transfers between devices, shards(): third = lax.ppermute(other, 'trc', swap[3])  3.16 us
    ppermute x1, starting transfers between devices, shards(): third = lax.ppermute(other, 'trc', swap[3])  3.15 us
    ppermute x1, starting transfers between devices, shards(): second = lax.ppermute(mine, 'trc', swap[2])  2.31 us
    ppermute x1, starting transfers between devices, shards(): got = lax.ppermute(give, 'trc', swap[1])  2.12 us
  transfers between devices with their start and end apart: 7, of which 4 were waited for; matrix products, arithmetic and copies ran while one was open for 1% of the time, Pallas kernels for 5%

profile of v3, /device:TPU:1, one launch (start us, length us, event | category | flops | bytes accessed | tf_op | source)
XLA Modules:
  0.0 44.4 jit_solution(17027717031427713407)
XLA Ops:
  0.0 1.2 %pack.1 = (bf16[784,128]{1,0:T(8,128)(2,1)S(1)}, bf16[784,128]{1,0:T(8,128)(2,1)S(1)}, f32[1024,128]{1,0:T(8,128)S(1)}, f32[16,128]{1,0:T(8,128)S(1)}, f32[16,12...) custom-call(s32[1,1]{1,0:T(1,128)} %bitcast.1.refs_0_.tile_ref, ...), custom_call_target="tpu_custom_call" | custom-call | tf_op jit(solution)/shard_map/pack/pallas_call | solution.py:466
  1.3 3.9 %collective-permute-start = (bf16[784,128]{1,0:T(8,128)(2,1)S(1)}, bf16[784,128]{1,0:T(8,128)(2,1)S(1)}, u32[]{:S(2)}, u32[]{:S(2)}) collective-permute-start(bf16[784,128]{1,0:T(8,128)(2,1)S(1)} %get-tuple-element.36), channel_id=1, source_target_pairs={{0,4},{4,0},{1,5},{5,1},{2,6},{6,2},{3,7},{7,3}} | collective-permute-start | bytes 602120 | tf_op jit(solution)/shard_map/ppermute | solution.py:479
  5.2 0.7 %collective-permute-start.1 = (bf16[784,128]{1,0:T(8,128)(2,1)S(1)}, bf16[784,128]{1,0:T(8,128)(2,1)S(1)}, u32[]{:S(2)}, u32[]{:S(2)}) collective-permute-start(bf16[784,128]{1,0:T(8,128)(2,1)S(1)} %get-tuple-element.36), channel_id=1, source_target_pairs={{8,12},{12,8},{16,20},{20,16},{24,28},{28,24},{32,36},{36,32},{40,... | collective-permute-start | bytes 602120 | tf_op jit(solution)/shard_map/ppermute | solution.py:481
  5.9 15.3 %collective-permute-start.2 = (bf16[784,128]{1,0:T(8,128)(2,1)S(1)}, bf16[784,128]{1,0:T(8,128)(2,1)S(1)}, u32[]{:S(2)}, u32[]{:S(2)}) collective-permute-start(bf16[784,128]{1,0:T(8,128)(2,1)S(1)} %get-tuple-element.37), channel_id=1, source_target_pairs={{0,508},{4,8},{8,4},{12,16},{16,12},{20,24},{24,20},{28,32},{32,28... | collective-permute-start | bytes 602120 | tf_op jit(solution)/shard_map/ppermute | solution.py:480
  21.2 0.1 reshape.50.entry_ref
  21.3 0.1 reshape.52.mix_ref
  21.3 0.1 reshape.51.sun_ref
  21.4 0.9 %local.1 = (f32[16,64,128]{2,1,0:T(8,128)S(1)}, f32[7,16,128]{2,1,0:T(8,128)S(1)}, bf16[32,128]{1,0:T(8,128)(2,1)S(1)}, bf16[256,256]{1,0:T(8,128)(2,1)S(1)}) custom-call(s32[1,1]{1,0:T(1,128)} %bitcast.1.refs_0_.tile_ref, s32[1,2]{1,0:T(1,128)S(1)} %get-tuple-element.26.flag_ref, f32[1024,128]{1,0:T(8,128)S(1)} %get-tuple-element.25.x_ref, ...), custom_call_target="tpu_custom_call" | custom-call | flops 4000000 | bytes 1048576 | tf_op jit(solution)/shard_map/local/pallas_call | solution.py:483
  22.4 0.0 collective-permute-done.a0_ref
  22.4 0.0 collective-permute-done.1.a1_ref
  22.4 3.2 %collective-permute-done.2.b_ref = bf16[784,128]{1,0:T(8,128)(2,1)S(1)} collective-permute-done((bf16[784,128]{1,0:T(8,128)(2,1)S(1)}, bf16[784,128]{1,0:T(8,128)(2,1)S(1)}, u32[]{:S(2)}, u32[]{:S(2)}) %collective-permute-start.2) | collective-permute-done | bytes 200736 | tf_op jit(solution)/shard_map/ppermute | solution.py:480
  25.6 0.0 copy-start
  25.6 0.5 %flow.1 = (bf16[544,128]{1,0:T(8,128)(2,1)S(1)}, bf16[544,128]{1,0:T(8,128)(2,1)S(1)}) custom-call(s32[1,1]{1,0:T(1,128)} %bitcast.rank_ref, f32[1024,128]{1,0:T(8,128)S(1)} %get-tuple-element.25.x_ref, f32[16,64,128]{2,1,0:T(8,128)S(1)} %get-tuple-element.32.base_ref, f32[7,16,128]{2,1,0:T(8,128)S(1)} %get-tuple-element.33.weight_ref, ...), custom_call_target="tpu_custom_call" | custom-call | tf_op jit(solution)/shard_map/flow/pallas_call | solution.py:511
  26.1 0.0 copy-start.1
  26.1 3.4 %collective-permute-start.3 = (bf16[544,128]{1,0:T(8,128)(2,1)S(1)}, bf16[544,128]{1,0:T(8,128)(2,1)S(1)}, u32[]{:S(2)}, u32[]{:S(2)}) collective-permute-start(bf16[544,128]{1,0:T(8,128)(2,1)S(1)} %get-tuple-element.39), channel_id=1, source_target_pairs={{0,1},{1,0},{2,3},{3,2},{4,5},{5,4},{6,7},{7,6},{8,9},{9,8},{10,11... | collective-permute-start | bytes 417800 | tf_op jit(solution)/shard_map/ppermute | solution.py:522
  29.5 2.3 %collective-permute-start.4 = (bf16[544,128]{1,0:T(8,128)(2,1)S(1)}, bf16[544,128]{1,0:T(8,128)(2,1)S(1)}, u32[]{:S(2)}, u32[]{:S(2)}) collective-permute-start(bf16[544,128]{1,0:T(8,128)(2,1)S(1)} %get-tuple-element.38.block0_ref), channel_id=1, source_target_pairs={{0,2},{1,3},{2,0},{3,1},{4,6},{5,7},{6,4},{7,5},{8,10},{9,11},{10,... | collective-permute-start | bytes 417800 | tf_op jit(solution)/shard_map/ppermute | solution.py:520
  31.8 3.2 %collective-permute-start.5 = (bf16[544,128]{1,0:T(8,128)(2,1)S(1)}, bf16[544,128]{1,0:T(8,128)(2,1)S(1)}, u32[]{:S(2)}, u32[]{:S(2)}) collective-permute-start(bf16[544,128]{1,0:T(8,128)(2,1)S(1)} %get-tuple-element.39), channel_id=1, source_target_pairs={{0,3},{1,2},{2,1},{3,0},{4,7},{5,6},{6,5},{7,4},{8,11},{9,10},{10,... | collective-permute-start | bytes 417800 | tf_op jit(solution)/shard_map/ppermute | solution.py:521
  35.0 0.0 copy-done.1
  35.0 0.1 copy.11
  35.1 0.0 copy-done
  35.2 0.4 maps.1
  35.5 0.0 collective-permute-done.3.block1_ref
  35.6 1.1 %collective-permute-done.4.block2_ref = bf16[544,128]{1,0:T(8,128)(2,1)S(1)} collective-permute-done((bf16[544,128]{1,0:T(8,128)(2,1)S(1)}, bf16[544,128]{1,0:T(8,128)(2,1)S(1)}, u32[]{:S(2)}, u32[]{:S(2)}) %collective-permute-start.4) | collective-permute-done | bytes 139296 | tf_op jit(solution)/shard_map/ppermute | solution.py:520
  36.6 3.2 %collective-permute-done.5.block3_ref = bf16[544,128]{1,0:T(8,128)(2,1)S(1)} collective-permute-done((bf16[544,128]{1,0:T(8,128)(2,1)S(1)}, bf16[544,128]{1,0:T(8,128)(2,1)S(1)}, u32[]{:S(2)}, u32[]{:S(2)}) %collective-permute-start.5) | collective-permute-done | bytes 139296 | tf_op jit(solution)/shard_map/ppermute | solution.py:521
  39.8 0.5 %chem.1 = (f32[512,128]{1,0:T(8,128)S(1)}, f32[512,128]{1,0:T(8,128)S(1)}) custom-call(s32[1,1]{1,0:T(1,128)} %bitcast.rank_ref, bf16[544,128]{1,0:T(8,128)(2,1)S(1)} %get-tuple-element.38.block0_ref, bf16[544,128]{1,0:T(8,128)(2,1)S(1)} %collective-permute-done.3.block1_ref, bf16[544,128]{1,0:T(8,128)(2,1)S(1)} %collective-permute-done.4.block2_ref, ...), custom_call_target="tpu_custom_call" | custom-call | tf_op jit(solution)/shard_map/chem/pallas_call | solution.py:538
  40.3 2.1 %collective-permute-start.6 = (f32[512,128]{1,0:T(8,128)S(1)}, f32[512,128]{1,0:T(8,128)S(1)}, u32[]{:S(2)}, u32[]{:S(2)}) collective-permute-start(f32[512,128]{1,0:T(8,128)S(1)} %get-tuple-element.43), channel_id=1, source_target_pairs={{0,1},{1,0},{2,3},{3,2},{4,5},{5,4},{6,7},{7,6},{8,9},{9,8},{10,11... | collective-permute-start | bytes 786440 | tf_op jit(solution)/shard_map/ppermute | solution.py:554
  42.4 0.7 %keep.1.part_hbm = f32[256,2,2,128]{3,2,1,0:T(2,128)} custom-call(s32[1,1]{1,0:T(1,128)} %bitcast.rank_ref, f32[256,2,128]{2,1,0:T(2,128)S(1)} %bitcast.17), custom_call_target="tpu_custom_call" | custom-call | flops 1000000 | bytes 524288 | tf_op jit(solution)/shard_map/keep/pallas_call | solution.py:557
  43.1 0.6 %collective-permute-done.6 = f32[512,128]{1,0:T(8,128)S(1)} collective-permute-done((f32[512,128]{1,0:T(8,128)S(1)}, f32[512,128]{1,0:T(8,128)S(1)}, u32[]{:S(2)}, u32[]{:S(2)}) %collective-permute-start.6) | collective-permute-done | bytes 262176 | tf_op jit(solution)/shard_map/ppermute | solution.py:554
  43.7 0.7 %fill.1 = f32[256,2,2,128]{3,2,1,0:T(2,128)} custom-call(s32[1,1]{1,0:T(1,128)} %bitcast.rank_ref, f32[256,2,128]{2,1,0:T(2,128)S(1)} %bitcast.15, f32[256,2,2,128]{3,2,1,0:T(2,128)} %keep.1.part_hbm), custom_call_target="tpu_custom_call", output_to_operand_aliasing={{}: (2, {})} | custom-call | tf_op jit(solution)/shard_map/fill/pallas_call | solution.py:567
  (4 shorter events, 0.0 us)
Async XLA Ops:
  1.3 21.1 %collective-permute-start = (bf16[784,128]{1,0:T(8,128)(2,1)S(1)}, bf16[784,128]{1,0:T(8,128)(2,1)S(1)}, u32[]{:S(2)}, u32[]{:S(2)}) collective-permute-start(bf16[784,128]{1,0:T(8,128)(2,1)S(1)} %get-tuple-element.36), channel_id=1, source_target_pairs={{0,4},{4,0},{1,5},{5,1},{2,6},{6,2},{3,7},{7,3}} | collective-permute-start | bytes 602120 | tf_op jit(solution)/shard_map/ppermute | solution.py:479
  5.2 17.2 %collective-permute-start.1 = (bf16[784,128]{1,0:T(8,128)(2,1)S(1)}, bf16[784,128]{1,0:T(8,128)(2,1)S(1)}, u32[]{:S(2)}, u32[]{:S(2)}) collective-permute-start(bf16[784,128]{1,0:T(8,128)(2,1)S(1)} %get-tuple-element.36), channel_id=1, source_target_pairs={{8,12},{12,8},{16,20},{20,16},{24,28},{28,24},{32,36},{36,32},{40,... | collective-permute-start | bytes 602120 | tf_op jit(solution)/shard_map/ppermute | solution.py:481
  5.9 19.7 %collective-permute-start.2 = (bf16[784,128]{1,0:T(8,128)(2,1)S(1)}, bf16[784,128]{1,0:T(8,128)(2,1)S(1)}, u32[]{:S(2)}, u32[]{:S(2)}) collective-permute-start(bf16[784,128]{1,0:T(8,128)(2,1)S(1)} %get-tuple-element.37), channel_id=1, source_target_pairs={{0,508},{4,8},{8,4},{12,16},{16,12},{20,24},{24,20},{28,32},{32,28... | collective-permute-start | bytes 602120 | tf_op jit(solution)/shard_map/ppermute | solution.py:480
  25.6 9.6 %copy-start = (bf16[4,256,256]{2,1,0:T(8,128)(2,1)S(1)}, bf16[4,256,256]{2,1,0:T(8,128)(2,1)}, u32[]{:S(2)}) copy-start(bf16[4,256,256]{2,1,0:T(8,128)(2,1)} %map_ref.1) | copy-start | bytes 1572868
  26.1 8.9 %copy-start.1 = (f32[4,256]{1,0:T(4,128)S(1)}, f32[4,256]{1,0:T(4,128)}, u32[]{:S(2)}) copy-start(f32[4,256]{1,0:T(4,128)} %param.16) | copy-start | bytes 12292
  26.1 9.5 %collective-permute-start.3 = (bf16[544,128]{1,0:T(8,128)(2,1)S(1)}, bf16[544,128]{1,0:T(8,128)(2,1)S(1)}, u32[]{:S(2)}, u32[]{:S(2)}) collective-permute-start(bf16[544,128]{1,0:T(8,128)(2,1)S(1)} %get-tuple-element.39), channel_id=1, source_target_pairs={{0,1},{1,0},{2,3},{3,2},{4,5},{5,4},{6,7},{7,6},{8,9},{9,8},{10,11... | collective-permute-start | bytes 417800 | tf_op jit(solution)/shard_map/ppermute | solution.py:522
  29.5 7.1 %collective-permute-start.4 = (bf16[544,128]{1,0:T(8,128)(2,1)S(1)}, bf16[544,128]{1,0:T(8,128)(2,1)S(1)}, u32[]{:S(2)}, u32[]{:S(2)}) collective-permute-start(bf16[544,128]{1,0:T(8,128)(2,1)S(1)} %get-tuple-element.38.block0_ref), channel_id=1, source_target_pairs={{0,2},{1,3},{2,0},{3,1},{4,6},{5,7},{6,4},{7,5},{8,10},{9,11},{10,... | collective-permute-start | bytes 417800 | tf_op jit(solution)/shard_map/ppermute | solution.py:520
  31.8 8.0 %collective-permute-start.5 = (bf16[544,128]{1,0:T(8,128)(2,1)S(1)}, bf16[544,128]{1,0:T(8,128)(2,1)S(1)}, u32[]{:S(2)}, u32[]{:S(2)}) collective-permute-start(bf16[544,128]{1,0:T(8,128)(2,1)S(1)} %get-tuple-element.39), channel_id=1, source_target_pairs={{0,3},{1,2},{2,1},{3,0},{4,7},{5,6},{6,5},{7,4},{8,11},{9,10},{10,... | collective-permute-start | bytes 417800 | tf_op jit(solution)/shard_map/ppermute | solution.py:521
  40.3 3.4 %collective-permute-start.6 = (f32[512,128]{1,0:T(8,128)S(1)}, f32[512,128]{1,0:T(8,128)S(1)}, u32[]{:S(2)}, u32[]{:S(2)}) collective-permute-start(f32[512,128]{1,0:T(8,128)S(1)} %get-tuple-element.43), channel_id=1, source_target_pairs={{0,1},{1,0},{2,3},{3,2},{4,5},{5,4},{6,7},{7,6},{8,9},{9,8},{10,11... | collective-permute-start | bytes 786440 | tf_op jit(solution)/shard_map/ppermute | solution.py:554

commit v4 on v3

--- a/solution.py
+++ b/solution.py
@@ -125,7 +125,6 @@
     levels,
     width,
     quarter,
-    tile_ref,
     flag_ref,
     x_ref,
     cycle_ref,
@@ -144,15 +143,10 @@
     chunk = 32
     row = lax.broadcasted_iota(jnp.int32, (LANES, LANES), 0)
     col = lax.broadcasted_iota(jnp.int32, (LANES, LANES), 1)
-    even = (tile_ref[0, 0] & 1) == 0
     for side in range(2):
         flag = jnp.broadcast_to(flag_ref[0:1, side : side + 1], (LANES, LANES))
         source = jnp.where(flag > 0, LANES - 1 - col, col)
-        turn = jnp.where(row == source, 1.0, 0.0)
-        from_a = jnp.logical_xor(even, side == 0)
-        place = slice(side * LANES, (side + 1) * LANES)
-        turn_ref[0:LANES, place] = jnp.where(from_a, turn, 0.0).astype(BF16)
-        turn_ref[LANES : 2 * LANES, place] = jnp.where(from_a, 0.0, turn).astype(BF16)
+        turn_ref[side] = jnp.where(row == source, 1.0, 0.0).astype(BF16)
     entries = entry_ref.shape[0]
     tab_ref[...] = jnp.zeros_like(tab_ref)
     tab_ref[0:entries, :] = entry_ref[...].astype(F32)
@@ -224,68 +218,111 @@
         shift_ref[k] = off_ref[rank ^ k]
 
 
+def halo_terms(levels, width, quarter, side, level, start, chunk, closing, x_ref, weight_ref, turn_ref, halo_of):
+    grid = levels * width
+    begins = [(level * 3 + i) * quarter + start for i in range(3)]
+    values = jnp.concatenate([halo_of(begin, chunk) for begin in begins], axis=0)
+    values = jnp.dot(values, turn_ref[side], preferred_element_type=F32)
+    offset = width if side else -3
+    outer = {offset + i: values[i * chunk : (i + 1) * chunk] for i in range(3)}
+    terms = []
+    for c in range(width):
+        cell = level * width + c
+        total = None
+        for k in range(-3, 4):
+            if c + k in outer and not (c == width - 1 and k == 3):
+                term = outer[c + k] * weight_ref[3 + k, cell : cell + 1, :]
+                total = term if total is None else total + term
+        if side and c == width - 1:
+            for k in range(-3, 3):
+                if width + k in outer:
+                    value = outer[width + k]
+                else:
+                    begin = start * grid + level * width + width + k
+                    value = x_ref[pl.ds(begin, chunk, stride=grid), :]
+                total = total - value * closing[3 + k][level : level + 1, :]
+        terms.append(total)
+    return terms
+
+
+def closing_weights(levels, quarter, turn_ref, halo_of):
+    split = halo_of(levels * 3 * quarter, 4 * levels)
+    split = jnp.dot(split, turn_ref[1], preferred_element_type=F32)
+    return face_weights(split[0:levels] + split[levels : 2 * levels] + split[2 * levels : 3 * levels])
+
+
+def near_kernel(
+    levels, width, quarter, tile_ref, x_ref, base_ref, weight_ref, turn_ref, a0_ref, a1_ref, near_ref
+):
+    chunk = 32
+    even = (tile_ref[0, 0] & 1) == 0
+
+    def halo_of(begin, size):
+        return a0_ref[begin : begin + size, :] + a1_ref[begin : begin + size, :]
+
+    def work(side):
+        closing = closing_weights(levels, quarter, turn_ref, halo_of) if side else None
+        for level in range(levels):
+            for start in range(0, quarter, chunk):
+                terms = halo_terms(
+                    levels, width, quarter, side, level, start, chunk, closing,
+                    x_ref, weight_ref, turn_ref, halo_of,
+                )
+                for c in range(width):
+                    cell = level * width + c
+                    total = base_ref[cell, start : start + chunk, :]
+                    if terms[c] is not None:
+                        total = total + terms[c]
+                    near_ref[cell, start : start + chunk, :] = total
+
+    pl.when(even)(lambda: work(1))
+    pl.when(jnp.logical_not(even))(lambda: work(0))
+
+
 def flow_kernel(
     levels,
     width,
     quarter,
     rank_ref,
+    tile_ref,
     x_ref,
-    base_ref,
+    near_ref,
     weight_ref,
     table_ref,
     turn_ref,
-    a0_ref,
-    a1_ref,
     b_ref,
     mine_ref,
     other_ref,
 ):
-    grid = levels * width
-    even = (rank_ref[0, 0] & 1) == 0
-    halo = levels * 3 * quarter
-
-    def received(begin, size):
-        rows = slice(begin, begin + size)
-        return jnp.concatenate([a0_ref[rows, :] + a1_ref[rows, :], b_ref[rows, :]], axis=1)
-
-    def turned(values):
-        both = jnp.dot(values, turn_ref[...], preferred_element_type=F32)
-        return both[:, 0:LANES], both[:, LANES : 2 * LANES]
-
-    _, split = turned(received(halo, 4 * levels))
-    closing = split[0:levels] + split[levels : 2 * levels] + split[2 * levels : 3 * levels]
-    closing = face_weights(closing)
     chunk = 32
-    for level in range(levels):
-        for start in range(0, quarter, chunk):
-            begins = [(level * 3 + i) * quarter + start for i in range(3)]
-            low, high = turned(
-                jnp.concatenate([received(begin, chunk) for begin in begins], axis=0)
-            )
-            outer = {i - 3: low[i * chunk : (i + 1) * chunk] for i in range(3)}
-            outer.update({width + i: high[i * chunk : (i + 1) * chunk] for i in range(3)})
-            moved = []
-            for c in range(width):
-                cell = level * width + c
-                total = base_ref[cell, start : start + chunk, :]
-                for k in range(-3, 4):
-                    if c + k in outer and not (c == width - 1 and k == 3):
-                        total = total + outer[c + k] * weight_ref[3 + k, cell : cell + 1, :]
-                if c == width - 1:
-                    for k in range(-3, 3):
-                        if width + k in outer:
-                            value = outer[width + k]
-                        else:
-                            begin = start * grid + level * width + width + k
-                            value = x_ref[pl.ds(begin, chunk, stride=grid), :]
-                        total = total - value * closing[3 + k][level : level + 1, :]
-                moved.append(total)
-            for k in range(width // 2):
-                low, high = moved[k], moved[width // 2 + k]
-                begin = (level * (width // 2) + k) * quarter + start
-                mine_ref[begin : begin + chunk, :] = jnp.where(even, low, high).astype(BF16)
-                other_ref[begin : begin + chunk, :] = jnp.where(even, high, low).astype(BF16)
-    begin = grid // 2 * quarter
+    half = width // 2
+    first_core = (rank_ref[0, 0] & 1) == 0
+    even = (tile_ref[0, 0] & 1) == 0
+
+    def halo_of(begin, size):
+        return b_ref[begin : begin + size, :]
+
+    def work(side):
+        closing = closing_weights(levels, quarter, turn_ref, halo_of) if side else None
+        for level in range(levels):
+            for start in range(0, quarter, chunk):
+                terms = halo_terms(
+                    levels, width, quarter, side, level, start, chunk, closing,
+                    x_ref, weight_ref, turn_ref, halo_of,
+                )
+                moved = []
+                for c in range(width):
+                    total = near_ref[level * width + c, start : start + chunk, :]
+                    moved.append(total if terms[c] is None else total + terms[c])
+                for k in range(half):
+                    low, high = moved[k], moved[half + k]
+                    begin = (level * half + k) * quarter + start
+                    mine_ref[begin : begin + chunk, :] = jnp.where(first_core, low, high).astype(BF16)
+                    other_ref[begin : begin + chunk, :] = jnp.where(first_core, high, low).astype(BF16)
+
+    pl.when(even)(lambda: work(0))
+    pl.when(jnp.logical_not(even))(lambda: work(1))
+    begin = levels * half * quarter
     mine_ref[begin : begin + TABLE_ROWS, :] = table_ref[...]
     other_ref[begin : begin + TABLE_ROWS, :] = table_ref[...]
 
@@ -486,9 +523,9 @@
             shape((grid, quarter, length), F32),
             shape((7, grid, length), F32),
             shape((TABLE_ROWS, length), BF16),
-            shape((2 * length, 2 * length), BF16),
+            shape((2, length, length), BF16),
         ),
-        in_specs=[smem()] + [vmem()] * 7,
+        in_specs=[vmem()] * 7,
         out_specs=(vmem(),) * 4,
         scratch_shapes=[
             pltpu.VMEM((7, grid, length), F32),
@@ -498,7 +535,6 @@
         cost_estimate=pl.CostEstimate(flops=4000000, bytes_accessed=1 << 20, transcendentals=0),
         name="local",
     )(
-        tile,
         flags,
         x,
         cycle,
@@ -508,14 +544,22 @@
         mix.reshape(levels - 1, length),
     )
     rows = grid // 2 * quarter
+    near = pl.pallas_call(
+        functools.partial(near_kernel, levels, width, quarter),
+        out_shape=shape((grid, quarter, length), F32),
+        in_specs=[smem()] + [vmem()] * 6,
+        out_specs=vmem(),
+        compiler_params=params(8),
+        name="near",
+    )(tile, x, base, weights, turns, from_a0, from_a1)
     mine, other = pl.pallas_call(
         functools.partial(flow_kernel, levels, width, quarter),
         out_shape=(shape((rows + TABLE_ROWS, length), BF16),) * 2,
-        in_specs=[smem()] + [vmem()] * 8,
+        in_specs=[smem()] * 2 + [vmem()] * 6,
         out_specs=(vmem(),) * 2,
         compiler_params=params(8),
         name="flow",
-    )(rank, x, base, weights, table, turns, from_a0, from_a1, from_b)
+    )(rank, tile, x, near, weights, table, turns, from_b)
     swap = {k: [(i, i ^ k) for i in range(parts)] for k in (1, 2, 3)}
     second = lax.ppermute(mine, "trc", swap[2])
     third = lax.ppermute(other, "trc", swap[3])

time: 44.7 us -> 44.5 us (level)
  no operation moved by 1% of the time
where the time goes in v4:
time: 44.5 us; the launch traced here: 44.2 us
  starting transfers between devices  30.9 us (69%)
  waiting for transfers between devices  7.68 us (17%)
  Pallas kernels  4.99 us (11%)
    ppermute x1, starting transfers between devices, shards(): from_b = lax.ppermute(to_b, 'tile', seams)  15.3 us
    ppermute x1, starting transfers between devices, shards(): from_a0 = lax.ppermute(to_a, 'tile', pairs[:2])  3.94 us
    ppermute x1, starting transfers between devices, shards(): first = lax.ppermute(other, 'trc', swap[1])  3.43 us
    ppermute x1, waiting for transfers between devices, shards(): third = lax.ppermute(other, 'trc', swap[3])  3.16 us
    ppermute x1, starting transfers between devices, shards(): third = lax.ppermute(other, 'trc', swap[3])  3.15 us
    ppermute x1, waiting for transfers between devices, shards(): from_b = lax.ppermute(to_b, 'tile', seams)  2.86 us
    ppermute x1, starting transfers between devices, shards(): second = lax.ppermute(mine, 'trc', swap[2])  2.31 us
    ppermute x1, starting transfers between devices, shards(): got = lax.ppermute(give, 'trc', swap[1])  2.12 us
  transfers between devices with their start and end apart: 7, of which 4 were waited for; matrix products, arithmetic and copies ran while one was open for 1% of the time, Pallas kernels for 5%

profile of v4, /device:TPU:1, one launch (start us, length us, event | category | flops | bytes accessed | tf_op | source)
XLA Modules:
  0.0 44.2 jit_solution(17326514519023467830)
XLA Ops:
  0.0 1.2 %pack.1 = (bf16[784,128]{1,0:T(8,128)(2,1)S(1)}, bf16[784,128]{1,0:T(8,128)(2,1)S(1)}, f32[1024,128]{1,0:T(8,128)S(1)}, f32[16,128]{1,0:T(8,128)S(1)}, f32[16,12...) custom-call(s32[1,1]{1,0:T(1,128)} %bitcast.1.refs_0_.tile_ref, ...), custom_call_target="tpu_custom_call" | custom-call | tf_op jit(solution)/shard_map/pack/pallas_call | solution.py:503
  1.3 3.9 %collective-permute-start = (bf16[784,128]{1,0:T(8,128)(2,1)S(1)}, bf16[784,128]{1,0:T(8,128)(2,1)S(1)}, u32[]{:S(2)}, u32[]{:S(2)}) collective-permute-start(bf16[784,128]{1,0:T(8,128)(2,1)S(1)} %get-tuple-element.35), channel_id=1, source_target_pairs={{0,4},{4,0},{1,5},{5,1},{2,6},{6,2},{3,7},{7,3}} | collective-permute-start | bytes 602120 | tf_op jit(solution)/shard_map/ppermute | solution.py:516
  5.2 0.7 %collective-permute-start.1 = (bf16[784,128]{1,0:T(8,128)(2,1)S(1)}, bf16[784,128]{1,0:T(8,128)(2,1)S(1)}, u32[]{:S(2)}, u32[]{:S(2)}) collective-permute-start(bf16[784,128]{1,0:T(8,128)(2,1)S(1)} %get-tuple-element.35), channel_id=1, source_target_pairs={{8,12},{12,8},{16,20},{20,16},{24,28},{28,24},{32,36},{36,32},{40,... | collective-permute-start | bytes 602120 | tf_op jit(solution)/shard_map/ppermute | solution.py:518
  5.9 15.3 %collective-permute-start.2 = (bf16[784,128]{1,0:T(8,128)(2,1)S(1)}, bf16[784,128]{1,0:T(8,128)(2,1)S(1)}, u32[]{:S(2)}, u32[]{:S(2)}) collective-permute-start(bf16[784,128]{1,0:T(8,128)(2,1)S(1)} %get-tuple-element.37), channel_id=1, source_target_pairs={{0,508},{4,8},{8,4},{12,16},{16,12},{20,24},{24,20},{28,32},{32,28... | collective-permute-start | bytes 602120 | tf_op jit(solution)/shard_map/ppermute | solution.py:517
  21.2 0.1 reshape.50.entry_ref
  21.3 0.1 reshape.52.mix_ref
  21.3 0.1 reshape.51.sun_ref
  21.4 0.9 %local.1 = (f32[16,64,128]{2,1,0:T(8,128)S(1)}, f32[7,16,128]{2,1,0:T(8,128)S(1)}, bf16[32,128]{1,0:T(8,128)(2,1)S(1)}, bf16[2,128,128]{2,1,0:T(8,128)(2,1)S(1)}) custom-call(s32[1,2]{1,0:T(1,128)S(1)} %get-tuple-element.26.flag_ref, f32[1024,128]{1,0:T(8,128)S(1)} %get-tuple-element.25.x_ref, f32[16,128]{1,0:T(8,128)S(1)} %get-tuple-element.27.cycle_ref, ...), custom_call_target="tpu_custom_call" | custom-call | flops 4000000 | bytes 1048576 | tf_op jit(solution)/shard_map/local/pallas_call | solution.py:520
  22.3 0.0 collective-permute-done.a0_ref
  22.3 0.0 collective-permute-done.1.a1_ref
  22.4 0.3 near.1.near_ref
  22.7 2.9 %collective-permute-done.2.b_ref = bf16[784,128]{1,0:T(8,128)(2,1)S(1)} collective-permute-done((bf16[784,128]{1,0:T(8,128)(2,1)S(1)}, bf16[784,128]{1,0:T(8,128)(2,1)S(1)}, u32[]{:S(2)}, u32[]{:S(2)}) %collective-permute-start.2) | collective-permute-done | bytes 200736 | tf_op jit(solution)/shard_map/ppermute | solution.py:517
  25.6 0.0 copy-start
  25.6 0.2 flow.1
  25.8 0.0 copy-start.1
  25.8 3.4 %collective-permute-start.3 = (bf16[544,128]{1,0:T(8,128)(2,1)S(1)}, bf16[544,128]{1,0:T(8,128)(2,1)S(1)}, u32[]{:S(2)}, u32[]{:S(2)}) collective-permute-start(bf16[544,128]{1,0:T(8,128)(2,1)S(1)} %get-tuple-element.39), channel_id=1, source_target_pairs={{0,1},{1,0},{2,3},{3,2},{4,5},{5,4},{6,7},{7,6},{8,9},{9,8},{10,11... | collective-permute-start | bytes 417800 | tf_op jit(solution)/shard_map/ppermute | solution.py:566
  29.3 2.3 %collective-permute-start.4 = (bf16[544,128]{1,0:T(8,128)(2,1)S(1)}, bf16[544,128]{1,0:T(8,128)(2,1)S(1)}, u32[]{:S(2)}, u32[]{:S(2)}) collective-permute-start(bf16[544,128]{1,0:T(8,128)(2,1)S(1)} %get-tuple-element.38.block0_ref), channel_id=1, source_target_pairs={{0,2},{1,3},{2,0},{3,1},{4,6},{5,7},{6,4},{7,5},{8,10},{9,11},{10,... | collective-permute-start | bytes 417800 | tf_op jit(solution)/shard_map/ppermute | solution.py:564
  31.6 3.2 %collective-permute-start.5 = (bf16[544,128]{1,0:T(8,128)(2,1)S(1)}, bf16[544,128]{1,0:T(8,128)(2,1)S(1)}, u32[]{:S(2)}, u32[]{:S(2)}) collective-permute-start(bf16[544,128]{1,0:T(8,128)(2,1)S(1)} %get-tuple-element.39), channel_id=1, source_target_pairs={{0,3},{1,2},{2,1},{3,0},{4,7},{5,6},{6,5},{7,4},{8,11},{9,10},{10,... | collective-permute-start | bytes 417800 | tf_op jit(solution)/shard_map/ppermute | solution.py:565
  34.8 0.0 copy-done.1
  34.8 0.1 copy.11
  34.9 0.0 copy-done
  34.9 0.4 maps.1
  35.3 0.0 collective-permute-done.3.block1_ref
  35.3 1.1 %collective-permute-done.4.block2_ref = bf16[544,128]{1,0:T(8,128)(2,1)S(1)} collective-permute-done((bf16[544,128]{1,0:T(8,128)(2,1)S(1)}, bf16[544,128]{1,0:T(8,128)(2,1)S(1)}, u32[]{:S(2)}, u32[]{:S(2)}) %collective-permute-start.4) | collective-permute-done | bytes 139296 | tf_op jit(solution)/shard_map/ppermute | solution.py:564
  36.4 3.2 %collective-permute-done.5.block3_ref = bf16[544,128]{1,0:T(8,128)(2,1)S(1)} collective-permute-done((bf16[544,128]{1,0:T(8,128)(2,1)S(1)}, bf16[544,128]{1,0:T(8,128)(2,1)S(1)}, u32[]{:S(2)}, u32[]{:S(2)}) %collective-permute-start.5) | collective-permute-done | bytes 139296 | tf_op jit(solution)/shard_map/ppermute | solution.py:565
  39.6 0.5 %chem.1 = (f32[512,128]{1,0:T(8,128)S(1)}, f32[512,128]{1,0:T(8,128)S(1)}) custom-call(s32[1,1]{1,0:T(1,128)} %bitcast.rank_ref, bf16[544,128]{1,0:T(8,128)(2,1)S(1)} %get-tuple-element.38.block0_ref, bf16[544,128]{1,0:T(8,128)(2,1)S(1)} %collective-permute-done.3.block1_ref, bf16[544,128]{1,0:T(8,128)(2,1)S(1)} %collective-permute-done.4.block2_ref, ...), custom_call_target="tpu_custom_call" | custom-call | tf_op jit(solution)/shard_map/chem/pallas_call | solution.py:582
  40.0 2.1 %collective-permute-start.6 = (f32[512,128]{1,0:T(8,128)S(1)}, f32[512,128]{1,0:T(8,128)S(1)}, u32[]{:S(2)}, u32[]{:S(2)}) collective-permute-start(f32[512,128]{1,0:T(8,128)S(1)} %get-tuple-element.43), channel_id=1, source_target_pairs={{0,1},{1,0},{2,3},{3,2},{4,5},{5,4},{6,7},{7,6},{8,9},{9,8},{10,11... | collective-permute-start | bytes 786440 | tf_op jit(solution)/shard_map/ppermute | solution.py:598
  42.2 0.7 %keep.1.part_hbm = f32[256,2,2,128]{3,2,1,0:T(2,128)} custom-call(s32[1,1]{1,0:T(1,128)} %bitcast.rank_ref, f32[256,2,128]{2,1,0:T(2,128)S(1)} %bitcast.17), custom_call_target="tpu_custom_call" | custom-call | flops 1000000 | bytes 524288 | tf_op jit(solution)/shard_map/keep/pallas_call | solution.py:601
  42.9 0.6 %collective-permute-done.6 = f32[512,128]{1,0:T(8,128)S(1)} collective-permute-done((f32[512,128]{1,0:T(8,128)S(1)}, f32[512,128]{1,0:T(8,128)S(1)}, u32[]{:S(2)}, u32[]{:S(2)}) %collective-permute-start.6) | collective-permute-done | bytes 262176 | tf_op jit(solution)/shard_map/ppermute | solution.py:598
  43.5 0.7 %fill.1 = f32[256,2,2,128]{3,2,1,0:T(2,128)} custom-call(s32[1,1]{1,0:T(1,128)} %bitcast.rank_ref, f32[256,2,128]{2,1,0:T(2,128)S(1)} %bitcast.15, f32[256,2,2,128]{3,2,1,0:T(2,128)} %keep.1.part_hbm), custom_call_target="tpu_custom_call", output_to_operand_aliasing={{}: (2, {})} | custom-call | tf_op jit(solution)/shard_map/fill/pallas_call | solution.py:611
  (4 shorter events, 0.0 us)
Async XLA Ops:
  1.3 21.1 %collective-permute-start = (bf16[784,128]{1,0:T(8,128)(2,1)S(1)}, bf16[784,128]{1,0:T(8,128)(2,1)S(1)}, u32[]{:S(2)}, u32[]{:S(2)}) collective-permute-start(bf16[784,128]{1,0:T(8,128)(2,1)S(1)} %get-tuple-element.35), channel_id=1, source_target_pairs={{0,4},{4,0},{1,5},{5,1},{2,6},{6,2},{3,7},{7,3}} | collective-permute-start | bytes 602120 | tf_op jit(solution)/shard_map/ppermute | solution.py:516
  5.2 17.1 %collective-permute-start.1 = (bf16[784,128]{1,0:T(8,128)(2,1)S(1)}, bf16[784,128]{1,0:T(8,128)(2,1)S(1)}, u32[]{:S(2)}, u32[]{:S(2)}) collective-permute-start(bf16[784,128]{1,0:T(8,128)(2,1)S(1)} %get-tuple-element.35), channel_id=1, source_target_pairs={{8,12},{12,8},{16,20},{20,16},{24,28},{28,24},{32,36},{36,32},{40,... | collective-permute-start | bytes 602120 | tf_op jit(solution)/shard_map/ppermute | solution.py:518
  5.9 19.7 %collective-permute-start.2 = (bf16[784,128]{1,0:T(8,128)(2,1)S(1)}, bf16[784,128]{1,0:T(8,128)(2,1)S(1)}, u32[]{:S(2)}, u32[]{:S(2)}) collective-permute-start(bf16[784,128]{1,0:T(8,128)(2,1)S(1)} %get-tuple-element.37), channel_id=1, source_target_pairs={{0,508},{4,8},{8,4},{12,16},{16,12},{20,24},{24,20},{28,32},{32,28... | collective-permute-start | bytes 602120 | tf_op jit(solution)/shard_map/ppermute | solution.py:517
  25.6 9.3 %copy-start = (bf16[4,256,256]{2,1,0:T(8,128)(2,1)S(1)}, bf16[4,256,256]{2,1,0:T(8,128)(2,1)}, u32[]{:S(2)}) copy-start(bf16[4,256,256]{2,1,0:T(8,128)(2,1)} %map_ref.1) | copy-start | bytes 1572868
  25.8 8.9 %copy-start.1 = (f32[4,256]{1,0:T(4,128)S(1)}, f32[4,256]{1,0:T(4,128)}, u32[]{:S(2)}) copy-start(f32[4,256]{1,0:T(4,128)} %param.16) | copy-start | bytes 12292
  25.8 9.5 %collective-permute-start.3 = (bf16[544,128]{1,0:T(8,128)(2,1)S(1)}, bf16[544,128]{1,0:T(8,128)(2,1)S(1)}, u32[]{:S(2)}, u32[]{:S(2)}) collective-permute-start(bf16[544,128]{1,0:T(8,128)(2,1)S(1)} %get-tuple-element.39), channel_id=1, source_target_pairs={{0,1},{1,0},{2,3},{3,2},{4,5},{5,4},{6,7},{7,6},{8,9},{9,8},{10,11... | collective-permute-start | bytes 417800 | tf_op jit(solution)/shard_map/ppermute | solution.py:566
  29.3 7.1 %collective-permute-start.4 = (bf16[544,128]{1,0:T(8,128)(2,1)S(1)}, bf16[544,128]{1,0:T(8,128)(2,1)S(1)}, u32[]{:S(2)}, u32[]{:S(2)}) collective-permute-start(bf16[544,128]{1,0:T(8,128)(2,1)S(1)} %get-tuple-element.38.block0_ref), channel_id=1, source_target_pairs={{0,2},{1,3},{2,0},{3,1},{4,6},{5,7},{6,4},{7,5},{8,10},{9,11},{10,... | collective-permute-start | bytes 417800 | tf_op jit(solution)/shard_map/ppermute | solution.py:564
  31.6 8.0 %collective-permute-start.5 = (bf16[544,128]{1,0:T(8,128)(2,1)S(1)}, bf16[544,128]{1,0:T(8,128)(2,1)S(1)}, u32[]{:S(2)}, u32[]{:S(2)}) collective-permute-start(bf16[544,128]{1,0:T(8,128)(2,1)S(1)} %get-tuple-element.39), channel_id=1, source_target_pairs={{0,3},{1,2},{2,1},{3,0},{4,7},{5,6},{6,5},{7,4},{8,11},{9,10},{10,... | collective-permute-start | bytes 417800 | tf_op jit(solution)/shard_map/ppermute | solution.py:565
  40.0 3.4 %collective-permute-start.6 = (f32[512,128]{1,0:T(8,128)S(1)}, f32[512,128]{1,0:T(8,128)S(1)}, u32[]{:S(2)}, u32[]{:S(2)}) collective-permute-start(f32[512,128]{1,0:T(8,128)S(1)} %get-tuple-element.43), channel_id=1, source_target_pairs={{0,1},{1,0},{2,3},{3,2},{4,5},{5,4},{6,7},{7,6},{8,9},{9,8},{10,11... | collective-permute-start | bytes 786440 | tf_op jit(solution)/shard_map/ppermute | solution.py:598

commit v5 on v4

--- a/solution.py
+++ b/solution.py
@@ -354,11 +354,14 @@
     tail1_ref,
     tail2_ref,
     tail3_ref,
+    away_ref,
     map_ref,
     last_ref,
     off_ref,
     keep_ref,
     give_ref,
+    spare_ref,
+    flag_ref,
     chem_ref,
 ):
     block_refs = (block0_ref, block1_ref, block2_ref, block3_ref)
@@ -378,7 +381,10 @@
 
     sun = substeps * levels
     lit = row_of(sun) > 0.0
-    any_lit = jnp.max(row_of(sun)) > 0.0
+    suns = jnp.concatenate([t[sun : sun + 1, :] for t in tables], axis=0)
+    any_lit = jnp.max(suns) > 0.0
+    flag_ref[...] = jnp.broadcast_to(jnp.max(suns, axis=(0, 1), keepdims=True), flag_ref.shape).astype(jnp.int32)
+    away = [jnp.where(even, tables[half + k], tables[k]) for k in range(half)]
 
     @pl.when(any_lit)
     def lit_tile():
@@ -412,39 +418,31 @@
                 for k in range(half):
                     chem_ref[level * half + k] = chem[:, k * LANES : (k + 1) * LANES]
 
-    @pl.when(jnp.logical_not(any_lit))
-    def dark_tile():
-        for group in range(levels * half):
-            for p in range(2):
-                rows = slice(p * quarter, (p + 1) * quarter)
-                chem_ref[group, rows, :] = block(p, group).astype(F32)
-
-    chunk = 32
-    for k in range(half):
-        pieces = [
-            columns[k][sun + 1 + i * (levels - 1) : sun + 1 + (i + 1) * (levels - 1), :]
-            for i in range(3)
-        ]
-        mixed = pieces[0] + pieces[1] + pieces[2]
-        mixing = [mixed[i : i + 1, :] for i in range(levels - 1)]
-        inverse, ratio = [], []
-        for level in range(levels):
-            diagonal = 1.0
-            if level > 0:
-                diagonal = diagonal + mixing[level - 1]
-            if level < levels - 1:
-                diagonal = diagonal + mixing[level]
-            if level > 0:
-                diagonal = diagonal - mixing[level - 1] * ratio[level - 1]
-            inverse.append(1.0 / diagonal)
-            if level < levels - 1:
-                ratio.append(mixing[level] * inverse[level])
-        for p, out_ref in enumerate((keep_ref, give_ref)):
+    def solve(columns, source_of, out_ref):
+        chunk = 32
+        for k in range(half):
+            pieces = [
+                columns[k][sun + 1 + i * (levels - 1) : sun + 1 + (i + 1) * (levels - 1), :]
+                for i in range(3)
+            ]
+            mixed = pieces[0] + pieces[1] + pieces[2]
+            mixing = [mixed[i : i + 1, :] for i in range(levels - 1)]
+            inverse, ratio = [], []
+            for level in range(levels):
+                diagonal = 1.0
+                if level > 0:
+                    diagonal = diagonal + mixing[level - 1]
+                if level < levels - 1:
+                    diagonal = diagonal + mixing[level]
+                if level > 0:
+                    diagonal = diagonal - mixing[level - 1] * ratio[level - 1]
+                inverse.append(1.0 / diagonal)
+                if level < levels - 1:
+                    ratio.append(mixing[level] * inverse[level])
             for begin in range(0, quarter, chunk):
                 solved = []
                 for level in range(levels):
-                    rows = slice(p * quarter + begin, p * quarter + begin + chunk)
-                    value = chem_ref[level * half + k, rows, :]
+                    value = source_of(level * half + k, begin, chunk)
                     if level > 0:
                         value = value + mixing[level - 1] * solved[-1]
                     solved.append(value * inverse[level])
@@ -454,6 +452,31 @@
                     place = begin * levels * half + level * half + k
                     out_ref[pl.ds(place, chunk, stride=levels * half), :] = solved[level]
 
+    @pl.when(any_lit)
+    def lit_mixing():
+        for p, out_ref in enumerate((keep_ref, give_ref)):
+            solve(
+                columns,
+                lambda g, begin, chunk: chem_ref[
+                    g, p * quarter + begin : p * quarter + begin + chunk, :
+                ],
+                out_ref,
+            )
+
+    @pl.when(jnp.logical_not(any_lit))
+    def dark_mixing():
+        for tabs, ref, out_ref in (
+            (columns, block0_ref, keep_ref),
+            (away, away_ref, spare_ref),
+        ):
+            solve(
+                tabs,
+                lambda g, begin, chunk: ref[
+                    g * quarter + begin : g * quarter + begin + chunk, :
+                ].astype(F32),
+                out_ref,
+            )
+
 
 def keep_kernel(rank_ref, keep_ref, out_hbm, sem):
     copy = pltpu.make_async_copy(keep_ref, out_hbm.at[:, rank_ref[0, 0] & 1], sem)
@@ -466,6 +489,18 @@
     copy = pltpu.make_async_copy(got_ref, out_hbm.at[:, 1 - (rank_ref[0, 0] & 1)], sem)
     copy.start()
     copy.wait()
+
+
+def both_kernel(rank_ref, keep_ref, spare_ref, out_hbm, sems):
+    core = rank_ref[0, 0] & 1
+    copies = [
+        pltpu.make_async_copy(keep_ref, out_hbm.at[:, core], sems.at[0]),
+        pltpu.make_async_copy(spare_ref, out_hbm.at[:, 1 - core], sems.at[1]),
+    ]
+    for copy in copies:
+        copy.start()
+    for copy in copies:
+        copy.wait()
 
 
 def shards(
@@ -579,11 +614,11 @@
         name="maps",
     )(rank, linear_maps, offsets.T.reshape(parts, quarter, entries))
     blocks = [mine, first, second, third]
-    keep, give = pl.pallas_call(
+    keep, give, spare, flag = pl.pallas_call(
         functools.partial(chem_kernel, levels, width, quarter, entries, substeps),
-        out_shape=(shape((rows, length), F32),) * 2,
-        in_specs=[smem()] + [vmem()] * 11,
-        out_specs=(vmem(),) * 2,
+        out_shape=(shape((rows, length), F32),) * 3 + (shape((8, length), jnp.int32),),
+        in_specs=[smem()] + [vmem()] * 12,
+        out_specs=(vmem(),) * 4,
         scratch_shapes=[pltpu.VMEM((grid // 2, 2 * quarter, length), F32)],
         compiler_params=params(24),
         name="chem",
@@ -591,33 +626,49 @@
         rank,
         *blocks,
         *[b[rows:] for b in blocks],
+        other,
         full.reshape(entries * species, species),
         last.reshape(2 * entries * quarter, species),
         shift.reshape(species, entries),
     )
-    got = lax.ppermute(give, "trc", swap[1])
     pair = (quarter * levels, width // 2, length)
     whole = shape((quarter * levels, 2, width // 2, length), F32)
-    part = pl.pallas_call(
-        keep_kernel,
-        out_shape=whole,
-        in_specs=[smem(), vmem()],
-        out_specs=hbm(),
-        scratch_shapes=[pltpu.SemaphoreType.DMA],
-        compiler_params=params(4),
-        cost_estimate=pl.CostEstimate(flops=1000000, bytes_accessed=1 << 19, transcendentals=0),
-        name="keep",
-    )(rank, keep.reshape(pair))
-    out = pl.pallas_call(
-        fill_kernel,
-        out_shape=whole,
-        in_specs=[smem(), vmem(), hbm()],
-        out_specs=hbm(),
-        scratch_shapes=[pltpu.SemaphoreType.DMA],
-        input_output_aliases={2: 0},
-        compiler_params=params(4),
-        name="fill",
-    )(rank, got.reshape(pair), part)
+
+    def lit_end(rank, keep, give, spare):
+        got = lax.ppermute(give, "trc", swap[1])
+        part = pl.pallas_call(
+            keep_kernel,
+            out_shape=whole,
+            in_specs=[smem(), vmem()],
+            out_specs=hbm(),
+            scratch_shapes=[pltpu.SemaphoreType.DMA],
+            compiler_params=params(4),
+            cost_estimate=pl.CostEstimate(flops=1000000, bytes_accessed=1 << 19, transcendentals=0),
+            name="keep",
+        )(rank, keep.reshape(pair))
+        return pl.pallas_call(
+            fill_kernel,
+            out_shape=whole,
+            in_specs=[smem(), vmem(), hbm()],
+            out_specs=hbm(),
+            scratch_shapes=[pltpu.SemaphoreType.DMA],
+            input_output_aliases={2: 0},
+            compiler_params=params(4),
+            name="fill",
+        )(rank, got.reshape(pair), part)
+
+    def dark_end(rank, keep, give, spare):
+        return pl.pallas_call(
+            both_kernel,
+            out_shape=whole,
+            in_specs=[smem(), vmem(), vmem()],
+            out_specs=hbm(),
+            scratch_shapes=[pltpu.SemaphoreType.DMA((2,))],
+            compiler_params=params(4),
+            name="both",
+        )(rank, keep.reshape(pair), spare.reshape(pair))
+
+    out = lax.switch(flag[0, 0], (dark_end, lit_end), rank, keep, give, spare)
     return out.reshape(quarter, levels, width, length)
 
 

time: 44.5 us -> 42.3 us (0.951)
  starting transfers between devices: 30.9 us -> 28.8 us
  between operations: 0.19 us -> 0.82 us
  Pallas kernels: 4.99 us -> 4.37 us
  waiting for transfers between devices: 7.68 us -> 7.11 us
  local copies, waits for them, and re-layouts: 0.4 us -> 0.91 us
    ppermute x1 -> x0, starting transfers between devices: 2.12 us -> none  [shards(): got = lax.ppermute(give, 'trc', swap[1])]
    pallas_call x2 -> x1, Pallas kernels: 1.43 us -> 0.81 us  [dark_end(): pl.pallas_call(both_kernel, out_shape=whole, in_specs=[smem(), vmem(), vm...]
    ppermute x1 -> x0, waiting for transfers between devices: 0.58 us -> none  [shards(): got = lax.ppermute(give, 'trc', swap[1])]
    slice x0 -> x1, local copies, waits for them, and re-layouts: none -> 0.51 us  [shards(): out = lax.switch(flag[0, 0], (dark_end, lit_end), rank, keep, give, spare)]
  transfers between devices with their start and end apart: 7 -> 6, of which waited for: 4 -> 3; matrix products, arithmetic and copies ran while one was open for 1% -> 1% of each run, Pallas kernels for 5% -> 4%
where the time goes in v5:
time: 42.3 us; the launch traced here: 42 us
  starting transfers between devices  28.8 us (68%)
  waiting for transfers between devices  7.11 us (17%)
  Pallas kernels  4.37 us (10%)
  local copies, waits for them, and re-layouts  0.91 us (2%)
  between operations  0.82 us (2%)
    ppermute x1, starting transfers between devices, shards(): from_b = lax.ppermute(to_b, 'tile', seams)  15.3 us
    ppermute x1, starting transfers between devices, shards(): from_a0 = lax.ppermute(to_a, 'tile', pairs[:2])  3.94 us
    ppermute x1, starting transfers between devices, shards(): first = lax.ppermute(other, 'trc', swap[1])  3.43 us
    ppermute x1, waiting for transfers between devices, shards(): third = lax.ppermute(other, 'trc', swap[3])  3.16 us
    ppermute x1, starting transfers between devices, shards(): third = lax.ppermute(other, 'trc', swap[3])  3.15 us
    ppermute x1, waiting for transfers between devices, shards(): from_b = lax.ppermute(to_b, 'tile', seams)  2.86 us
    ppermute x1, starting transfers between devices, shards(): second = lax.ppermute(mine, 'trc', swap[2])  2.31 us
    pallas_call x1, Pallas kernels, shards(): pl.pallas_call(functools.partial(pack_kernel, levels, width, quarter, pie...  1.25 us
  transfers between devices with their start and end apart: 6, of which 3 were waited for; matrix products, arithmetic and copies ran while one was open for 1% of the time, Pallas kernels for 4%

profile of v5, /device:TPU:1, one launch (start us, length us, event | category | flops | bytes accessed | tf_op | source)
XLA Modules:
  0.0 42.0 jit_solution(12435334120361639355)
XLA Ops:
  0.0 1.2 %pack.1 = (bf16[784,128]{1,0:T(8,128)(2,1)S(1)}, bf16[784,128]{1,0:T(8,128)(2,1)S(1)}, f32[1024,128]{1,0:T(8,128)S(1)}, f32[16,128]{1,0:T(8,128)S(1)}, f32[16,12...) custom-call(s32[1,1]{1,0:T(1,128)} %bitcast.7.refs_0_.tile_ref, ...), custom_call_target="tpu_custom_call" | custom-call | tf_op jit(solution)/shard_map/pack/pallas_call | solution.py:538
  1.3 3.9 %collective-permute-start.1 = (bf16[784,128]{1,0:T(8,128)(2,1)S(1)}, bf16[784,128]{1,0:T(8,128)(2,1)S(1)}, u32[]{:S(2)}, u32[]{:S(2)}) collective-permute-start(bf16[784,128]{1,0:T(8,128)(2,1)S(1)} %get-tuple-element.59), channel_id=1, source_target_pairs={{0,4},{4,0},{1,5},{5,1},{2,6},{6,2},{3,7},{7,3}} | collective-permute-start | bytes 602120 | tf_op jit(solution)/shard_map/ppermute | solution.py:551
  5.2 0.7 %collective-permute-start.2 = (bf16[784,128]{1,0:T(8,128)(2,1)S(1)}, bf16[784,128]{1,0:T(8,128)(2,1)S(1)}, u32[]{:S(2)}, u32[]{:S(2)}) collective-permute-start(bf16[784,128]{1,0:T(8,128)(2,1)S(1)} %get-tuple-element.59), channel_id=1, source_target_pairs={{8,12},{12,8},{16,20},{20,16},{24,28},{28,24},{32,36},{36,32},{40,... | collective-permute-start | bytes 602120 | tf_op jit(solution)/shard_map/ppermute | solution.py:553
  5.9 15.3 %collective-permute-start.3 = (bf16[784,128]{1,0:T(8,128)(2,1)S(1)}, bf16[784,128]{1,0:T(8,128)(2,1)S(1)}, u32[]{:S(2)}, u32[]{:S(2)}) collective-permute-start(bf16[784,128]{1,0:T(8,128)(2,1)S(1)} %get-tuple-element.61), channel_id=1, source_target_pairs={{0,508},{4,8},{8,4},{12,16},{16,12},{20,24},{24,20},{28,32},{32,28... | collective-permute-start | bytes 602120 | tf_op jit(solution)/shard_map/ppermute | solution.py:552
  21.2 0.1 reshape.63.entry_ref
  21.3 0.1 reshape.65.mix_ref
  21.3 0.1 reshape.64.sun_ref
  21.4 0.9 %local.1 = (f32[16,64,128]{2,1,0:T(8,128)S(1)}, f32[7,16,128]{2,1,0:T(8,128)S(1)}, bf16[32,128]{1,0:T(8,128)(2,1)S(1)}, bf16[2,128,128]{2,1,0:T(8,128)(2,1)S(1)}) custom-call(s32[1,2]{1,0:T(1,128)S(1)} %get-tuple-element.50.flag_ref, f32[1024,128]{1,0:T(8,128)S(1)} %get-tuple-element.49.x_ref, f32[16,128]{1,0:T(8,128)S(1)} %get-tuple-element.51.cycle_ref, ...), custom_call_target="tpu_custom_call" | custom-call | flops 4000000 | bytes 1048576 | tf_op jit(solution)/shard_map/local/pallas_call | solution.py:555
  22.3 0.0 collective-permute-done.1.a0_ref
  22.3 0.0 collective-permute-done.2.a1_ref
  22.4 0.3 near.1.near_ref
  22.7 2.9 %collective-permute-done.3.b_ref = bf16[784,128]{1,0:T(8,128)(2,1)S(1)} collective-permute-done((bf16[784,128]{1,0:T(8,128)(2,1)S(1)}, bf16[784,128]{1,0:T(8,128)(2,1)S(1)}, u32[]{:S(2)}, u32[]{:S(2)}) %collective-permute-start.3) | collective-permute-done | bytes 200736 | tf_op jit(solution)/shard_map/ppermute | solution.py:552
  25.6 0.0 copy-start
  25.6 0.2 flow.1
  25.8 0.0 copy-start.1
  25.8 3.4 %collective-permute-start.4 = (bf16[544,128]{1,0:T(8,128)(2,1)S(1)}, bf16[544,128]{1,0:T(8,128)(2,1)S(1)}, u32[]{:S(2)}, u32[]{:S(2)}) collective-permute-start(bf16[544,128]{1,0:T(8,128)(2,1)S(1)} %get-tuple-element.63.away_ref), channel_id=1, source_target_pairs={{0,1},{1,0},{2,3},{3,2},{4,5},{5,4},{6,7},{7,6},{8,9},{9,8},{10,11... | collective-permute-start | bytes 417800 | tf_op jit(solution)/shard_map/ppermute | solution.py:601
  29.3 2.3 %collective-permute-start.5 = (bf16[544,128]{1,0:T(8,128)(2,1)S(1)}, bf16[544,128]{1,0:T(8,128)(2,1)S(1)}, u32[]{:S(2)}, u32[]{:S(2)}) collective-permute-start(bf16[544,128]{1,0:T(8,128)(2,1)S(1)} %get-tuple-element.62.block0_ref), channel_id=1, source_target_pairs={{0,2},{1,3},{2,0},{3,1},{4,6},{5,7},{6,4},{7,5},{8,10},{9,11},{10,... | collective-permute-start | bytes 417800 | tf_op jit(solution)/shard_map/ppermute | solution.py:599
  31.6 3.2 %collective-permute-start.6 = (bf16[544,128]{1,0:T(8,128)(2,1)S(1)}, bf16[544,128]{1,0:T(8,128)(2,1)S(1)}, u32[]{:S(2)}, u32[]{:S(2)}) collective-permute-start(bf16[544,128]{1,0:T(8,128)(2,1)S(1)} %get-tuple-element.63.away_ref), channel_id=1, source_target_pairs={{0,3},{1,2},{2,1},{3,0},{4,7},{5,6},{6,5},{7,4},{8,11},{9,10},{10,... | collective-permute-start | bytes 417800 | tf_op jit(solution)/shard_map/ppermute | solution.py:600
  34.8 0.0 copy-done.1
  34.8 0.1 copy.13
  34.9 0.0 copy-done
  34.9 0.4 maps.1
  35.3 0.0 collective-permute-done.4.block1_ref
  35.3 1.1 %collective-permute-done.5.block2_ref = bf16[544,128]{1,0:T(8,128)(2,1)S(1)} collective-permute-done((bf16[544,128]{1,0:T(8,128)(2,1)S(1)}, bf16[544,128]{1,0:T(8,128)(2,1)S(1)}, u32[]{:S(2)}, u32[]{:S(2)}) %collective-permute-start.5) | collective-permute-done | bytes 139296 | tf_op jit(solution)/shard_map/ppermute | solution.py:599
  36.4 3.2 %collective-permute-done.6.block3_ref = bf16[544,128]{1,0:T(8,128)(2,1)S(1)} collective-permute-done((bf16[544,128]{1,0:T(8,128)(2,1)S(1)}, bf16[544,128]{1,0:T(8,128)(2,1)S(1)}, u32[]{:S(2)}, u32[]{:S(2)}) %collective-permute-start.6) | collective-permute-done | bytes 139296 | tf_op jit(solution)/shard_map/ppermute | solution.py:600
  39.6 0.5 %chem.1 = (f32[512,128]{1,0:T(8,128)S(1)}, f32[512,128]{1,0:T(8,128)S(1)}, f32[512,128]{1,0:T(8,128)S(1)}, s32[8,128]{1,0:T(8,128)S(1)}) custom-call(s32[1,1]{1,0:T(1,128)} %bitcast.6.rank_ref, bf16[544,128]{1,0:T(8,128)(2,1)S(1)} %get-tuple-element.62.block0_ref, bf16[544,128]{1,0:T(8,128)(2,1)S(1)} %collective-permute-done.4.block1_ref, ...), custom_call_target="tpu_custom_call" | custom-call | tf_op jit(solution)/shard_map/chem/pallas_call | solution.py:617
  40.0 0.5 %slice.19 = s32[1,1]{1,0:T(1,128)} slice(s32[8,128]{1,0:T(8,128)S(1)} %get-tuple-element.67), slice={[0:1], [0:1]} | slice | bytes 8 | tf_op jit(solution)/shard_map/slice | solution.py:671
  41.2 0.8 %conditional.1 = (f32[64,4,4,128]{3,2,1,0:T(4,128)}) conditional(s32[]{:T(128)} %bitcast.16, (f32[512,128]{1,0:T(8,128)S(1)}, f32[512,128]{1,0:T(8,128)S(1)}, s32[1,1]{1,0:T(1,128)}) %tuple.13, (f32[512,128]{1,0:T(8,128)S(1)}, f32[512,128]{1,0:T(8,128)S(1)}, s32[1,1]{1,0:T(1,128)}) %tuple.14), branch_computations={%region_0.0_spmd, %region_1.0_spmd} | conditional | flops 1000000 | bytes 1572912 | solution.py:671
  41.2 0.8 %both.1 = f32[256,2,2,128]{3,2,1,0:T(2,128)} custom-call(s32[1,1]{1,0:T(1,128)} %get-tuple-element.21.rank_ref, f32[256,2,128]{2,1,0:T(2,128)S(1)} %bitcast.22, f32[256,2,128]{2,1,0:T(2,128)S(1)} %bitcast.25), custom_call_target="tpu_custom_call" | custom-call | tf_op jit(solution)/shard_map/cond/branch_0_fun/both/pallas_call | solution.py:661
  (4 shorter events, 0.0 us)
Async XLA Ops:
  1.3 21.1 %collective-permute-start.1 = (bf16[784,128]{1,0:T(8,128)(2,1)S(1)}, bf16[784,128]{1,0:T(8,128)(2,1)S(1)}, u32[]{:S(2)}, u32[]{:S(2)}) collective-permute-start(bf16[784,128]{1,0:T(8,128)(2,1)S(1)} %get-tuple-element.59), channel_id=1, source_target_pairs={{0,4},{4,0},{1,5},{5,1},{2,6},{6,2},{3,7},{7,3}} | collective-permute-start | bytes 602120 | tf_op jit(solution)/shard_map/ppermute | solution.py:551
  5.2 17.1 %collective-permute-start.2 = (bf16[784,128]{1,0:T(8,128)(2,1)S(1)}, bf16[784,128]{1,0:T(8,128)(2,1)S(1)}, u32[]{:S(2)}, u32[]{:S(2)}) collective-permute-start(bf16[784,128]{1,0:T(8,128)(2,1)S(1)} %get-tuple-element.59), channel_id=1, source_target_pairs={{8,12},{12,8},{16,20},{20,16},{24,28},{28,24},{32,36},{36,32},{40,... | collective-permute-start | bytes 602120 | tf_op jit(solution)/shard_map/ppermute | solution.py:553
  5.9 19.7 %collective-permute-start.3 = (bf16[784,128]{1,0:T(8,128)(2,1)S(1)}, bf16[784,128]{1,0:T(8,128)(2,1)S(1)}, u32[]{:S(2)}, u32[]{:S(2)}) collective-permute-start(bf16[784,128]{1,0:T(8,128)(2,1)S(1)} %get-tuple-element.61), channel_id=1, source_target_pairs={{0,508},{4,8},{8,4},{12,16},{16,12},{20,24},{24,20},{28,32},{32,28... | collective-permute-start | bytes 602120 | tf_op jit(solution)/shard_map/ppermute | solution.py:552
  25.6 9.3 %copy-start = (bf16[4,256,256]{2,1,0:T(8,128)(2,1)S(1)}, bf16[4,256,256]{2,1,0:T(8,128)(2,1)}, u32[]{:S(2)}) copy-start(bf16[4,256,256]{2,1,0:T(8,128)(2,1)} %map_ref.1) | copy-start | bytes 1572868
  25.8 8.9 %copy-start.1 = (f32[4,256]{1,0:T(4,128)S(1)}, f32[4,256]{1,0:T(4,128)}, u32[]{:S(2)}) copy-start(f32[4,256]{1,0:T(4,128)} %param.18) | copy-start | bytes 12292
  25.8 9.5 %collective-permute-start.4 = (bf16[544,128]{1,0:T(8,128)(2,1)S(1)}, bf16[544,128]{1,0:T(8,128)(2,1)S(1)}, u32[]{:S(2)}, u32[]{:S(2)}) collective-permute-start(bf16[544,128]{1,0:T(8,128)(2,1)S(1)} %get-tuple-element.63.away_ref), channel_id=1, source_target_pairs={{0,1},{1,0},{2,3},{3,2},{4,5},{5,4},{6,7},{7,6},{8,9},{9,8},{10,11... | collective-permute-start | bytes 417800 | tf_op jit(solution)/shard_map/ppermute | solution.py:601
  29.3 7.1 %collective-permute-start.5 = (bf16[544,128]{1,0:T(8,128)(2,1)S(1)}, bf16[544,128]{1,0:T(8,128)(2,1)S(1)}, u32[]{:S(2)}, u32[]{:S(2)}) collective-permute-start(bf16[544,128]{1,0:T(8,128)(2,1)S(1)} %get-tuple-element.62.block0_ref), channel_id=1, source_target_pairs={{0,2},{1,3},{2,0},{3,1},{4,6},{5,7},{6,4},{7,5},{8,10},{9,11},{10,... | collective-permute-start | bytes 417800 | tf_op jit(solution)/shard_map/ppermute | solution.py:599
  31.6 8.0 %collective-permute-start.6 = (bf16[544,128]{1,0:T(8,128)(2,1)S(1)}, bf16[544,128]{1,0:T(8,128)(2,1)S(1)}, u32[]{:S(2)}, u32[]{:S(2)}) collective-permute-start(bf16[544,128]{1,0:T(8,128)(2,1)S(1)} %get-tuple-element.63.away_ref), channel_id=1, source_target_pairs={{0,3},{1,2},{2,1},{3,0},{4,7},{5,6},{6,5},{7,4},{8,11},{9,10},{10,... | collective-permute-start | bytes 417800 | tf_op jit(solution)/shard_map/ppermute | solution.py:600

commit v6 on v4

--- a/solution.py
+++ b/solution.py
@@ -412,39 +412,31 @@
                 for k in range(half):
                     chem_ref[level * half + k] = chem[:, k * LANES : (k + 1) * LANES]
 
-    @pl.when(jnp.logical_not(any_lit))
-    def dark_tile():
-        for group in range(levels * half):
-            for p in range(2):
-                rows = slice(p * quarter, (p + 1) * quarter)
-                chem_ref[group, rows, :] = block(p, group).astype(F32)
-
-    chunk = 32
-    for k in range(half):
-        pieces = [
-            columns[k][sun + 1 + i * (levels - 1) : sun + 1 + (i + 1) * (levels - 1), :]
-            for i in range(3)
-        ]
-        mixed = pieces[0] + pieces[1] + pieces[2]
-        mixing = [mixed[i : i + 1, :] for i in range(levels - 1)]
-        inverse, ratio = [], []
-        for level in range(levels):
-            diagonal = 1.0
-            if level > 0:
-                diagonal = diagonal + mixing[level - 1]
-            if level < levels - 1:
-                diagonal = diagonal + mixing[level]
-            if level > 0:
-                diagonal = diagonal - mixing[level - 1] * ratio[level - 1]
-            inverse.append(1.0 / diagonal)
-            if level < levels - 1:
-                ratio.append(mixing[level] * inverse[level])
-        for p, out_ref in enumerate((keep_ref, give_ref)):
+    def solve(columns, source_of, out_ref):
+        chunk = 32
+        for k in range(half):
+            pieces = [
+                columns[k][sun + 1 + i * (levels - 1) : sun + 1 + (i + 1) * (levels - 1), :]
+                for i in range(3)
+            ]
+            mixed = pieces[0] + pieces[1] + pieces[2]
+            mixing = [mixed[i : i + 1, :] for i in range(levels - 1)]
+            inverse, ratio = [], []
+            for level in range(levels):
+                diagonal = 1.0
+                if level > 0:
+                    diagonal = diagonal + mixing[level - 1]
+                if level < levels - 1:
+                    diagonal = diagonal + mixing[level]
+                if level > 0:
+                    diagonal = diagonal - mixing[level - 1] * ratio[level - 1]
+                inverse.append(1.0 / diagonal)
+                if level < levels - 1:
+                    ratio.append(mixing[level] * inverse[level])
             for begin in range(0, quarter, chunk):
                 solved = []
                 for level in range(levels):
-                    rows = slice(p * quarter + begin, p * quarter + begin + chunk)
-                    value = chem_ref[level * half + k, rows, :]
+                    value = source_of(level * half + k, begin, chunk)
                     if level > 0:
                         value = value + mixing[level - 1] * solved[-1]
                     solved.append(value * inverse[level])
@@ -453,6 +445,28 @@
                 for level in range(levels):
                     place = begin * levels * half + level * half + k
                     out_ref[pl.ds(place, chunk, stride=levels * half), :] = solved[level]
+
+    @pl.when(any_lit)
+    def lit_mixing():
+        for p, out_ref in enumerate((keep_ref, give_ref)):
+            solve(
+                columns,
+                lambda g, begin, chunk: chem_ref[
+                    g, p * quarter + begin : p * quarter + begin + chunk, :
+                ],
+                out_ref,
+            )
+
+    @pl.when(jnp.logical_not(any_lit))
+    def dark_mixing():
+        for ref, out_ref in ((block0_ref, keep_ref), (block1_ref, give_ref)):
+            solve(
+                columns,
+                lambda g, begin, chunk: ref[
+                    g * quarter + begin : g * quarter + begin + chunk, :
+                ].astype(F32),
+                out_ref,
+            )
 
 
 def keep_kernel(rank_ref, keep_ref, out_hbm, sem):

time: 44.5 us -> 44.5 us (level)
  no operation moved by 1% of the time
where the time goes in v6:
time: 44.5 us; the launch traced here: 44.1 us
  starting transfers between devices  30.9 us (69%)
  waiting for transfers between devices  7.68 us (17%)
  Pallas kernels  4.95 us (11%)
    ppermute x1, starting transfers between devices, shards(): from_b = lax.ppermute(to_b, 'tile', seams)  15.3 us
    ppermute x1, starting transfers between devices, shards(): from_a0 = lax.ppermute(to_a, 'tile', pairs[:2])  3.94 us
    ppermute x1, starting transfers between devices, shards(): first = lax.ppermute(other, 'trc', swap[1])  3.43 us
    ppermute x1, waiting for transfers between devices, shards(): third = lax.ppermute(other, 'trc', swap[3])  3.16 us
    ppermute x1, starting transfers between devices, shards(): third = lax.ppermute(other, 'trc', swap[3])  3.15 us
    ppermute x1, waiting for transfers between devices, shards(): from_b = lax.ppermute(to_b, 'tile', seams)  2.86 us
    ppermute x1, starting transfers between devices, shards(): second = lax.ppermute(mine, 'trc', swap[2])  2.31 us
    ppermute x1, starting transfers between devices, shards(): got = lax.ppermute(give, 'trc', swap[1])  2.12 us
  transfers between devices with their start and end apart: 7, of which 4 were waited for; matrix products, arithmetic and copies ran while one was open for 1% of the time, Pallas kernels for 5%

profile of v6, /device:TPU:1, one launch (start us, length us, event | category | flops | bytes accessed | tf_op | source)
XLA Modules:
  0.0 44.1 jit_solution(8750799074686949827)
XLA Ops:
  0.0 1.2 %pack.1 = (bf16[784,128]{1,0:T(8,128)(2,1)S(1)}, bf16[784,128]{1,0:T(8,128)(2,1)S(1)}, f32[1024,128]{1,0:T(8,128)S(1)}, f32[16,128]{1,0:T(8,128)S(1)}, f32[16,12...) custom-call(s32[1,1]{1,0:T(1,128)} %bitcast.1.refs_0_.tile_ref, ...), custom_call_target="tpu_custom_call" | custom-call | tf_op jit(solution)/shard_map/pack/pallas_call | solution.py:517
  1.3 3.9 %collective-permute-start = (bf16[784,128]{1,0:T(8,128)(2,1)S(1)}, bf16[784,128]{1,0:T(8,128)(2,1)S(1)}, u32[]{:S(2)}, u32[]{:S(2)}) collective-permute-start(bf16[784,128]{1,0:T(8,128)(2,1)S(1)} %get-tuple-element.35), channel_id=1, source_target_pairs={{0,4},{4,0},{1,5},{5,1},{2,6},{6,2},{3,7},{7,3}} | collective-permute-start | bytes 602120 | tf_op jit(solution)/shard_map/ppermute | solution.py:530
  5.2 0.7 %collective-permute-start.1 = (bf16[784,128]{1,0:T(8,128)(2,1)S(1)}, bf16[784,128]{1,0:T(8,128)(2,1)S(1)}, u32[]{:S(2)}, u32[]{:S(2)}) collective-permute-start(bf16[784,128]{1,0:T(8,128)(2,1)S(1)} %get-tuple-element.35), channel_id=1, source_target_pairs={{8,12},{12,8},{16,20},{20,16},{24,28},{28,24},{32,36},{36,32},{40,... | collective-permute-start | bytes 602120 | tf_op jit(solution)/shard_map/ppermute | solution.py:532
  5.9 15.3 %collective-permute-start.2 = (bf16[784,128]{1,0:T(8,128)(2,1)S(1)}, bf16[784,128]{1,0:T(8,128)(2,1)S(1)}, u32[]{:S(2)}, u32[]{:S(2)}) collective-permute-start(bf16[784,128]{1,0:T(8,128)(2,1)S(1)} %get-tuple-element.37), channel_id=1, source_target_pairs={{0,508},{4,8},{8,4},{12,16},{16,12},{20,24},{24,20},{28,32},{32,28... | collective-permute-start | bytes 602120 | tf_op jit(solution)/shard_map/ppermute | solution.py:531
  21.2 0.1 reshape.50.entry_ref
  21.3 0.1 reshape.52.mix_ref
  21.3 0.1 reshape.51.sun_ref
  21.4 0.9 %local.1 = (f32[16,64,128]{2,1,0:T(8,128)S(1)}, f32[7,16,128]{2,1,0:T(8,128)S(1)}, bf16[32,128]{1,0:T(8,128)(2,1)S(1)}, bf16[2,128,128]{2,1,0:T(8,128)(2,1)S(1)}) custom-call(s32[1,2]{1,0:T(1,128)S(1)} %get-tuple-element.26.flag_ref, f32[1024,128]{1,0:T(8,128)S(1)} %get-tuple-element.25.x_ref, f32[16,128]{1,0:T(8,128)S(1)} %get-tuple-element.27.cycle_ref, ...), custom_call_target="tpu_custom_call" | custom-call | flops 4000000 | bytes 1048576 | tf_op jit(solution)/shard_map/local/pallas_call | solution.py:534
  22.3 0.0 collective-permute-done.a0_ref
  22.3 0.0 collective-permute-done.1.a1_ref
  22.4 0.3 near.1.near_ref
  22.7 2.9 %collective-permute-done.2.b_ref = bf16[784,128]{1,0:T(8,128)(2,1)S(1)} collective-permute-done((bf16[784,128]{1,0:T(8,128)(2,1)S(1)}, bf16[784,128]{1,0:T(8,128)(2,1)S(1)}, u32[]{:S(2)}, u32[]{:S(2)}) %collective-permute-start.2) | collective-permute-done | bytes 200736 | tf_op jit(solution)/shard_map/ppermute | solution.py:531
  25.6 0.0 copy-start
  25.6 0.2 flow.1
  25.8 0.0 copy-start.1
  25.8 3.4 %collective-permute-start.3 = (bf16[544,128]{1,0:T(8,128)(2,1)S(1)}, bf16[544,128]{1,0:T(8,128)(2,1)S(1)}, u32[]{:S(2)}, u32[]{:S(2)}) collective-permute-start(bf16[544,128]{1,0:T(8,128)(2,1)S(1)} %get-tuple-element.39), channel_id=1, source_target_pairs={{0,1},{1,0},{2,3},{3,2},{4,5},{5,4},{6,7},{7,6},{8,9},{9,8},{10,11... | collective-permute-start | bytes 417800 | tf_op jit(solution)/shard_map/ppermute | solution.py:580
  29.3 2.3 %collective-permute-start.4 = (bf16[544,128]{1,0:T(8,128)(2,1)S(1)}, bf16[544,128]{1,0:T(8,128)(2,1)S(1)}, u32[]{:S(2)}, u32[]{:S(2)}) collective-permute-start(bf16[544,128]{1,0:T(8,128)(2,1)S(1)} %get-tuple-element.38.block0_ref), channel_id=1, source_target_pairs={{0,2},{1,3},{2,0},{3,1},{4,6},{5,7},{6,4},{7,5},{8,10},{9,11},{10,... | collective-permute-start | bytes 417800 | tf_op jit(solution)/shard_map/ppermute | solution.py:578
  31.6 3.2 %collective-permute-start.5 = (bf16[544,128]{1,0:T(8,128)(2,1)S(1)}, bf16[544,128]{1,0:T(8,128)(2,1)S(1)}, u32[]{:S(2)}, u32[]{:S(2)}) collective-permute-start(bf16[544,128]{1,0:T(8,128)(2,1)S(1)} %get-tuple-element.39), channel_id=1, source_target_pairs={{0,3},{1,2},{2,1},{3,0},{4,7},{5,6},{6,5},{7,4},{8,11},{9,10},{10,... | collective-permute-start | bytes 417800 | tf_op jit(solution)/shard_map/ppermute | solution.py:579
  34.8 0.0 copy-done.1
  34.8 0.1 copy.11
  34.9 0.0 copy-done
  34.9 0.4 maps.1
  35.3 0.0 collective-permute-done.3.block1_ref
  35.3 1.1 %collective-permute-done.4.block2_ref = bf16[544,128]{1,0:T(8,128)(2,1)S(1)} collective-permute-done((bf16[544,128]{1,0:T(8,128)(2,1)S(1)}, bf16[544,128]{1,0:T(8,128)(2,1)S(1)}, u32[]{:S(2)}, u32[]{:S(2)}) %collective-permute-start.4) | collective-permute-done | bytes 139296 | tf_op jit(solution)/shard_map/ppermute | solution.py:578
  36.4 3.2 %collective-permute-done.5.block3_ref = bf16[544,128]{1,0:T(8,128)(2,1)S(1)} collective-permute-done((bf16[544,128]{1,0:T(8,128)(2,1)S(1)}, bf16[544,128]{1,0:T(8,128)(2,1)S(1)}, u32[]{:S(2)}, u32[]{:S(2)}) %collective-permute-start.5) | collective-permute-done | bytes 139296 | tf_op jit(solution)/shard_map/ppermute | solution.py:579
  39.6 0.4 chem.1
  40.0 2.1 %collective-permute-start.6 = (f32[512,128]{1,0:T(8,128)S(1)}, f32[512,128]{1,0:T(8,128)S(1)}, u32[]{:S(2)}, u32[]{:S(2)}) collective-permute-start(f32[512,128]{1,0:T(8,128)S(1)} %get-tuple-element.43), channel_id=1, source_target_pairs={{0,1},{1,0},{2,3},{3,2},{4,5},{5,4},{6,7},{7,6},{8,9},{9,8},{10,11... | collective-permute-start | bytes 786440 | tf_op jit(solution)/shard_map/ppermute | solution.py:612
  42.1 0.7 %keep.1.part_hbm = f32[256,2,2,128]{3,2,1,0:T(2,128)} custom-call(s32[1,1]{1,0:T(1,128)} %bitcast.rank_ref, f32[256,2,128]{2,1,0:T(2,128)S(1)} %bitcast.17), custom_call_target="tpu_custom_call" | custom-call | flops 1000000 | bytes 524288 | tf_op jit(solution)/shard_map/keep/pallas_call | solution.py:615
  42.8 0.6 %collective-permute-done.6 = f32[512,128]{1,0:T(8,128)S(1)} collective-permute-done((f32[512,128]{1,0:T(8,128)S(1)}, f32[512,128]{1,0:T(8,128)S(1)}, u32[]{:S(2)}, u32[]{:S(2)}) %collective-permute-start.6) | collective-permute-done | bytes 262176 | tf_op jit(solution)/shard_map/ppermute | solution.py:612
  43.4 0.7 %fill.1 = f32[256,2,2,128]{3,2,1,0:T(2,128)} custom-call(s32[1,1]{1,0:T(1,128)} %bitcast.rank_ref, f32[256,2,128]{2,1,0:T(2,128)S(1)} %bitcast.15, f32[256,2,2,128]{3,2,1,0:T(2,128)} %keep.1.part_hbm), custom_call_target="tpu_custom_call", output_to_operand_aliasing={{}: (2, {})} | custom-call | tf_op jit(solution)/shard_map/fill/pallas_call | solution.py:625
  (4 shorter events, 0.0 us)
Async XLA Ops:
  1.3 21.1 %collective-permute-start = (bf16[784,128]{1,0:T(8,128)(2,1)S(1)}, bf16[784,128]{1,0:T(8,128)(2,1)S(1)}, u32[]{:S(2)}, u32[]{:S(2)}) collective-permute-start(bf16[784,128]{1,0:T(8,128)(2,1)S(1)} %get-tuple-element.35), channel_id=1, source_target_pairs={{0,4},{4,0},{1,5},{5,1},{2,6},{6,2},{3,7},{7,3}} | collective-permute-start | bytes 602120 | tf_op jit(solution)/shard_map/ppermute | solution.py:530
  5.2 17.1 %collective-permute-start.1 = (bf16[784,128]{1,0:T(8,128)(2,1)S(1)}, bf16[784,128]{1,0:T(8,128)(2,1)S(1)}, u32[]{:S(2)}, u32[]{:S(2)}) collective-permute-start(bf16[784,128]{1,0:T(8,128)(2,1)S(1)} %get-tuple-element.35), channel_id=1, source_target_pairs={{8,12},{12,8},{16,20},{20,16},{24,28},{28,24},{32,36},{36,32},{40,... | collective-permute-start | bytes 602120 | tf_op jit(solution)/shard_map/ppermute | solution.py:532
  5.9 19.7 %collective-permute-start.2 = (bf16[784,128]{1,0:T(8,128)(2,1)S(1)}, bf16[784,128]{1,0:T(8,128)(2,1)S(1)}, u32[]{:S(2)}, u32[]{:S(2)}) collective-permute-start(bf16[784,128]{1,0:T(8,128)(2,1)S(1)} %get-tuple-element.37), channel_id=1, source_target_pairs={{0,508},{4,8},{8,4},{12,16},{16,12},{20,24},{24,20},{28,32},{32,28... | collective-permute-start | bytes 602120 | tf_op jit(solution)/shard_map/ppermute | solution.py:531
  25.6 9.3 %copy-start = (bf16[4,256,256]{2,1,0:T(8,128)(2,1)S(1)}, bf16[4,256,256]{2,1,0:T(8,128)(2,1)}, u32[]{:S(2)}) copy-start(bf16[4,256,256]{2,1,0:T(8,128)(2,1)} %map_ref.1) | copy-start | bytes 1572868
  25.8 8.9 %copy-start.1 = (f32[4,256]{1,0:T(4,128)S(1)}, f32[4,256]{1,0:T(4,128)}, u32[]{:S(2)}) copy-start(f32[4,256]{1,0:T(4,128)} %param.16) | copy-start | bytes 12292
  25.8 9.5 %collective-permute-start.3 = (bf16[544,128]{1,0:T(8,128)(2,1)S(1)}, bf16[544,128]{1,0:T(8,128)(2,1)S(1)}, u32[]{:S(2)}, u32[]{:S(2)}) collective-permute-start(bf16[544,128]{1,0:T(8,128)(2,1)S(1)} %get-tuple-element.39), channel_id=1, source_target_pairs={{0,1},{1,0},{2,3},{3,2},{4,5},{5,4},{6,7},{7,6},{8,9},{9,8},{10,11... | collective-permute-start | bytes 417800 | tf_op jit(solution)/shard_map/ppermute | solution.py:580
  29.3 7.1 %collective-permute-start.4 = (bf16[544,128]{1,0:T(8,128)(2,1)S(1)}, bf16[544,128]{1,0:T(8,128)(2,1)S(1)}, u32[]{:S(2)}, u32[]{:S(2)}) collective-permute-start(bf16[544,128]{1,0:T(8,128)(2,1)S(1)} %get-tuple-element.38.block0_ref), channel_id=1, source_target_pairs={{0,2},{1,3},{2,0},{3,1},{4,6},{5,7},{6,4},{7,5},{8,10},{9,11},{10,... | collective-permute-start | bytes 417800 | tf_op jit(solution)/shard_map/ppermute | solution.py:578
  31.6 8.0 %collective-permute-start.5 = (bf16[544,128]{1,0:T(8,128)(2,1)S(1)}, bf16[544,128]{1,0:T(8,128)(2,1)S(1)}, u32[]{:S(2)}, u32[]{:S(2)}) collective-permute-start(bf16[544,128]{1,0:T(8,128)(2,1)S(1)} %get-tuple-element.39), channel_id=1, source_target_pairs={{0,3},{1,2},{2,1},{3,0},{4,7},{5,6},{6,5},{7,4},{8,11},{9,10},{10,... | collective-permute-start | bytes 417800 | tf_op jit(solution)/shard_map/ppermute | solution.py:579
  40.0 3.4 %collective-permute-start.6 = (f32[512,128]{1,0:T(8,128)S(1)}, f32[512,128]{1,0:T(8,128)S(1)}, u32[]{:S(2)}, u32[]{:S(2)}) collective-permute-start(f32[512,128]{1,0:T(8,128)S(1)} %get-tuple-element.43), channel_id=1, source_target_pairs={{0,1},{1,0},{2,3},{3,2},{4,5},{5,4},{6,7},{7,6},{8,9},{9,8},{10,11... | collective-permute-start | bytes 786440 | tf_op jit(solution)/shard_map/ppermute | solution.py:612
